TPU v7x, 32 devices: a whole 2x2x4 slice. The times are simulated.
32 devices in a mesh: dp: 4 (over x, core), ctx: 2 (over y), tensor: 4 (over z).
Axes of the slice: x: 2, y: 2, z: 4, core: 2. Of those that a mesh axis runs over, the one named last changes fastest.
Arguments:
- hidden_in: bfloat16 [8, 1024, 2048], P('dp', 'ctx'), may hold values from -36.5 to 36.5
- lengths: int32 [8], replicated, may hold values from 256 to 1024, as said below
- w_query: bfloat16 [2048, 2048], P(('dp', 'ctx'), 'tensor'), may hold values from -0.125 to 0.125
- w_keyval: bfloat16 [2048, 4, 128], P(('dp', 'ctx'), 'tensor'), may hold values from -0.125 to 0.125
- w_output: bfloat16 [2048, 2048], P(('dp', 'ctx'), 'tensor'), may hold values from -1.5 to 1.5
- w_gateup: bfloat16 [2048, 2, 5632], P(('dp', 'ctx'), None, 'tensor'), may hold values from -0.125 to 0.125
- w_down: bfloat16 [2048, 5632], P(('dp', 'ctx'), 'tensor'), may hold values from -0.078125 to 0.078125
- gain_attn: bfloat16 [2048], P(('dp', 'ctx')), may hold values from 0.5 to 1.5
- gain_mlp: bfloat16 [2048], P(('dp', 'ctx')), may hold values from 0.5 to 1.5
- cotangent: bfloat16 [8, 1024, 2048], P('dp', 'ctx'), may hold values from -6 to 6
Outputs:
- output: bfloat16 [8, 1024, 2048], P('dp', 'ctx')
- input_grad: bfloat16 [8, 1024, 2048], P('dp', 'ctx')
- grad_query: float32 [2048, 2048], P(('dp', 'ctx'), 'tensor')
- grad_keyval: float32 [2048, 4, 128], P(('dp', 'ctx'), 'tensor')
- grad_output: float32 [2048, 2048], P(('dp', 'ctx'), 'tensor')
- grad_gateup: float32 [2048, 2, 5632], P(('dp', 'ctx'), None, 'tensor')
- grad_down: float32 [2048, 5632], P(('dp', 'ctx'), 'tensor')
- grad_gain_attn: float32 [2048], P(('dp', 'ctx'))
- grad_gain_mlp: float32 [2048], P(('dp', 'ctx'))
- root_means: float32 [3], replicated
Inputs may be any that keep to these rules, and one draw needn't show every extreme that they name: `lengths`: in every draw the first slot has exactly 1024 valid tokens and the last exactly 256.
All inputs are finite; a program needn't handle non-finite values.
Results may differ from a plain program's by a relative error of at most 0.014.
Values may be sent and summed in bfloat16 or wider, within the bound.
No kernel may reach another device: no remote copies, remote signals or barrier semaphores. Data moves between devices by JAX's collectives and lax.ppermute only.
A program may use at most 384 MiB of HBM per device.

v0:
```python
import jax
import jax.numpy as jnp
from jax import lax
from jax.sharding import PartitionSpec as P

D = 2048
HD = 64


EPS = 1e-05
THETA = 10000.0
NEG_FILL = -1e30


def from_behind(block, axis, distance):
    devices = range(lax.axis_size(axis))
    route = [(i - distance, i) for i in devices if i - distance in devices]
    return lax.ppermute(block, axis, route)


def rms_scale(values):
    return lax.rsqrt(jnp.mean(values * values, axis=-1, keepdims=True) + EPS)


def rope_tables(positions, head_width):
    frequency = THETA ** (-jnp.arange(0, head_width, 2).astype(jnp.float32) / head_width)
    angles = positions.astype(jnp.float32)[:, None] * frequency[None, :]
    angles = jnp.concatenate([angles, angles], axis=-1)
    return (jnp.cos(angles), jnp.sin(angles))


def rotate(values, cosine, sine):
    half_width = values.shape[-1] // 2
    turned = jnp.concatenate([-values[..., half_width:], values[..., :half_width]], axis=-1)
    return values * cosine + turned * sine


def rotate_back(grads, cosine, sine):
    half_width = grads.shape[-1] // 2
    scaled = grads * sine
    turned = jnp.concatenate([scaled[..., half_width:], -scaled[..., :half_width]], axis=-1)
    return grads * cosine + turned


def contract_rows(left, right):
    return lax.dot_general(
        left, right, (((0,), (0,)), ((), ())), preferred_element_type=jnp.float32
    )


def contract_cols(left, right):
    return lax.dot_general(
        left, right, (((1,), (1,)), ((), ())), preferred_element_type=jnp.float32
    )


def score_block(queries, pair, positions, key_positions, length):
    allowed = (
        (key_positions[None, :] <= positions[:, None])
        & (key_positions[None, :] >= 0)
        & (key_positions[None, :] < length)
    )
    raw_scores = jnp.einsum(
        "qhd,pd->hqp", queries, pair[:, :HD], preferred_element_type=jnp.float32
    )
    return jnp.where(allowed[None], raw_scores * HD ** (-0.5), NEG_FILL)


def forward_step(weights, positions, key_positions, cosine, sine, squares, packed):
    query_w, keyval_w, output_w, gateup_w, down_w, attn_gain, mlp_gain = weights
    token_rows, length = packed
    tokens = token_rows.astype(jnp.float32)
    rows, width = tokens.shape
    heads = query_w.shape[1] // HD
    live_mask = (positions < length).astype(jnp.float32)[:, None]
    normed = (tokens * rms_scale(tokens) * attn_gain.astype(jnp.float32)).astype(jnp.bfloat16)
    query_lin = jnp.dot(normed, query_w, preferred_element_type=jnp.float32)
    keyval_lin = jnp.dot(normed, keyval_w.reshape(width, -1), preferred_element_type=jnp.float32)
    queries = rotate(
        query_lin.reshape(rows, heads, HD), cosine[:, None, :], sine[:, None, :]
    ).astype(jnp.bfloat16)
    keys = rotate(keyval_lin[:, :HD], cosine, sine)
    local_pair = jnp.concatenate([keys, keyval_lin[:, HD:]], axis=-1).astype(jnp.bfloat16)
    remote_pair = from_behind(local_pair, "ctx", 1)
    pair = jnp.concatenate([remote_pair, local_pair], axis=0)
    scores = score_block(queries, pair, positions, key_positions, length)
    top = jnp.max(scores, axis=-1, keepdims=True)
    shifted = jnp.exp(scores - top)
    total = jnp.sum(shifted, axis=-1, keepdims=True)
    attend = (shifted / total).astype(jnp.bfloat16)
    log_total = top + jnp.log(total)
    context = jnp.einsum("hqp,pd->qhd", attend, pair[:, HD:], preferred_element_type=jnp.float32)
    context = context.reshape(rows, heads * HD).astype(jnp.bfloat16)
    attn_part = contract_cols(context, output_w)
    attn_out = lax.psum(attn_part, "tensor")
    middle = tokens + attn_out
    normed_mlp = (middle * rms_scale(middle) * mlp_gain.astype(jnp.float32)).astype(jnp.bfloat16)
    gateup = jnp.dot(
        normed_mlp, gateup_w.reshape(width, -1), preferred_element_type=jnp.float32
    ).reshape(rows, 2, -1)
    hidden = (jax.nn.silu(gateup[:, 0]) * gateup[:, 1]).astype(jnp.bfloat16)
    mlp_part = contract_cols(hidden, down_w)
    mlp_out = lax.psum(mlp_part.astype(jnp.bfloat16), "tensor").astype(jnp.float32)
    result = (middle + mlp_out) * live_mask
    squares = squares + jnp.stack(
        [
            jnp.sum(result * result),
            jnp.sum(attn_out * attn_out * live_mask),
            jnp.sum(mlp_out * mlp_out * live_mask),
        ]
    )
    saved = (normed, queries, pair, log_total, context, middle, normed_mlp, gateup)
    return (squares, (result.astype(jnp.bfloat16), saved))


def backward_step(weights, positions, key_positions, cosine, sine, totals, packed):
    query_w, keyval_w, output_w, gateup_w, down_w, attn_gain, mlp_gain = weights
    token_rows, seed_rows, length, saved = packed
    normed, queries, pair, log_total, context, middle, normed_mlp, gateup = saved
    tokens = token_rows.astype(jnp.float32)
    rows, width = tokens.shape
    heads = queries.shape[1]
    live_mask = (positions < length).astype(jnp.float32)[:, None]
    seed = seed_rows.astype(jnp.float32) * live_mask
    mlp_seed = seed.astype(jnp.bfloat16)
    gate_lin = gateup[:, 0]
    up_lin = gateup[:, 1]
    sigmoid_gate = jax.nn.sigmoid(gate_lin)
    activated = jax.nn.silu(gate_lin)
    hidden = (activated * up_lin).astype(jnp.bfloat16)
    grad_hidden = jnp.dot(mlp_seed, down_w, preferred_element_type=jnp.float32)
    grad_gate = grad_hidden * up_lin * (sigmoid_gate * (1.0 + gate_lin * (1.0 - sigmoid_gate)))
    grad_up = grad_hidden * activated
    grad_gateup = jnp.stack([grad_gate, grad_up], axis=1).reshape(rows, -1).astype(jnp.bfloat16)
    gateup_flat = gateup_w.reshape(width, -1)
    mlp_back_part = contract_cols(grad_gateup, gateup_flat)
    grad_normed_mlp = lax.psum(mlp_back_part, "tensor")
    mlp_scale = rms_scale(middle)
    weighted_mlp = grad_normed_mlp * mlp_gain.astype(jnp.float32)
    grad_middle = (
        seed
        + mlp_scale * weighted_mlp
        - middle * mlp_scale**3 * jnp.mean(weighted_mlp * middle, axis=-1, keepdims=True)
    )
    seed_part_low = grad_middle.astype(jnp.bfloat16)
    grad_context = (
        jnp.dot(seed_part_low, output_w, preferred_element_type=jnp.float32)
        .astype(jnp.bfloat16)
        .reshape(rows, heads, HD)
    )
    scores = score_block(queries, pair, positions, key_positions, length)
    attend_full = jnp.exp(scores - log_total)
    grad_attend = jnp.einsum(
        "qhd,pd->hqp", grad_context, pair[:, HD:], preferred_element_type=jnp.float32
    )
    center = jnp.sum(attend_full * grad_attend, axis=-1, keepdims=True)
    grad_raw = (attend_full * (grad_attend - center) * HD ** (-0.5)).astype(jnp.bfloat16)
    grad_values = jnp.einsum(
        "hqp,qhd->pd",
        attend_full.astype(jnp.bfloat16),
        grad_context,
        preferred_element_type=jnp.float32,
    )
    grad_queries = jnp.einsum(
        "hqp,pd->qhd", grad_raw, pair[:, :HD], preferred_element_type=jnp.float32
    )
    grad_keys = jnp.einsum("hqp,qhd->pd", grad_raw, queries, preferred_element_type=jnp.float32)
    grad_pair = jnp.concatenate([grad_keys, grad_values], axis=-1)
    returned = from_behind(grad_pair[:rows], "ctx", -1)
    grad_own = grad_pair[rows:] + returned
    grad_keyval = jnp.concatenate(
        [rotate_back(grad_own[:, :HD], cosine, sine), grad_own[:, HD:]], axis=-1
    ).astype(jnp.bfloat16)
    grad_query_lin = (
        rotate_back(grad_queries, cosine[:, None, :], sine[:, None, :])
        .reshape(rows, -1)
        .astype(jnp.bfloat16)
    )
    keyval_flat = keyval_w.reshape(width, -1)
    attn_back_part = contract_cols(grad_query_lin, query_w) + contract_cols(
        grad_keyval, keyval_flat
    )
    grad_normed = lax.psum(attn_back_part, "tensor")
    attn_scale = rms_scale(tokens)
    weighted_attn = grad_normed * attn_gain.astype(jnp.float32)
    grad_tokens = (
        grad_middle
        + attn_scale * weighted_attn
        - tokens * attn_scale**3 * jnp.mean(weighted_attn * tokens, axis=-1, keepdims=True)
    )
    updates = (
        contract_rows(normed, grad_query_lin),
        contract_rows(normed, grad_keyval).reshape(keyval_w.shape),
        contract_rows(seed_part_low, context),
        contract_rows(normed_mlp, grad_gateup).reshape(gateup_w.shape),
        contract_rows(mlp_seed, hidden),
        jnp.sum(grad_normed * tokens * attn_scale, axis=0),
        jnp.sum(grad_normed_mlp * middle * mlp_scale, axis=0),
    )
    totals = tuple((running + extra for running, extra in zip(totals, updates)))
    return (totals, grad_tokens.astype(jnp.bfloat16))


def body(
    hidden_in,
    lengths,
    w_query,
    w_keyval,
    w_output,
    w_gateup,
    w_down,
    gain_attn,
    gain_mlp,
    cotangent,
):
    micro, rows, width = hidden_in.shape
    positions = lax.axis_index("ctx") * rows + jnp.arange(rows, dtype=jnp.int32)
    key_positions = jnp.concatenate([positions - rows, positions])
    cosine, sine = rope_tables(positions, HD)
    slot_lengths = lax.dynamic_slice_in_dim(lengths, lax.axis_index("dp") * micro, micro)
    shards = (w_query, w_keyval, w_output, w_gateup, w_down, gain_attn, gain_mlp)

    def forward_fn(squares, packed):
        fresh = (
            lax.all_gather(w_query, ("dp", "ctx"), axis=0, tiled=True),
            lax.all_gather(w_keyval, ("dp", "ctx"), axis=0, tiled=True),
            lax.all_gather(w_output, ("dp", "ctx"), axis=0, tiled=True),
            lax.all_gather(w_gateup, ("dp", "ctx"), axis=0, tiled=True),
            lax.all_gather(w_down, ("dp", "ctx"), axis=0, tiled=True),
            lax.all_gather(gain_attn, ("dp", "ctx"), axis=0, tiled=True),
            lax.all_gather(gain_mlp, ("dp", "ctx"), axis=0, tiled=True),
        )
        return forward_step(fresh, positions, key_positions, cosine, sine, squares, packed)

    def backward_fn(totals, packed):
        fresh = (
            lax.all_gather(w_query, ("dp", "ctx"), axis=0, tiled=True),
            lax.all_gather(w_keyval, ("dp", "ctx"), axis=0, tiled=True),
            lax.all_gather(w_output, ("dp", "ctx"), axis=0, tiled=True),
            lax.all_gather(w_gateup, ("dp", "ctx"), axis=0, tiled=True),
            lax.all_gather(w_down, ("dp", "ctx"), axis=0, tiled=True),
            lax.all_gather(gain_attn, ("dp", "ctx"), axis=0, tiled=True),
            lax.all_gather(gain_mlp, ("dp", "ctx"), axis=0, tiled=True),
        )
        return backward_step(fresh, positions, key_positions, cosine, sine, totals, packed)

    squares, (results, saved) = lax.scan(
        forward_fn, jnp.zeros((3,), jnp.float32), (hidden_in, slot_lengths)
    )
    empty_totals = tuple((jnp.zeros((D,) + shard.shape[1:], jnp.float32) for shard in shards))
    totals, grad_rows = lax.scan(
        backward_fn, empty_totals, (hidden_in, cotangent, slot_lengths, saved)
    )
    square_totals = lax.psum(squares, ("dp", "ctx"))
    valid_count = jnp.sum(lengths).astype(jnp.float32) * D
    root_means = jnp.sqrt(square_totals / valid_count)
    reduced = (
        lax.psum_scatter(totals[0], ("dp", "ctx"), scatter_dimension=0, tiled=True),
        lax.psum_scatter(totals[1], ("dp", "ctx"), scatter_dimension=0, tiled=True),
        lax.psum_scatter(totals[2], ("dp", "ctx"), scatter_dimension=0, tiled=True),
        lax.psum_scatter(totals[3], ("dp", "ctx"), scatter_dimension=0, tiled=True),
        lax.psum_scatter(totals[4], ("dp", "ctx"), scatter_dimension=0, tiled=True),
        lax.psum_scatter(totals[5], ("dp", "ctx"), scatter_dimension=0, tiled=True),
        lax.psum_scatter(totals[6], ("dp", "ctx"), scatter_dimension=0, tiled=True),
    )
    return (
        results,
        grad_rows,
        reduced[0],
        reduced[1],
        reduced[2],
        reduced[3],
        reduced[4],
        reduced[5],
        reduced[6],
        root_means,
    )


def solution(mesh):
    placed = (
        P("dp", "ctx", None),
        P(),
        P(("dp", "ctx"), "tensor"),
        P(("dp", "ctx"), "tensor", None),
        P(("dp", "ctx"), "tensor"),
        P(("dp", "ctx"), None, "tensor"),
        P(("dp", "ctx"), "tensor"),
        P(("dp", "ctx")),
        P(("dp", "ctx")),
        P("dp", "ctx", None),
    )
    return jax.shard_map(
        body,
        mesh=mesh,
        in_specs=placed,
        out_specs=(
            P("dp", "ctx", None),
            P("dp", "ctx", None),
            P(("dp", "ctx"), "tensor"),
            P(("dp", "ctx"), "tensor", None),
            P(("dp", "ctx"), "tensor"),
            P(("dp", "ctx"), None, "tensor"),
            P(("dp", "ctx"), "tensor"),
            P(("dp", "ctx")),
            P(("dp", "ctx")),
            P(),
        ),
        check_vma=False,
    )
```

profile of v0, /device:TPU:0, one launch (start us, length us, event | category | flops | bytes accessed | tf_op | source)
XLA Modules:
  0.0 2640.3 jit_solution(12595167485632672327)
XLA Ops:
  20.6 915.7 %while.54 = (s32[]{:T(128)}, f32[3]{0:T(128)S(1)}, bf16[2,512,2048]{2,1,0:T(8,128)(2,1)}, bf16[2,512,2048]{2,1,0:T(8,128)(2,1)}, bf16[2,512,8,64]{1,3,2,0:T(8,12...) while((s32[]{:T(128)}, f32[3]{0:T(128)S(1)}, ...), condition=%wide.region_10.11_spmd.clone, body=%wide.region_0.10_spmd.clone.sunk | while | flops 12453074944 | bytes 434036544 | solution.py:247
  117.7 140.5 %all-reduce.12.cloned.1.call-done = f32[512,2048]{1,0:T(8,128)} async-done(((f32[512,2048]{1,0:T(8,128)}), f32[512,2048]{1,0:T(8,128)}) %all-reduce.12.cloned.1.call-update) | async-done | bytes 4194320 | tf_op jit(solution)/shard_map/while/body/eval_jaxpr/psum | solution.py:95
  266.8 59.9 %all-gather.31.cloned.1.call-done = bf16[2048,2,1408]{2,1,0:T(2,128)(2,1)} async-done(((bf16[256,2,1408]{2,1,0:T(2,128)(2,1)}), bf16[2048,2,1408]{2,1,0:T(2,128)(2,1)}) %all-gather.31.cloned.1.call-update) | async-done | bytes 11534352 | tf_op jit(solution)/shard_map/while/body/eval_jaxpr/all_gather | solution.py:228
  402.2 65.4 %all-reduce.14.cloned.1.call-done = bf16[512,2048]{1,0:T(8,128)(2,1)} async-done(((bf16[512,2048]{1,0:T(8,128)(2,1)}), bf16[512,2048]{1,0:T(8,128)(2,1)}) %all-reduce.14.cloned.1.call-update) | async-done | bytes 2097168 | tf_op jit(solution)/shard_map/while/body/eval_jaxpr/psum | solution.py:103
  575.6 138.7 %all-reduce.12.cloned.1.call-done = f32[512,2048]{1,0:T(8,128)} async-done(((f32[512,2048]{1,0:T(8,128)}), f32[512,2048]{1,0:T(8,128)}) %all-reduce.12.cloned.1.call-update) | async-done | bytes 4194320 | tf_op jit(solution)/shard_map/while/body/eval_jaxpr/psum | solution.py:95
  722.9 59.9 %all-gather.31.cloned.1.call-done = bf16[2048,2,1408]{2,1,0:T(2,128)(2,1)} async-done(((bf16[256,2,1408]{2,1,0:T(2,128)(2,1)}), bf16[2048,2,1408]{2,1,0:T(2,128)(2,1)}) %all-gather.31.cloned.1.call-update) | async-done | bytes 11534352 | tf_op jit(solution)/shard_map/while/body/eval_jaxpr/all_gather | solution.py:228
  858.5 65.3 %all-reduce.14.cloned.1.call-done = bf16[512,2048]{1,0:T(8,128)(2,1)} async-done(((bf16[512,2048]{1,0:T(8,128)(2,1)}), bf16[512,2048]{1,0:T(8,128)(2,1)}) %all-reduce.14.cloned.1.call-update) | async-done | bytes 2097168 | tf_op jit(solution)/shard_map/while/body/eval_jaxpr/psum | solution.py:103
  938.8 1127.0 %while.55 = (s32[]{:T(128)}, f32[2048,512]{1,0:T(8,128)}, f32[2048,1,128]{2,0,1:T(8,128)}, f32[2048,512]{1,0:T(8,128)}, f32[2048,2,1408]{2,0,1:T(8,128)}, /*inde...) while((s32[]{:T(128)}, f32[2048,512]{1,0:T(8,128)}, ...), condition=%wide.region_21.22_spmd.clone, body=%wide.region_11.21_spmd.clone.sunk | while | flops 25381644288 | bytes 722071680 | solution.py:251
  955.7 35.1 %all-gather.37.cloned.1.call-done = bf16[2048,1408]{1,0:T(8,128)(2,1)} async-done(((bf16[256,1408]{1,0:T(8,128)(2,1)}), bf16[2048,1408]{1,0:T(8,128)(2,1)}) %all-gather.37.cloned.1.call-update) | async-done | bytes 5767184 | tf_op jit(solution)/shard_map/while/body/eval_jaxpr/all_gather | solution.py:241
  1001.0 60.0 %all-gather.35.cloned.1.call-done = bf16[2048,2,1408]{2,0,1:T(8,128)(2,1)} async-done(((bf16[256,2,1408]{2,0,1:T(8,128)(2,1)}), bf16[2048,2,1408]{2,0,1:T(8,128)(2,1)}) %all-gather.35.cloned.1.call-update) | async-done | bytes 11534352 | tf_op jit(solution)/shard_map/while/body/eval_jaxpr/all_gather | solution.py:240
  1117.4 109.6 %all-reduce.16.cloned.1.call-done = f32[512,2048]{1,0:T(8,128)} async-done(((f32[512,2048]{1,0:T(8,128)}), f32[512,2048]{1,0:T(8,128)}) %all-reduce.16.cloned.1.call-update) | async-done | bytes 4194320 | tf_op jit(solution)/shard_map/while/body/eval_jaxpr/psum | solution.py:137
  1300.7 26.5 %broadcast_multiply_fusion.8 = (f32[512,8,64]{0,2,1:T(8,128)}, f32[512,8,64]{0,2,1:T(8,128)}) fusion(f32[512,64]{0,1:T(8,128)} %copy-done.17, f32[8,512,1024]{1,2,0:T(8,128)} %fusion.260, f32[1024,512,8]{1,0,2:T(8,128)} %fusion.265, bf16[1024,128]{0,1:T(8,128)(2,1)S(1)} %dynamic-slice_bitcast_fusion.5), kind=kOutput, calls=%fused_computation.172.clone.1 | convolution fusion | flops 558109696 | bytes 69468160 | tf_op jit(solution)/shard_map/while/body/eval_jaxpr/hqp,pd->qhd/dot_general | solution.py:164
  1394.4 99.7 %all-reduce.18.cloned.1.call-done = f32[512,2048]{1,0:T(8,128)} async-done(((f32[512,2048]{1,0:T(8,128)}), f32[512,2048]{1,0:T(8,128)}) %all-reduce.18.cloned.1.call-update) | async-done | bytes 4194320 | tf_op jit(solution)/shard_map/while/body/eval_jaxpr/psum | solution.py:183
  1514.2 35.1 %all-gather.37.cloned.1.call-done = bf16[2048,1408]{1,0:T(8,128)(2,1)} async-done(((bf16[256,1408]{1,0:T(8,128)(2,1)}), bf16[2048,1408]{1,0:T(8,128)(2,1)}) %all-gather.37.cloned.1.call-update) | async-done | bytes 5767184 | tf_op jit(solution)/shard_map/while/body/eval_jaxpr/all_gather | solution.py:241
  1559.5 60.0 %all-gather.35.cloned.1.call-done = bf16[2048,2,1408]{2,0,1:T(8,128)(2,1)} async-done(((bf16[256,2,1408]{2,0,1:T(8,128)(2,1)}), bf16[2048,2,1408]{2,0,1:T(8,128)(2,1)}) %all-gather.35.cloned.1.call-update) | async-done | bytes 11534352 | tf_op jit(solution)/shard_map/while/body/eval_jaxpr/all_gather | solution.py:240
  1676.5 109.1 %all-reduce.16.cloned.1.call-done = f32[512,2048]{1,0:T(8,128)} async-done(((f32[512,2048]{1,0:T(8,128)}), f32[512,2048]{1,0:T(8,128)}) %all-reduce.16.cloned.1.call-update) | async-done | bytes 4194320 | tf_op jit(solution)/shard_map/while/body/eval_jaxpr/psum | solution.py:137
  1859.2 26.5 %broadcast_multiply_fusion.8 = (f32[512,8,64]{0,2,1:T(8,128)}, f32[512,8,64]{0,2,1:T(8,128)}) fusion(f32[512,64]{0,1:T(8,128)} %copy-done.17, f32[8,512,1024]{1,2,0:T(8,128)} %fusion.260, f32[1024,512,8]{1,0,2:T(8,128)} %fusion.265, bf16[1024,128]{0,1:T(8,128)(2,1)S(1)} %dynamic-slice_bitcast_fusion.5), kind=kOutput, calls=%fused_computation.172.clone.1 | convolution fusion | flops 558109696 | bytes 69468160 | tf_op jit(solution)/shard_map/while/body/eval_jaxpr/hqp,pd->qhd/dot_general | solution.py:164
  1960.9 91.7 %all-reduce.18.cloned.1.call-done = f32[512,2048]{1,0:T(8,128)} async-done(((f32[512,2048]{1,0:T(8,128)}), f32[512,2048]{1,0:T(8,128)}) %all-reduce.18.cloned.1.call-update) | async-done | bytes 4194320 | tf_op jit(solution)/shard_map/while/body/eval_jaxpr/psum | solution.py:183
  2065.9 38.7 %copy.57 = f32[2048,2,1408]{2,1,0:T(2,128)} copy(f32[2048,2,1408]{2,0,1:T(8,128)} %get-tuple-element.318) | data formatting | bytes 46137344 | tf_op jit(solution)/shard_map/while | solution.py:251
  2137.6 252.9 %all-reduce.10.cloned.1.call-done = f32[2048,2,1408]{2,1,0:T(2,128)} async-done(((f32[2048,2,1408]{2,1,0:T(2,128)}), f32[2048,2,1408]{2,1,0:T(2,128)}) %all-reduce.10.cloned.1.call-update) | async-done | bytes 23068688
  2394.9 35.5 %reduce-scatter.7.cloned.1.call-done = f32[256,1,128]{2,1,0:T(1,128)} async-done(((f32[2048,1,128]{2,1,0:T(1,128)}), f32[256,1,128]{2,1,0:T(1,128)}) %reduce-scatter.7.cloned.1.call-update) | async-done | bytes 131088 | tf_op jit(solution)/shard_map/reduce_scatter | solution.py:259
  2430.4 55.4 %reduce-scatter.5.cloned.1.call-done = f32[256,512]{1,0:T(8,128)} async-done(((f32[2048,512]{1,0:T(8,128)}), f32[256,512]{1,0:T(8,128)}) %reduce-scatter.5.cloned.1.call-update) | async-done | bytes 524304 | tf_op jit(solution)/shard_map/reduce_scatter | solution.py:258
  2485.8 55.2 %reduce-scatter.9.cloned.1.call-done = f32[256,512]{1,0:T(8,128)} async-done(((f32[2048,512]{1,0:T(8,128)}), f32[256,512]{1,0:T(8,128)}) %reduce-scatter.9.cloned.1.call-update) | async-done | bytes 524304 | tf_op jit(solution)/shard_map/reduce_scatter | solution.py:260
  2541.0 91.1 %reduce-scatter.11.cloned.1.call-done = f32[256,1408]{1,0:T(8,128)} async-done(((f32[2048,1408]{1,0:T(8,128)}), f32[256,1408]{1,0:T(8,128)}) %reduce-scatter.11.cloned.1.call-update) | async-done | bytes 1441808 | tf_op jit(solution)/shard_map/reduce_scatter | solution.py:262
  (482 shorter events, 898.3 us)
Async XLA Ops:
  21.4 75.5 %all-gather.27.cloned.1.call-start = ((), (), s32[]{:S(2)}) async-start(), calls=%async_computation.10 | async-start | bytes 2359296 | tf_op jit(solution)/shard_map/while/body/eval_jaxpr/all_gather | solution.py:227
  63.2 195.0 %all-reduce.12.cloned.1.call-start = ((), (), s32[]{:S(2)}) async-start(), calls=%async_computation.11 | async-start | bytes 8388608 | tf_op jit(solution)/shard_map/while/body/eval_jaxpr/psum | solution.py:95
  101.8 224.8 %all-gather.31.cloned.1.call-start = ((), (), s32[]{:S(2)}) async-start(), calls=%async_computation.13 | async-start | bytes 12976128 | tf_op jit(solution)/shard_map/while/body/eval_jaxpr/all_gather | solution.py:228
  102.4 269.3 %all-gather.29.cloned.1.call-start = ((), (), s32[]{:S(2)}) async-start(), calls=%async_computation.12 | async-start | bytes 6488064 | tf_op jit(solution)/shard_map/while/body/eval_jaxpr/all_gather | solution.py:229
  103.0 364.6 %all-reduce.14.cloned.1.call-start = ((), (), s32[]{:S(2)}) async-start(), calls=%async_computation.14 | async-start | bytes 4194304 | tf_op jit(solution)/shard_map/while/body/eval_jaxpr/psum | solution.py:103
  520.7 193.6 %all-reduce.12.cloned.1.call-start = ((), (), s32[]{:S(2)}) async-start(), calls=%async_computation.11 | async-start | bytes 8388608 | tf_op jit(solution)/shard_map/while/body/eval_jaxpr/psum | solution.py:95
  558.9 223.9 %all-gather.31.cloned.1.call-start = ((), (), s32[]{:S(2)}) async-start(), calls=%async_computation.13 | async-start | bytes 12976128 | tf_op jit(solution)/shard_map/while/body/eval_jaxpr/all_gather | solution.py:228
  559.5 268.5 %all-gather.29.cloned.1.call-start = ((), (), s32[]{:S(2)}) async-start(), calls=%async_computation.12 | async-start | bytes 6488064 | tf_op jit(solution)/shard_map/while/body/eval_jaxpr/all_gather | solution.py:229
  560.2 363.6 %all-reduce.14.cloned.1.call-start = ((), (), s32[]{:S(2)}) async-start(), calls=%async_computation.14 | async-start | bytes 4194304 | tf_op jit(solution)/shard_map/while/body/eval_jaxpr/psum | solution.py:103
  946.3 114.6 %all-gather.35.cloned.1.call-start = ((), (), s32[]{:S(2)}) async-start(), calls=%async_computation.16 | async-start | bytes 12976128 | tf_op jit(solution)/shard_map/while/body/eval_jaxpr/all_gather | solution.py:240
  946.9 280.1 %all-reduce.16.cloned.1.call-start = ((), (), s32[]{:S(2)}) async-start(), calls=%async_computation.18 | async-start | bytes 8388608 | tf_op jit(solution)/shard_map/while/body/eval_jaxpr/psum | solution.py:137
  1071.9 183.8 %all-gather.33.cloned.1.call-start = ((), (), s32[]{:S(2)}) async-start(), calls=%async_computation.15 | async-start | bytes 2359296 | tf_op jit(solution)/shard_map/while/body/eval_jaxpr/all_gather | solution.py:239
  1072.5 257.5 %all-gather.39.cloned.1.call-start = ((), (), s32[]{:S(2)}) async-start(), calls=%async_computation.19 | async-start | bytes 2359296 | tf_op jit(solution)/shard_map/while/body/eval_jaxpr/all_gather | solution.py:237
  1073.1 421.0 %all-reduce.18.cloned.1.call-start = ((), (), s32[]{:S(2)}) async-start(), calls=%async_computation.20 | async-start | bytes 8388608 | tf_op jit(solution)/shard_map/while/body/eval_jaxpr/psum | solution.py:183
  1504.9 114.7 %all-gather.35.cloned.1.call-start = ((), (), s32[]{:S(2)}) async-start(), calls=%async_computation.16 | async-start | bytes 12976128 | tf_op jit(solution)/shard_map/while/body/eval_jaxpr/all_gather | solution.py:240
  1505.5 280.1 %all-reduce.16.cloned.1.call-start = ((), (), s32[]{:S(2)}) async-start(), calls=%async_computation.18 | async-start | bytes 8388608 | tf_op jit(solution)/shard_map/while/body/eval_jaxpr/psum | solution.py:137
  1630.5 184.0 %all-gather.33.cloned.1.call-start = ((), (), s32[]{:S(2)}) async-start(), calls=%async_computation.15 | async-start | bytes 2359296 | tf_op jit(solution)/shard_map/while/body/eval_jaxpr/all_gather | solution.py:239
  1631.2 257.3 %all-gather.39.cloned.1.call-start = ((), (), s32[]{:S(2)}) async-start(), calls=%async_computation.19 | async-start | bytes 2359296 | tf_op jit(solution)/shard_map/while/body/eval_jaxpr/all_gather | solution.py:237
  1632.0 420.6 %all-reduce.18.cloned.1.call-start = ((), (), s32[]{:S(2)}) async-start(), calls=%async_computation.20 | async-start | bytes 8388608 | tf_op jit(solution)/shard_map/while/body/eval_jaxpr/psum | solution.py:183
  2065.9 324.7 %all-reduce.10.cloned.1.call-start = ((), (), s32[]{:S(2)}) async-start(), calls=%async_computation.8 | async-start | bytes 46137344
  2104.6 325.8 %reduce-scatter.7.cloned.1.call-start = ((), (), s32[]{:S(2)}) async-start(), calls=%async_computation.5 | async-start | bytes 1179648 | tf_op jit(solution)/shard_map/reduce_scatter | solution.py:259
  2105.2 380.6 %reduce-scatter.5.cloned.1.call-start = ((), (), s32[]{:S(2)}) async-start(), calls=%async_computation.4 | async-start | bytes 4718592 | tf_op jit(solution)/shard_map/reduce_scatter | solution.py:258
  2105.8 435.2 %reduce-scatter.9.cloned.1.call-start = ((), (), s32[]{:S(2)}) async-start(), calls=%async_computation.6 | async-start | bytes 4718592 | tf_op jit(solution)/shard_map/reduce_scatter | solution.py:260
  2106.5 525.6 %reduce-scatter.11.cloned.1.call-start = ((), (), s32[]{:S(2)}) async-start(), calls=%async_computation.7 | async-start | bytes 12976128 | tf_op jit(solution)/shard_map/reduce_scatter | solution.py:262
  (99 other events, 2615.9 us)
Sparse Core Ops, SparseCore 0:
  24.1 32.3 all-gather.24
  63.3 27.7 all-gather.26
  101.9 156.1 all-reduce.11
  259.9 66.6 all-gather.30
  328.4 43.3 all-gather.28
  381.0 86.4 all-reduce.13
  483.4 27.5 all-gather.24
  520.8 26.1 all-gather.26
  559.0 155.2 all-reduce.11
  716.0 66.6 all-gather.30
  784.6 43.3 all-gather.28
  837.3 86.4 all-reduce.13
  948.5 42.2 all-gather.36
  993.3 67.6 all-gather.34
  1072.0 154.9 all-reduce.15
  1228.8 26.8 all-gather.32
  1257.4 27.9 all-gather.38
  1337.0 157.0 all-reduce.17
  1507.0 42.3 all-gather.36
  1551.8 67.6 all-gather.34
  1630.6 154.9 all-reduce.15
  1787.5 26.8 all-gather.32
  1816.3 27.9 all-gather.38
  1895.5 157.0 all-reduce.17
Sparse Core Ops, SparseCore 1:
  2104.7 285.7 all-reduce.9
  2394.5 35.9 reduce-scatter.6
  2434.6 51.2 reduce-scatter.4
  2489.8 51.2 reduce-scatter.8
  2545.5 86.6 reduce-scatter.10
where the time goes:
time: 2660 us; the launch traced here: 2640 us
  waiting for transfers between devices  1690 us (64%)
  matrix products  371 us (14%)
  blocking collectives  213 us (8%)
  local copies, waits for them, and re-layouts  190 us (7%)
  other arithmetic  140 us (5%)
    psum x2, waiting for transfers between devices, forward_step(): attn_out = lax.psum(attn_part, 'tensor')  279 us
    unnamed x6, waiting for transfers between devices  255 us
    psum x2, waiting for transfers between devices, backward_step(): grad_normed_mlp = lax.psum(mlp_back_part, 'tensor')  219 us
    psum x2, waiting for transfers between devices, backward_step(): grad_normed = lax.psum(attn_back_part, 'tensor')  191 us
    psum x2, waiting for transfers between devices, forward_step(): lax.psum(mlp_part.astype(jnp.bfloat16), 'tensor').astype(jnp.float32)  131 us
    all_gather x2, waiting for transfers between devices, backward_fn(): lax.all_gather(w_gateup, ('dp', 'ctx'), axis=0, tiled=True)  120 us
    all_gather x2, waiting for transfers between devices, forward_fn(): lax.all_gather(w_gateup, ('dp', 'ctx'), axis=0, tiled=True)  120 us
    reduce_scatter x1, waiting for transfers between devices, body(): lax.psum_scatter(totals[4], ('dp', 'ctx'), scatter_dimension=0, tiled=True)  91.1 us
  transfers between devices with their start and end apart: 33, of which 25 were waited for; matrix products, arithmetic and copies ran while one was open for 20% of the time, Pallas kernels for 0%

commit v1 on v0

v1 whole, which is shorter than its diff:
```python
import functools

import jax
import jax.numpy as jnp
from jax import lax
from jax.experimental import pallas as pl
from jax.experimental.pallas import tpu as pltpu
from jax.sharding import PartitionSpec as P

HD = 64
EPS = 1e-05
THETA = 10000.0
NEG_FILL = -1e30
SLOT_STEP = 1 << 16
NEVER = 1 << 30
BQ = 256
BK = 256
F32 = jnp.float32
BF16 = jnp.bfloat16
ROW_AXES = ("dp", "ctx")


def dot(left, right, left_dim, right_dim):
    return lax.dot_general(
        left, right, (((left_dim,), (right_dim,)), ((), ())), preferred_element_type=F32
    )


def rms_scale(values):
    return lax.rsqrt(jnp.mean(values * values, axis=-1, keepdims=True) + EPS)


def mask_bias(key_code, query_info):
    code, start = query_info[0:1, :], query_info[1:2, :]
    allowed = (key_code <= code) & (key_code >= start)
    return jnp.where(allowed, 0.0, NEG_FILL)


def attend_kernel(heads, blocks, flags, q_ref, info_ref, k_ref, vt_ref, code_ref, o_ref, lse_ref, m_ref, l_ref, acc_ref):
    m_ref[...] = jnp.full_like(m_ref, NEG_FILL)
    l_ref[...] = jnp.zeros_like(l_ref)
    acc_ref[...] = jnp.zeros_like(acc_ref)
    row = pl.program_id(0)

    def step(kb, carry):
        @pl.when(flags[row * blocks + kb] > 0)
        def _():
            at = pl.multiple_of(kb * BK, BK)
            keys = k_ref[pl.ds(at, BK), :]
            values_t = vt_ref[:, pl.ds(at, BK)]
            bias = mask_bias(code_ref[pl.ds(at, BK), :], info_ref[...])
            for h in range(heads):
                part = slice(h * HD, (h + 1) * HD)
                scores = dot(keys, q_ref[part, :], 1, 0) + bias
                before = m_ref[h : h + 1, :]
                top = jnp.maximum(before, jnp.max(scores, axis=0, keepdims=True))
                shrink = jnp.exp(before - top)
                weights = jnp.exp(scores - top)
                l_ref[h : h + 1, :] = shrink * l_ref[h : h + 1, :] + jnp.sum(weights, axis=0, keepdims=True)
                acc_ref[part, :] = shrink * acc_ref[part, :] + dot(values_t, weights.astype(BF16), 1, 0)
                m_ref[h : h + 1, :] = top

        return carry

    lax.fori_loop(0, blocks, step, 0)
    total = l_ref[...]
    total = jnp.where(total == 0.0, 1.0, total)
    lse_ref[...] = m_ref[...] + jnp.log(total)
    for h in range(heads):
        part = slice(h * HD, (h + 1) * HD)
        o_ref[part, :] = (acc_ref[part, :] / total[h : h + 1, :]).astype(BF16)


def attend(flags, q_t, info, keys, values_t, codes):
    width, rows = q_t.shape
    heads = width // HD
    count = keys.shape[0]
    blocks = count // BK
    whole = lambda i, f: (0, 0)
    column = lambda i, f: (0, i)
    return pl.pallas_call(
        functools.partial(attend_kernel, heads, blocks),
        out_shape=(
            jax.ShapeDtypeStruct((width, rows), BF16),
            jax.ShapeDtypeStruct((heads, rows), F32),
        ),
        grid_spec=pltpu.PrefetchScalarGridSpec(
            num_scalar_prefetch=1,
            grid=(rows // BQ,),
            in_specs=[
                pl.BlockSpec((width, BQ), column),
                pl.BlockSpec((2, BQ), column),
                pl.BlockSpec((count, HD), whole),
                pl.BlockSpec((HD, count), whole),
                pl.BlockSpec((count, 1), whole),
            ],
            out_specs=[pl.BlockSpec((width, BQ), column), pl.BlockSpec((heads, BQ), column)],
            scratch_shapes=[
                pltpu.VMEM((heads, BQ), F32),
                pltpu.VMEM((heads, BQ), F32),
                pltpu.VMEM((width, BQ), F32),
            ],
        ),
        compiler_params=pltpu.CompilerParams(vmem_limit_bytes=24 << 20),
        cost_estimate=pl.CostEstimate(
            flops=8 * rows * count * width, bytes_accessed=4 * rows * width, transcendentals=0
        ),
        name="attend",
    )(flags, q_t, info, keys, values_t, codes)


def attend_back_kernel(
    heads, blocks, flags, q_ref, do_ref, o_ref, lse_ref, info_ref, cos_ref, sin_ref, k_ref, v_ref, kt_ref, code_ref,
    dq_ref, dk_ref, dv_ref, acc_ref, delta_ref,
):
    row = pl.program_id(0)

    @pl.when(row == 0)
    def _():
        dk_ref[...] = jnp.zeros_like(dk_ref)
        dv_ref[...] = jnp.zeros_like(dv_ref)

    acc_ref[...] = jnp.zeros_like(acc_ref)
    for h in range(heads):
        part = slice(h * HD, (h + 1) * HD)
        delta_ref[h : h + 1, :] = jnp.sum(
            do_ref[part, :].astype(F32) * o_ref[part, :].astype(F32), axis=0, keepdims=True
        )

    def step(kb, carry):
        @pl.when(flags[row * blocks + kb] > 0)
        def _():
            at = pl.multiple_of(kb * BK, BK)
            keys = k_ref[pl.ds(at, BK), :]
            values = v_ref[pl.ds(at, BK), :]
            keys_t = kt_ref[:, pl.ds(at, BK)]
            bias = mask_bias(code_ref[pl.ds(at, BK), :], info_ref[...])
            grad_keys = jnp.zeros((BK, HD), F32)
            grad_values = jnp.zeros((BK, HD), F32)
            for h in range(heads):
                part = slice(h * HD, (h + 1) * HD)
                queries = q_ref[part, :]
                grads = do_ref[part, :]
                weights = jnp.exp(dot(keys, queries, 1, 0) + bias - lse_ref[h : h + 1, :])
                grad_weights = dot(values, grads, 1, 0)
                raw = (weights * (grad_weights - delta_ref[h : h + 1, :])).astype(BF16)
                grad_values = grad_values + dot(weights.astype(BF16), grads, 1, 1)
                grad_keys = grad_keys + dot(raw, queries, 1, 1)
                acc_ref[part, :] += dot(keys_t, raw, 1, 0)
            dk_ref[pl.ds(at, BK), :] += grad_keys
            dv_ref[pl.ds(at, BK), :] += grad_values

        return carry

    lax.fori_loop(0, blocks, step, 0)
    cosine, sine = cos_ref[...], sin_ref[...]
    half = HD // 2
    for h in range(heads):
        lower = acc_ref[h * HD : h * HD + half, :] * HD**-0.5
        upper = acc_ref[h * HD + half : (h + 1) * HD, :] * HD**-0.5
        dq_ref[h * HD : h * HD + half, :] = (lower * cosine + upper * sine).astype(BF16)
        dq_ref[h * HD + half : (h + 1) * HD, :] = (upper * cosine - lower * sine).astype(BF16)


def attend_back(flags, q_t, grad_t, o_t, lse, info, cosine_t, sine_t, keys, values, keys_t, codes):
    width, rows = q_t.shape
    heads = width // HD
    count = keys.shape[0]
    blocks = count // BK
    whole = lambda i, f: (0, 0)
    column = lambda i, f: (0, i)
    return pl.pallas_call(
        functools.partial(attend_back_kernel, heads, blocks),
        out_shape=(
            jax.ShapeDtypeStruct((width, rows), BF16),
            jax.ShapeDtypeStruct((count, HD), F32),
            jax.ShapeDtypeStruct((count, HD), F32),
        ),
        grid_spec=pltpu.PrefetchScalarGridSpec(
            num_scalar_prefetch=1,
            grid=(rows // BQ,),
            in_specs=[
                pl.BlockSpec((width, BQ), column),
                pl.BlockSpec((width, BQ), column),
                pl.BlockSpec((width, BQ), column),
                pl.BlockSpec((heads, BQ), column),
                pl.BlockSpec((2, BQ), column),
                pl.BlockSpec((HD // 2, BQ), column),
                pl.BlockSpec((HD // 2, BQ), column),
                pl.BlockSpec((count, HD), whole),
                pl.BlockSpec((count, HD), whole),
                pl.BlockSpec((HD, count), whole),
                pl.BlockSpec((count, 1), whole),
            ],
            out_specs=[
                pl.BlockSpec((width, BQ), column),
                pl.BlockSpec((count, HD), whole),
                pl.BlockSpec((count, HD), whole),
            ],
            scratch_shapes=[pltpu.VMEM((width, BQ), F32), pltpu.VMEM((heads, BQ), F32)],
        ),
        compiler_params=pltpu.CompilerParams(vmem_limit_bytes=32 << 20),
        cost_estimate=pl.CostEstimate(
            flops=20 * rows * count * width, bytes_accessed=8 * rows * width, transcendentals=0
        ),
        name="attend_back",
    )(flags, q_t, grad_t, o_t, lse, info, cosine_t, sine_t, keys, values, keys_t, codes)


def block_flags(codes, starts, key_codes):
    top = jnp.max(codes.reshape(-1, BQ), axis=1)
    low = jnp.min(starts.reshape(-1, BQ), axis=1)
    blocks = key_codes.reshape(-1, BK)
    key_low = jnp.min(blocks, axis=1)
    key_top = jnp.max(jnp.where(blocks < NEVER, blocks, -1), axis=1)
    seen = (key_low[None, :] <= top[:, None]) & (key_top[None, :] >= low[:, None])
    return seen.astype(jnp.int32).reshape(-1)


def chain_sum(part):
    place = lax.axis_index("tensor")
    inner = (place == 1) | (place == 2)
    first = lax.ppermute(part, "tensor", [(0, 1), (3, 2)])
    pair = lax.optimization_barrier((part.astype(F32) + first.astype(F32)).astype(BF16))
    second = lax.ppermute(pair, "tensor", [(1, 2), (2, 1)])
    total = lax.optimization_barrier((pair.astype(F32) + second.astype(F32)).astype(BF16))
    third = lax.ppermute(total, "tensor", [(1, 0), (2, 3)])
    return lax.optimization_barrier(jnp.where(inner, total, third))


def gather_rows(shard):
    return lax.all_gather(shard, ROW_AXES, axis=0, tiled=True)


def scatter_rows(grads):
    return lax.psum_scatter(grads, ROW_AXES, scatter_dimension=0, tiled=True).astype(F32)


def body(hidden_in, lengths, w_query, w_keyval, w_output, w_gateup, w_down, gain_attn, gain_mlp, cotangent):
    micro, span, width = hidden_in.shape
    rows = micro * span
    shard_rows = w_query.shape[0]
    q_width = w_query.shape[1]
    ff = w_down.shape[1]
    heads = q_width // HD
    half = HD // 2
    here = lax.axis_index("ctx")

    gains = jnp.stack([gain_attn, gain_mlp], axis=1)
    gains = jnp.pad(gains, ((0, 0), (0, 126)))
    packed = jnp.concatenate([w_query, w_keyval.reshape(shard_rows, -1), gains], axis=1)
    first = gather_rows(packed)
    qkv_w = first[:, : q_width + 2 * HD]
    gain_pair = first[:, q_width + 2 * HD : q_width + 2 * HD + 2].astype(F32).T
    attn_gain, mlp_gain = gain_pair[0:1], gain_pair[1:2]
    output_w = gather_rows(w_output)
    gateup_w = gather_rows(w_gateup.reshape(shard_rows, 2 * ff))
    down_w = gather_rows(w_down)

    slot_lengths = lax.dynamic_slice_in_dim(lengths, lax.axis_index("dp") * micro, micro)
    slot_of = jnp.repeat(jnp.arange(micro, dtype=jnp.int32), span)
    length_of = jnp.repeat(slot_lengths, span)
    offset = jnp.tile(jnp.arange(span, dtype=jnp.int32), micro)
    position = here * span + offset
    other_position = (1 - here) * span + offset
    live = (position < length_of).astype(F32)[:, None]
    starts = slot_of * SLOT_STEP
    codes = starts + position
    own_codes = jnp.where(position < length_of, codes, NEVER)
    other_codes = jnp.where(other_position < length_of, starts + other_position, NEVER)
    key_codes = jnp.concatenate([own_codes, other_codes])
    info = jnp.stack([codes, starts])
    flags = block_flags(codes, starts, key_codes)
    key_codes = key_codes[:, None]

    frequency = THETA ** (-jnp.arange(0, HD, 2).astype(F32) / HD)
    angles = position.astype(F32)[:, None] * frequency[None, :]
    cosine, sine = jnp.cos(angles), jnp.sin(angles)
    cosine_t, sine_t = cosine.T, sine.T

    hidden_flat = hidden_in.reshape(rows, width)
    tokens = hidden_flat.astype(F32)
    seed_flat = cotangent.reshape(rows, width)

    attn_scale = rms_scale(tokens)
    normed = (tokens * attn_scale * attn_gain).astype(BF16)
    q_lin = dot(qkv_w[:, :q_width], normed, 0, 1).reshape(heads, 2, half, rows) * HD**-0.5
    q_t = jnp.stack(
        [
            q_lin[:, 0] * cosine_t - q_lin[:, 1] * sine_t,
            q_lin[:, 1] * cosine_t + q_lin[:, 0] * sine_t,
        ],
        axis=1,
    ).astype(BF16).reshape(q_width, rows)
    kv_lin = dot(normed, qkv_w[:, q_width:], 1, 0)
    k_low, k_high = kv_lin[:, :half], kv_lin[:, half:HD]
    own_pair = jnp.concatenate(
        [k_low * cosine - k_high * sine, k_high * cosine + k_low * sine, kv_lin[:, HD:]], axis=1
    ).astype(BF16)
    other_pair = lax.ppermute(own_pair, "ctx", [(0, 1), (1, 0)])
    pairs = jnp.concatenate([own_pair, other_pair], axis=0)
    pairs_t = pairs.T
    keys, values = pairs[:, :HD], pairs[:, HD:]
    keys_t, values_t = pairs_t[:HD], pairs_t[HD:]
    chunks = [(m * span, span) for m in range(micro)]
    blocks = span // BQ

    context_t, lse = [], []
    flag_blocks = key_codes.shape[0] // BK
    for m in range(micro):
        lo = m * span
        one_flags = flags[m * blocks * flag_blocks : (m + 1) * blocks * flag_blocks]
        got = attend(one_flags, q_t[:, lo : lo + span], info[:, lo : lo + span], keys, values_t, key_codes)
        context_t.append(got[0])
        lse.append(got[1])
    attn_out, middle, mlp_scale, normed_mlp = [], [], [], []
    hidden, grad_gateup, mlp_out, grad_normed_mlp = [], [], [], []
    for m, (lo, size) in enumerate(chunks):
        part = dot(context_t[m], output_w, 0, 1).astype(BF16)
        attn_out.append(chain_sum(part).astype(F32))
        middle.append(tokens[lo : lo + size] + attn_out[m])
        mlp_scale.append(rms_scale(middle[m]))
        normed_mlp.append((middle[m] * mlp_scale[m] * mlp_gain).astype(BF16))

    seeds = [seed_flat[lo : lo + size].astype(F32) * live[lo : lo + size] for lo, size in chunks]
    for m, (lo, size) in enumerate(chunks):
        mlp_seed = seeds[m].astype(BF16)
        grad_hidden = dot(mlp_seed, down_w, 1, 0)
        gateup = dot(normed_mlp[m], gateup_w, 1, 0)
        gate, up = gateup[:, :ff], gateup[:, ff:]
        sigma = jax.nn.sigmoid(gate)
        activated = gate * sigma
        hidden.append((activated * up).astype(BF16))
        grad_gate = grad_hidden * up * (sigma * (1.0 + gate * (1.0 - sigma)))
        grad_gateup.append(jnp.concatenate([grad_gate, grad_hidden * activated], axis=1).astype(BF16))
        back = dot(grad_gateup[m], gateup_w, 1, 1).astype(BF16)
        grad_normed_mlp.append(chain_sum(back).astype(F32))
    for m in range(micro):
        mlp_out.append(chain_sum(dot(hidden[m], down_w, 1, 1).astype(BF16)).astype(F32))

    grad_middle, attn_seed, grad_q_t = [], [], []
    gain_mlp_sum = 0.0
    grad_keys, grad_values = 0.0, 0.0
    for m, (lo, size) in enumerate(chunks):
        weighted = grad_normed_mlp[m] * mlp_gain
        scale = mlp_scale[m]
        grad_middle.append(
            seeds[m] + scale * weighted - middle[m] * scale**3 * jnp.mean(weighted * middle[m], axis=-1, keepdims=True)
        )
        gain_mlp_sum = gain_mlp_sum + jnp.sum(grad_normed_mlp[m] * middle[m] * scale, axis=0)
        attn_seed.append(grad_middle[m].astype(BF16))
        grad_context_t = dot(output_w, attn_seed[m], 0, 1).astype(BF16)
        one_flags = flags[m * blocks * flag_blocks : (m + 1) * blocks * flag_blocks]
        got = attend_back(
            one_flags,
            q_t[:, lo : lo + size],
            grad_context_t,
            context_t[m],
            lse[m],
            info[:, lo : lo + size],
            cosine_t[:, lo : lo + size],
            sine_t[:, lo : lo + size],
            keys,
            values,
            keys_t,
            key_codes,
        )
        grad_q_t.append(got[0])
        grad_keys = grad_keys + got[1]
        grad_values = grad_values + got[2]
    sent = jnp.concatenate([grad_keys[rows:], grad_values[rows:]], axis=1)
    returned = lax.ppermute(sent, "ctx", [(0, 1), (1, 0)])
    own_keys = grad_keys[:rows] + returned[:, :HD]
    own_values = grad_values[:rows] + returned[:, HD:]
    low, high = own_keys[:, :half], own_keys[:, half:]
    grad_pair = jnp.concatenate([low * cosine + high * sine, high * cosine - low * sine, own_values], axis=1)
    grad_pair_t = grad_pair.astype(BF16).T
    grad_qkv_t = jnp.concatenate([jnp.concatenate(grad_q_t, axis=1), grad_pair_t], axis=0)
    input_grad = []
    gain_attn_sum = 0.0
    for m, (lo, size) in enumerate(chunks):
        back = dot(grad_qkv_t[:, lo : lo + size], qkv_w, 0, 1)
        grad_normed = chain_sum(back.astype(BF16)).astype(F32)
        one = tokens[lo : lo + size]
        scale = attn_scale[lo : lo + size]
        weighted = grad_normed * attn_gain
        input_grad.append(
            (grad_middle[m] + scale * weighted - one * scale**3 * jnp.mean(weighted * one, axis=-1, keepdims=True)).astype(BF16)
        )
        gain_attn_sum = gain_attn_sum + jnp.sum(grad_normed * one * scale, axis=0)

    output, squares = [], jnp.zeros((3,), F32)
    for m, (lo, size) in enumerate(chunks):
        alive = live[lo : lo + size]
        result = (middle[m] + mlp_out[m]) * alive
        output.append(result.astype(BF16))
        squares = squares + jnp.stack(
            [jnp.sum(result * result), jnp.sum(attn_out[m] ** 2 * alive), jnp.sum(mlp_out[m] ** 2 * alive)]
        )

    join = lambda parts: jnp.concatenate(parts, axis=0)
    mlp_seed = join(seeds).astype(BF16)
    grad_down = scatter_rows(dot(mlp_seed, join(hidden), 0, 0).astype(BF16))
    grad_gateup_w = scatter_rows(dot(join(normed_mlp), join(grad_gateup), 0, 0).astype(BF16))
    grad_output = scatter_rows(dot(join(attn_seed), jnp.concatenate(context_t, axis=1), 0, 1).astype(BF16))
    grad_qkv = scatter_rows(dot(normed, grad_qkv_t, 0, 1).astype(BF16))

    small = jnp.concatenate([gain_attn_sum, gain_mlp_sum, squares])
    small = lax.psum(small, ROW_AXES)
    valid_count = jnp.sum(lengths).astype(F32) * width
    root_means = jnp.sqrt(small[2 * width :] / valid_count)
    shard = (lax.axis_index("dp") * lax.axis_size("ctx") + here) * shard_rows
    return (
        join(output).reshape(hidden_in.shape),
        join(input_grad).reshape(hidden_in.shape),
        grad_qkv[:, :q_width],
        grad_qkv[:, q_width:].reshape(w_keyval.shape),
        grad_output,
        grad_gateup_w.reshape(w_gateup.shape),
        grad_down,
        lax.dynamic_slice_in_dim(small, shard, shard_rows),
        lax.dynamic_slice_in_dim(small, width + shard, shard_rows),
        root_means,
    )


def solution(mesh):
    placed = (
        P("dp", "ctx", None),
        P(),
        P(("dp", "ctx"), "tensor"),
        P(("dp", "ctx"), "tensor", None),
        P(("dp", "ctx"), "tensor"),
        P(("dp", "ctx"), None, "tensor"),
        P(("dp", "ctx"), "tensor"),
        P(("dp", "ctx")),
        P(("dp", "ctx")),
        P("dp", "ctx", None),
    )
    return jax.shard_map(
        body,
        mesh=mesh,
        in_specs=placed,
        out_specs=(
            P("dp", "ctx", None),
            P("dp", "ctx", None),
            P(("dp", "ctx"), "tensor"),
            P(("dp", "ctx"), "tensor", None),
            P(("dp", "ctx"), "tensor"),
            P(("dp", "ctx"), None, "tensor"),
            P(("dp", "ctx"), "tensor"),
            P(("dp", "ctx")),
            P(("dp", "ctx")),
            P(),
        ),
        check_vma=False,
    )
```

time: 2660 us -> 1050 us (0.39)
  waiting for transfers between devices: 1690 us -> 649 us
  matrix products: 371 us -> 121 us
  blocking collectives: 213 us -> 27.5 us
  local copies, waits for them, and re-layouts: 190 us -> 29.8 us
  starting transfers between devices: 10.2 us -> 51.6 us
  Pallas kernels: 0 us -> 29.7 us
    psum x8 -> x0, waiting for transfers between devices: 820 us -> none  [the longest x2 279 us: forward_step(): attn_out = lax.psum(attn_part, 'tensor')]
    ppermute x4 -> x26, waiting for transfers between devices: 2.16 us -> 622 us  [the longest x8 313 us: chain_sum(): third = lax.ppermute(total, 'tensor', [(1, 0), (2, 3)])]
    all_gather x16 -> x4, waiting for transfers between devices: 364 us -> 26 us  [gather_rows(): return lax.all_gather(shard, ROW_AXES, axis=0, tiled=True)]
    unnamed x6 -> x8, waiting for transfers between devices: 255 us -> 0.81 us
    dot_general x44 -> x20, matrix products: 371 us -> 121 us  [dot(): lax.dot_general(left, right, (((left_dim,), (right_dim,)), ((), ())), pre...]
    reduce_scatter x4, waiting for transfers between devices: 237 us -> 0.01 us  [scatter_rows(): lax.psum_scatter(grads, ROW_AXES, scatter_dimension=0, tiled=True)]
    all_gather x12 -> x0, blocking collectives: 187 us -> none  [the longest x2 37.8 us: forward_fn(): lax.all_gather(w_keyval, ('dp', 'ctx'), axis=0, tiled=True)]
    while x179 -> x0, local copies, waits for them, and re-layouts: 73.2 us -> none  [the longest x1 38.7 us: body(): lax.scan(backward_fn, empty_totals, (hidden_in, cotangent, slot_lengths,...]
  transfers between devices with their start and end apart: 33 -> 34, of which waited for: 25 -> 19; matrix products, arithmetic and copies ran while one was open for 20% -> 21% of each run, Pallas kernels for 0% -> 3%
where the time goes in v1:
time: 1050 us
  waiting for transfers between devices  649 us (62%)
  other arithmetic  123 us (12%)
  matrix products  121 us (12%)
  starting transfers between devices  51.6 us (5%)
  local copies, waits for them, and re-layouts  29.8 us (3%)
  Pallas kernels  29.7 us (3%)
  blocking collectives  27.5 us (3%)
  between operations  16.9 us (2%)
    ppermute x8, waiting for transfers between devices, chain_sum(): third = lax.ppermute(total, 'tensor', [(1, 0), (2, 3)])  313 us
    ppermute x8, waiting for transfers between devices, chain_sum(): first = lax.ppermute(part, 'tensor', [(0, 1), (3, 2)])  300 us
    dot_general x20, matrix products, dot(): lax.dot_general(left, right, (((left_dim,), (right_dim,)), ((), ())), pre...  121 us
    psum x1, blocking collectives, body(): small = lax.psum(small, ROW_AXES)  27.5 us
    all_gather x4, waiting for transfers between devices, gather_rows(): return lax.all_gather(shard, ROW_AXES, axis=0, tiled=True)  26 us
  transfers between devices with their start and end apart: 34, of which 19 were waited for; matrix products, arithmetic and copies ran while one was open for 21% of the time, Pallas kernels for 3%

profile of v1, /device:TPU:0, one launch (start us, length us, event | category | flops | bytes accessed | tf_op | source)
XLA Modules:
  0.0 1048.3 jit_solution(11679195397866970941)
XLA Ops:
  19.7 25.9 %all-gather.5.cloned.1.call-done = bf16[2048,768]{1,0:T(8,128)(2,1)} async-done(((bf16[256,768]{1,0:T(8,128)(2,1)}), bf16[2048,768]{1,0:T(8,128)(2,1)}) %all-gather.5.cloned.1.call-update) | async-done | bytes 3145744 | tf_op jit(solution)/shard_map/all_gather | solution.py:232
  99.3 33.3 %collective-permute-done.7 = bf16[512,2048]{1,0:T(8,128)(2,1)} collective-permute-done((bf16[512,2048]{1,0:T(8,128)(2,1)}, bf16[512,2048]{1,0:T(8,128)(2,1)}, u32[]{:S(2)}, u32[]{:S(2)}) %collective-permute-start.7) | collective-permute-done | bytes 2097184 | tf_op jit(solution)/shard_map/ppermute | solution.py:223
  136.4 40.1 %collective-permute-done.1 = bf16[512,2048]{1,0:T(8,128)(2,1)} collective-permute-done((bf16[512,2048]{1,0:T(8,128)(2,1)S(1)}, bf16[512,2048]{1,0:T(8,128)(2,1)}, u32[]{:S(2)}, u32[]{:S(2)}) %collective-permute-start.1) | collective-permute-done | bytes 2097184 | tf_op jit(solution)/shard_map/ppermute | solution.py:223
  197.1 34.8 %collective-permute-done.9 = bf16[512,2048]{1,0:T(8,128)(2,1)} collective-permute-done((bf16[512,2048]{1,0:T(8,128)(2,1)S(1)}, bf16[512,2048]{1,0:T(8,128)(2,1)}, u32[]{:S(2)}, u32[]{:S(2)}) %collective-permute-start.9) | collective-permute-done | bytes 2097184 | tf_op jit(solution)/shard_map/ppermute | solution.py:227
  233.8 45.2 %collective-permute-done.3 = bf16[512,2048]{1,0:T(8,128)(2,1)} collective-permute-done((bf16[512,2048]{1,0:T(8,128)(2,1)}, bf16[512,2048]{1,0:T(8,128)(2,1)}, u32[]{:S(2)}, u32[]{:S(2)}) %collective-permute-start.3) | collective-permute-done | bytes 2097184 | tf_op jit(solution)/shard_map/ppermute | solution.py:227
  286.0 11.9 %fusion.138 = f32[512,2816]{1,0:T(8,128)} fusion(bf16[512,2048]{1,0:T(8,128)(2,1)S(1)} %multiply_convert_fusion.2, bf16[2048,2816]{1,0:T(8,128)(2,1)} %all-gather.9.cloned.1.call-done), kind=kOutput, calls=%fused_computation.263 | convolution fusion | flops 5905580032 | bytes 19398656 | tf_op jit(solution)/shard_map/dot_general | solution.py:24
  298.0 10.9 %multiply_convert_fusion.6 = (bf16[512,1408]{1,0:T(8,128)(2,1)}, bf16[512,1408]{1,0:T(8,128)(2,1)}, bf16[512,1408]{1,0:T(8,128)(2,1)S(1)}) fusion(f32[512,2816]{1,0:T(8,128)} %fusion.138, bf16[512,2048]{1,0:T(8,128)(2,1)} %get-tuple-element.94, bf16[2048,1408]{1,0:T(8,128)(2,1)} %all-gather.11.cloned.1.call-done), kind=kOutput, calls=%fused_computation.132 | convolution fusion | flops 2963603456 | bytes 17956864 | tf_op jit(solution)/shard_map/dot_general | solution.py:24
  323.8 36.3 %collective-permute-done.4 = bf16[512,2048]{1,0:T(8,128)(2,1)S(1)} collective-permute-done((bf16[512,2048]{1,0:T(8,128)(2,1)S(1)}, bf16[512,2048]{1,0:T(8,128)(2,1)S(1)}, u32[]{:S(2)}, u32[]{:S(2)}) %collective-permute-start.4) | collective-permute-done | bytes 2097184 | tf_op jit(solution)/shard_map/ppermute | solution.py:223
  361.8 40.5 %collective-permute-done.13 = bf16[512,2048]{1,0:T(8,128)(2,1)S(1)} collective-permute-done((bf16[512,2048]{1,0:T(8,128)(2,1)S(1)}, bf16[512,2048]{1,0:T(8,128)(2,1)S(1)}, u32[]{:S(2)}, u32[]{:S(2)}) %collective-permute-start.13) | collective-permute-done | bytes 2097184 | tf_op jit(solution)/shard_map/ppermute | solution.py:223
  408.4 47.3 %collective-permute-done.6 = bf16[512,2048]{1,0:T(8,128)(2,1)S(1)} collective-permute-done((bf16[512,2048]{1,0:T(8,128)(2,1)S(1)}, bf16[512,2048]{1,0:T(8,128)(2,1)S(1)}, u32[]{:S(2)}, u32[]{:S(2)}) %collective-permute-start.6) | collective-permute-done | bytes 2097184 | tf_op jit(solution)/shard_map/ppermute | solution.py:227
  456.1 42.9 %collective-permute-done.15 = bf16[512,2048]{1,0:T(8,128)(2,1)S(1)} collective-permute-done((bf16[512,2048]{1,0:T(8,128)(2,1)S(1)}, bf16[512,2048]{1,0:T(8,128)(2,1)S(1)}, u32[]{:S(2)}, u32[]{:S(2)}) %collective-permute-start.15) | collective-permute-done | bytes 2097184 | tf_op jit(solution)/shard_map/ppermute | solution.py:227
  504.8 10.3 fusion.139
  526.0 9.5 convolution_convert_fusion.3
  536.9 35.0 %collective-permute-done.10 = bf16[512,2048]{1,0:T(8,128)(2,1)S(1)} collective-permute-done((bf16[512,2048]{1,0:T(8,128)(2,1)S(1)}, bf16[512,2048]{1,0:T(8,128)(2,1)S(1)}, u32[]{:S(2)}, u32[]{:S(2)}) %collective-permute-start.10) | collective-permute-done | bytes 2097184 | tf_op jit(solution)/shard_map/ppermute | solution.py:223
  575.0 38.8 %collective-permute-done.16 = bf16[512,2048]{1,0:T(8,128)(2,1)S(1)} collective-permute-done((bf16[512,2048]{1,0:T(8,128)(2,1)S(1)}, bf16[512,2048]{1,0:T(8,128)(2,1)S(1)}, u32[]{:S(2)}, u32[]{:S(2)}) %collective-permute-start.16) | collective-permute-done | bytes 2097184 | tf_op jit(solution)/shard_map/ppermute | solution.py:223
  638.6 42.9 %collective-permute-done.12 = bf16[512,2048]{1,0:T(8,128)(2,1)} collective-permute-done((bf16[512,2048]{1,0:T(8,128)(2,1)}, bf16[512,2048]{1,0:T(8,128)(2,1)}, u32[]{:S(2)}, u32[]{:S(2)}) %collective-permute-start.12) | collective-permute-done | bytes 2097184 | tf_op jit(solution)/shard_map/ppermute | solution.py:227
  683.4 39.2 %collective-permute-done.18 = bf16[512,2048]{1,0:T(8,128)(2,1)} collective-permute-done((bf16[512,2048]{1,0:T(8,128)(2,1)}, bf16[512,2048]{1,0:T(8,128)(2,1)}, u32[]{:S(2)}, u32[]{:S(2)}) %collective-permute-start.18) | collective-permute-done | bytes 2097184 | tf_op jit(solution)/shard_map/ppermute | solution.py:227
  770.2 10.9 %collective-permute-start.19 = (f32[1024,128]{0,1:T(8,128)S(1)}, f32[1024,128]{0,1:T(8,128)S(1)}, u32[]{:S(2)}, u32[]{:S(2)}) collective-permute-start(f32[1024,128]{0,1:T(8,128)S(1)} %pad_maximum_fusion.5), channel_id=1, source_target_pairs={{0,4},{4,0},{1,5},{5,1},{2,6},{6,2},{3,7},{7,3},{8,12},{12,8},{9,1... | collective-permute-start | bytes 1572872 | tf_op jit(solution)/shard_map/ppermute | solution.py:372
  796.2 18.0 %convolution_convert_fusion = bf16[2048,2816]{1,0:T(8,128)(2,1)} fusion(bf16[512,1408]{1,0:T(8,128)(2,1)} %get-tuple-element.83, bf16[512,1408]{1,0:T(8,128)(2,1)} %get-tuple-element.82, bf16[512,1408]{1,0:T(8,128)(2,1)} %get-tuple-element.81, bf16[512,1408]{1,0:T(8,128)(2,1)} %get-tuple-element.80, bf16[512,2048]{1,0:T(8,128)(2,1)} %copy-done.46, ...), kind=kOutput, calls=%fused_computation | convolution fusion | flops 11848384512 | bytes 21495808 | tf_op jit(solution)/shard_map/dot_general | solution.py:24
  824.4 42.6 %collective-permute-done.23 = bf16[512,2048]{1,0:T(8,128)(2,1)S(1)} collective-permute-done((bf16[512,2048]{1,0:T(8,128)(2,1)S(1)}, bf16[512,2048]{1,0:T(8,128)(2,1)S(1)}, u32[]{:S(2)}, u32[]{:S(2)}) %collective-permute-start.23) | collective-permute-done | bytes 2097184 | tf_op jit(solution)/shard_map/ppermute | solution.py:223
  868.8 32.9 %collective-permute-done.20 = bf16[512,2048]{1,0:T(8,128)(2,1)S(1)} collective-permute-done((bf16[512,2048]{1,0:T(8,128)(2,1)S(1)}, bf16[512,2048]{1,0:T(8,128)(2,1)S(1)}, u32[]{:S(2)}, u32[]{:S(2)}) %collective-permute-start.20) | collective-permute-done | bytes 2097184 | tf_op jit(solution)/shard_map/ppermute | solution.py:223
  927.8 24.9 %collective-permute-done.25 = bf16[512,2048]{1,0:T(8,128)(2,1)} collective-permute-done((bf16[512,2048]{1,0:T(8,128)(2,1)S(1)}, bf16[512,2048]{1,0:T(8,128)(2,1)}, u32[]{:S(2)}, u32[]{:S(2)}) %collective-permute-start.25) | collective-permute-done | bytes 2097184 | tf_op jit(solution)/shard_map/ppermute | solution.py:227
  954.5 35.8 %collective-permute-done.22 = bf16[512,2048]{1,0:T(8,128)(2,1)} collective-permute-done((bf16[512,2048]{1,0:T(8,128)(2,1)}, bf16[512,2048]{1,0:T(8,128)(2,1)}, u32[]{:S(2)}, u32[]{:S(2)}) %collective-permute-start.22) | collective-permute-done | bytes 2097184 | tf_op jit(solution)/shard_map/ppermute | solution.py:227
  997.9 27.5 %psum.7 = f32[4099]{0:T(1024)S(1)} all-reduce(f32[4099]{0:T(1024)S(1)} %pad_maximum_fusion.7), channel_id=1, replica_groups=mesh['dp'=4,'ctx'=2,'tensor'=4] {'dp','ctx'}, use_global_device_ids=true, to_apply=%region_25.26 | all-reduce | flops 4099 | bytes 32792 | tf_op jit(solution)/shard_map/psum | solution.py:409
  (388 shorter events, 293.8 us)
Async XLA Ops:
  10.5 68.0 %all-gather.7.cloned.1.call-start = ((), (), s32[]{:S(2)}) async-start(), calls=%async_computation.5 | async-start | bytes 2359296 | tf_op jit(solution)/shard_map/all_gather | solution.py:232
  11.3 274.8 %all-gather.9.cloned.1.call-start = ((), (), s32[]{:S(2)}) async-start(), calls=%async_computation.6 | async-start | bytes 12976128 | tf_op jit(solution)/shard_map/all_gather | solution.py:232
  13.9 284.0 %all-gather.11.cloned.1.call-start = ((), (), s32[]{:S(2)}) async-start(), calls=%async_computation.7 | async-start | bytes 6488064 | tf_op jit(solution)/shard_map/all_gather | solution.py:232
  82.9 49.7 %collective-permute-start.7 = (bf16[512,2048]{1,0:T(8,128)(2,1)}, bf16[512,2048]{1,0:T(8,128)(2,1)}, u32[]{:S(2)}, u32[]{:S(2)}) collective-permute-start(bf16[512,2048]{1,0:T(8,128)(2,1)} %convolution_convert_fusion.5), channel_id=1, source_target_pairs={{0,1},{3,2},{4,5},{7,6},{8,9},{11,10},{12,13},{15,14},{16,17},{19,... | collective-permute-start | bytes 6291464 | tf_op jit(solution)/shard_map/ppermute | solution.py:223
  96.6 79.9 %collective-permute-start.1 = (bf16[512,2048]{1,0:T(8,128)(2,1)S(1)}, bf16[512,2048]{1,0:T(8,128)(2,1)}, u32[]{:S(2)}, u32[]{:S(2)}) collective-permute-start(bf16[512,2048]{1,0:T(8,128)(2,1)S(1)} %convolution_convert_fusion.6), channel_id=1, source_target_pairs={{0,1},{3,2},{4,5},{7,6},{8,9},{11,10},{12,13},{15,14},{16,17},{19,... | collective-permute-start | bytes 6291464 | tf_op jit(solution)/shard_map/ppermute | solution.py:223
  99.2 821.1 %reduce-scatter.11.cloned.1.call-start = ((), (), s32[]{:S(2)}) async-start(), calls=%async_computation.11 | async-start | bytes 6488064 | tf_op jit(solution)/shard_map/reduce_scatter | solution.py:236
  180.7 51.2 %collective-permute-start.9 = (bf16[512,2048]{1,0:T(8,128)(2,1)S(1)}, bf16[512,2048]{1,0:T(8,128)(2,1)}, u32[]{:S(2)}, u32[]{:S(2)}) collective-permute-start(bf16[512,2048]{1,0:T(8,128)(2,1)S(1)} %add_convert_fusion.10), channel_id=1, source_target_pairs={{1,0},{2,3},{5,4},{6,7},{9,8},{10,11},{13,12},{14,15},{17,16},{18,... | collective-permute-start | bytes 6291464 | tf_op jit(solution)/shard_map/ppermute | solution.py:227
  184.1 94.9 %collective-permute-start.3 = (bf16[512,2048]{1,0:T(8,128)(2,1)}, bf16[512,2048]{1,0:T(8,128)(2,1)}, u32[]{:S(2)}, u32[]{:S(2)}) collective-permute-start(bf16[512,2048]{1,0:T(8,128)(2,1)} %add_convert_fusion.14), channel_id=1, source_target_pairs={{1,0},{2,3},{5,4},{6,7},{9,8},{10,11},{13,12},{14,15},{17,16},{18,... | collective-permute-start | bytes 6291464 | tf_op jit(solution)/shard_map/ppermute | solution.py:227
  312.6 47.5 %collective-permute-start.4 = (bf16[512,2048]{1,0:T(8,128)(2,1)S(1)}, bf16[512,2048]{1,0:T(8,128)(2,1)S(1)}, u32[]{:S(2)}, u32[]{:S(2)}) collective-permute-start(bf16[512,2048]{1,0:T(8,128)(2,1)S(1)} %convolution_convert_fusion.10), channel_id=1, source_target_pairs={{0,1},{3,2},{4,5},{7,6},{8,9},{11,10},{12,13},{15,14},{16,17},{19,... | collective-permute-start | bytes 6291464 | tf_op jit(solution)/shard_map/ppermute | solution.py:223
  322.4 80.0 %collective-permute-start.13 = (bf16[512,2048]{1,0:T(8,128)(2,1)S(1)}, bf16[512,2048]{1,0:T(8,128)(2,1)S(1)}, u32[]{:S(2)}, u32[]{:S(2)}) collective-permute-start(bf16[512,2048]{1,0:T(8,128)(2,1)S(1)} %convolution_convert_fusion.4), channel_id=1, source_target_pairs={{0,1},{3,2},{4,5},{7,6},{8,9},{11,10},{12,13},{15,14},{16,17},{19,... | collective-permute-start | bytes 6291464 | tf_op jit(solution)/shard_map/ppermute | solution.py:223
  404.7 51.0 %collective-permute-start.6 = (bf16[512,2048]{1,0:T(8,128)(2,1)S(1)}, bf16[512,2048]{1,0:T(8,128)(2,1)S(1)}, u32[]{:S(2)}, u32[]{:S(2)}) collective-permute-start(bf16[512,2048]{1,0:T(8,128)(2,1)S(1)} %add_convert_fusion.12), channel_id=1, source_target_pairs={{1,0},{2,3},{5,4},{6,7},{9,8},{10,11},{13,12},{14,15},{17,16},{18,... | collective-permute-start | bytes 6291464 | tf_op jit(solution)/shard_map/ppermute | solution.py:227
  406.9 92.0 %collective-permute-start.15 = (bf16[512,2048]{1,0:T(8,128)(2,1)S(1)}, bf16[512,2048]{1,0:T(8,128)(2,1)S(1)}, u32[]{:S(2)}, u32[]{:S(2)}) collective-permute-start(bf16[512,2048]{1,0:T(8,128)(2,1)S(1)} %add_convert_fusion.6), channel_id=1, source_target_pairs={{1,0},{2,3},{5,4},{6,7},{9,8},{10,11},{13,12},{14,15},{17,16},{18,... | collective-permute-start | bytes 6291464 | tf_op jit(solution)/shard_map/ppermute | solution.py:227
  524.4 47.5 %collective-permute-start.10 = (bf16[512,2048]{1,0:T(8,128)(2,1)S(1)}, bf16[512,2048]{1,0:T(8,128)(2,1)S(1)}, u32[]{:S(2)}, u32[]{:S(2)}) collective-permute-start(bf16[512,2048]{1,0:T(8,128)(2,1)S(1)} %convolution_convert_fusion.9), channel_id=1, source_target_pairs={{0,1},{3,2},{4,5},{7,6},{8,9},{11,10},{12,13},{15,14},{16,17},{19,... | collective-permute-start | bytes 6291464 | tf_op jit(solution)/shard_map/ppermute | solution.py:223
  535.5 78.3 %collective-permute-start.16 = (bf16[512,2048]{1,0:T(8,128)(2,1)S(1)}, bf16[512,2048]{1,0:T(8,128)(2,1)S(1)}, u32[]{:S(2)}, u32[]{:S(2)}) collective-permute-start(bf16[512,2048]{1,0:T(8,128)(2,1)S(1)} %convolution_convert_fusion.3), channel_id=1, source_target_pairs={{0,1},{3,2},{4,5},{7,6},{8,9},{11,10},{12,13},{15,14},{16,17},{19,... | collective-permute-start | bytes 6291464 | tf_op jit(solution)/shard_map/ppermute | solution.py:223
  572.8 54.1 %collective-permute-start.11 = (bf16[512,2048]{1,0:T(8,128)(2,1)S(1)}, bf16[512,2048]{1,0:T(8,128)(2,1)}, u32[]{:S(2)}, u32[]{:S(2)}) collective-permute-start(bf16[512,2048]{1,0:T(8,128)(2,1)S(1)} %add_convert_fusion.9), channel_id=1, source_target_pairs={{1,2},{2,1},{5,6},{6,5},{9,10},{10,9},{13,14},{14,13},{17,18},{18,... | collective-permute-start | bytes 6291464 | tf_op jit(solution)/shard_map/ppermute | solution.py:225
  626.9 295.7 %reduce-scatter.7.cloned.1.call-start = ((), (), s32[]{:S(2)}) async-start(), calls=%async_computation.9 | async-start | bytes 2359296 | tf_op jit(solution)/shard_map/reduce_scatter | solution.py:236
  630.6 50.9 %collective-permute-start.12 = (bf16[512,2048]{1,0:T(8,128)(2,1)}, bf16[512,2048]{1,0:T(8,128)(2,1)}, u32[]{:S(2)}, u32[]{:S(2)}) collective-permute-start(bf16[512,2048]{1,0:T(8,128)(2,1)} %add_convert_fusion.8), channel_id=1, source_target_pairs={{1,0},{2,3},{5,4},{6,7},{9,8},{10,11},{13,12},{14,15},{17,16},{18,... | collective-permute-start | bytes 6291464 | tf_op jit(solution)/shard_map/ppermute | solution.py:227
  637.0 85.6 %collective-permute-start.18 = (bf16[512,2048]{1,0:T(8,128)(2,1)}, bf16[512,2048]{1,0:T(8,128)(2,1)}, u32[]{:S(2)}, u32[]{:S(2)}) collective-permute-start(bf16[512,2048]{1,0:T(8,128)(2,1)} %add_convert_fusion.4), channel_id=1, source_target_pairs={{1,0},{2,3},{5,4},{6,7},{9,8},{10,11},{13,12},{14,15},{17,16},{18,... | collective-permute-start | bytes 6291464 | tf_op jit(solution)/shard_map/ppermute | solution.py:227
  754.0 170.5 %reduce-scatter.5.cloned.1.call-start = ((), (), s32[]{:S(2)}) async-start(), calls=%async_computation.8 | async-start | bytes 2949120 | tf_op jit(solution)/shard_map/reduce_scatter | solution.py:236
  795.9 240.9 %reduce-scatter.9.cloned.1.call-start = ((), (), s32[]{:S(2)}) async-start(), calls=%async_computation.10 | async-start | bytes 12976128 | tf_op jit(solution)/shard_map/reduce_scatter | solution.py:236
  818.1 49.0 %collective-permute-start.23 = (bf16[512,2048]{1,0:T(8,128)(2,1)S(1)}, bf16[512,2048]{1,0:T(8,128)(2,1)S(1)}, u32[]{:S(2)}, u32[]{:S(2)}) collective-permute-start(bf16[512,2048]{1,0:T(8,128)(2,1)S(1)} %convolution_convert_fusion.7), channel_id=1, source_target_pairs={{0,1},{3,2},{4,5},{7,6},{8,9},{11,10},{12,13},{15,14},{16,17},{19,... | collective-permute-start | bytes 6291464 | tf_op jit(solution)/shard_map/ppermute | solution.py:223
  823.0 78.7 %collective-permute-start.20 = (bf16[512,2048]{1,0:T(8,128)(2,1)S(1)}, bf16[512,2048]{1,0:T(8,128)(2,1)S(1)}, u32[]{:S(2)}, u32[]{:S(2)}) collective-permute-start(bf16[512,2048]{1,0:T(8,128)(2,1)S(1)} %convolution_convert_fusion.8), channel_id=1, source_target_pairs={{0,1},{3,2},{4,5},{7,6},{8,9},{11,10},{12,13},{15,14},{16,17},{19,... | collective-permute-start | bytes 6291464 | tf_op jit(solution)/shard_map/ppermute | solution.py:223
  904.6 48.1 %collective-permute-start.25 = (bf16[512,2048]{1,0:T(8,128)(2,1)S(1)}, bf16[512,2048]{1,0:T(8,128)(2,1)}, u32[]{:S(2)}, u32[]{:S(2)}) collective-permute-start(bf16[512,2048]{1,0:T(8,128)(2,1)S(1)} %add_convert_fusion), channel_id=1, source_target_pairs={{1,0},{2,3},{5,4},{6,7},{9,8},{10,11},{13,12},{14,15},{17,16},{18,... | collective-permute-start | bytes 6291464 | tf_op jit(solution)/shard_map/ppermute | solution.py:227
  908.1 82.2 %collective-permute-start.22 = (bf16[512,2048]{1,0:T(8,128)(2,1)}, bf16[512,2048]{1,0:T(8,128)(2,1)}, u32[]{:S(2)}, u32[]{:S(2)}) collective-permute-start(bf16[512,2048]{1,0:T(8,128)(2,1)} %add_convert_fusion.2), channel_id=1, source_target_pairs={{1,0},{2,3},{5,4},{6,7},{9,8},{10,11},{13,12},{14,15},{17,16},{18,... | collective-permute-start | bytes 6291464 | tf_op jit(solution)/shard_map/ppermute | solution.py:227
  (100 other events, 1718.1 us)
Sparse Core Ops, SparseCore 0:
  10.6 34.9 all-gather.4
  47.6 30.6 all-gather.6
  80.7 67.6 all-gather.8
  150.2 43.3 all-gather.10
  627.0 59.5 reduce-scatter.10
  754.1 42.6 reduce-scatter.6
  800.7 43.6 reduce-scatter.4
  847.8 86.7 reduce-scatter.8

commit v2 on v1

v2 whole, which is shorter than its diff:
```python
import functools

import jax
import jax.numpy as jnp
from jax import lax
from jax.experimental import pallas as pl
from jax.experimental.pallas import tpu as pltpu
from jax.sharding import PartitionSpec as P

HD = 64
EPS = 1e-05
THETA = 10000.0
NEG_FILL = -1e30
SLOT_STEP = 1 << 16
NEVER = 1 << 30
BQ = 256
BK = 256
SIDE = 1
F32 = jnp.float32
BF16 = jnp.bfloat16
SMALL_COST = pl.CostEstimate(flops=1024, bytes_accessed=1024, transcendentals=0)
ROW_AXES = ("dp", "ctx")


def dot(left, right, left_dim, right_dim):
    return lax.dot_general(
        left, right, (((left_dim,), (right_dim,)), ((), ())), preferred_element_type=F32
    )


def rms_scale(values):
    return lax.rsqrt(jnp.mean(values * values, axis=-1, keepdims=True) + EPS)


def mask_bias(key_code, query_info):
    code, start = query_info[0:1, :], query_info[1:2, :]
    allowed = (key_code <= code) & (key_code >= start)
    return jnp.where(allowed, 0.0, NEG_FILL)


def beside(parts):
    return jnp.concatenate(parts, axis=1)


def heads_of(ref, rows):
    return beside([ref[r * HD : (r + 1) * HD, :] for r in rows])


def rows_of(ref, rows):
    return beside([ref[r : r + 1, :] for r in rows])


def attend_kernel(heads, blocks, flags, q_ref, info_ref, k_ref, vt_ref, code_ref, o_ref, lse_ref, m_ref, l_ref, acc_ref):
    m_ref[...] = jnp.full_like(m_ref, NEG_FILL)
    l_ref[...] = jnp.zeros_like(l_ref)
    acc_ref[...] = jnp.zeros_like(acc_ref)
    row = pl.program_id(0)

    def step(kb, carry):
        @pl.when(flags[row * blocks + kb] > 0)
        def _():
            at = pl.multiple_of(kb * BK, BK)
            keys = k_ref[pl.ds(at, BK), :]
            values_t = vt_ref[:, pl.ds(at, BK)]
            bias = beside([mask_bias(code_ref[pl.ds(at, BK), :], info_ref[...])] * SIDE)
            for h in range(0, heads, SIDE):
                rows = range(h, h + SIDE)
                scores = dot(keys, heads_of(q_ref, rows), 1, 0) + bias
                before = rows_of(m_ref, rows)
                top = jnp.maximum(before, jnp.max(scores, axis=0, keepdims=True))
                shrink = jnp.exp(before - top)
                weights = jnp.exp(scores - top)
                total = shrink * rows_of(l_ref, rows) + jnp.sum(weights, axis=0, keepdims=True)
                out = shrink * heads_of(acc_ref, rows) + dot(values_t, weights.astype(BF16), 1, 0)
                for n, r in enumerate(rows):
                    lanes = slice(n * BQ, (n + 1) * BQ)
                    m_ref[r : r + 1, :] = top[:, lanes]
                    l_ref[r : r + 1, :] = total[:, lanes]
                    acc_ref[r * HD : (r + 1) * HD, :] = out[:, lanes]

        return carry

    lax.fori_loop(0, blocks, step, 0)
    total = l_ref[...]
    total = jnp.where(total == 0.0, 1.0, total)
    lse_ref[...] = m_ref[...] + jnp.log(total)
    for h in range(heads):
        part = slice(h * HD, (h + 1) * HD)
        o_ref[part, :] = (acc_ref[part, :] / total[h : h + 1, :]).astype(BF16)


def attend(flags, q_t, info, keys, values_t, codes):
    width, rows = q_t.shape
    heads = width // HD
    count = keys.shape[0]
    blocks = count // BK
    whole = lambda i, f: (0, 0)
    column = lambda i, f: (0, i)
    return pl.pallas_call(
        functools.partial(attend_kernel, heads, blocks),
        out_shape=(
            jax.ShapeDtypeStruct((width, rows), BF16),
            jax.ShapeDtypeStruct((heads, rows), F32),
        ),
        grid_spec=pltpu.PrefetchScalarGridSpec(
            num_scalar_prefetch=1,
            grid=(rows // BQ,),
            in_specs=[
                pl.BlockSpec((width, BQ), column),
                pl.BlockSpec((2, BQ), column),
                pl.BlockSpec((count, HD), whole),
                pl.BlockSpec((HD, count), whole),
                pl.BlockSpec((count, 1), whole),
            ],
            out_specs=[pl.BlockSpec((width, BQ), column), pl.BlockSpec((heads, BQ), column)],
            scratch_shapes=[
                pltpu.VMEM((heads, BQ), F32),
                pltpu.VMEM((heads, BQ), F32),
                pltpu.VMEM((width, BQ), F32),
            ],
        ),
        compiler_params=pltpu.CompilerParams(vmem_limit_bytes=24 << 20),
        cost_estimate=SMALL_COST,
        name="attend",
    )(flags, q_t, info, keys, values_t, codes)


def attend_back_kernel(
    heads, blocks, flags, q_ref, do_ref, o_ref, lse_ref, info_ref, cos_ref, sin_ref, k_ref, v_ref, kt_ref, code_ref,
    dq_ref, dk_ref, dv_ref, acc_ref, delta_ref,
):
    row = pl.program_id(0)

    @pl.when(row == 0)
    def _():
        dk_ref[...] = jnp.zeros_like(dk_ref)
        dv_ref[...] = jnp.zeros_like(dv_ref)

    acc_ref[...] = jnp.zeros_like(acc_ref)
    for h in range(heads):
        part = slice(h * HD, (h + 1) * HD)
        delta_ref[h : h + 1, :] = jnp.sum(
            do_ref[part, :].astype(F32) * o_ref[part, :].astype(F32), axis=0, keepdims=True
        )

    def step(kb, carry):
        @pl.when(flags[row * blocks + kb] > 0)
        def _():
            at = pl.multiple_of(kb * BK, BK)
            keys = k_ref[pl.ds(at, BK), :]
            values = v_ref[pl.ds(at, BK), :]
            keys_t = kt_ref[:, pl.ds(at, BK)]
            bias = beside([mask_bias(code_ref[pl.ds(at, BK), :], info_ref[...])] * SIDE)
            grad_keys = jnp.zeros((BK, HD), F32)
            grad_values = jnp.zeros((BK, HD), F32)
            for h in range(0, heads, SIDE):
                rows = range(h, h + SIDE)
                queries = heads_of(q_ref, rows)
                grads = heads_of(do_ref, rows)
                weights = jnp.exp(dot(keys, queries, 1, 0) + bias - rows_of(lse_ref, rows))
                grad_weights = dot(values, grads, 1, 0)
                raw = (weights * (grad_weights - rows_of(delta_ref, rows))).astype(BF16)
                grad_values = grad_values + dot(weights.astype(BF16), grads, 1, 1)
                grad_keys = grad_keys + dot(raw, queries, 1, 1)
                out = dot(keys_t, raw, 1, 0)
                for n, r in enumerate(rows):
                    acc_ref[r * HD : (r + 1) * HD, :] += out[:, n * BQ : (n + 1) * BQ]
            dk_ref[pl.ds(at, BK), :] += grad_keys
            dv_ref[pl.ds(at, BK), :] += grad_values

        return carry

    lax.fori_loop(0, blocks, step, 0)
    cosine, sine = cos_ref[...], sin_ref[...]
    half = HD // 2
    for h in range(heads):
        lower = acc_ref[h * HD : h * HD + half, :] * HD**-0.5
        upper = acc_ref[h * HD + half : (h + 1) * HD, :] * HD**-0.5
        dq_ref[h * HD : h * HD + half, :] = (lower * cosine + upper * sine).astype(BF16)
        dq_ref[h * HD + half : (h + 1) * HD, :] = (upper * cosine - lower * sine).astype(BF16)


def attend_back(flags, q_t, grad_t, o_t, lse, info, cosine_t, sine_t, keys, values, keys_t, codes):
    width, rows = q_t.shape
    heads = width // HD
    count = keys.shape[0]
    blocks = count // BK
    whole = lambda i, f: (0, 0)
    column = lambda i, f: (0, i)
    return pl.pallas_call(
        functools.partial(attend_back_kernel, heads, blocks),
        out_shape=(
            jax.ShapeDtypeStruct((width, rows), BF16),
            jax.ShapeDtypeStruct((count, HD), F32),
            jax.ShapeDtypeStruct((count, HD), F32),
        ),
        grid_spec=pltpu.PrefetchScalarGridSpec(
            num_scalar_prefetch=1,
            grid=(rows // BQ,),
            in_specs=[
                pl.BlockSpec((width, BQ), column),
                pl.BlockSpec((width, BQ), column),
                pl.BlockSpec((width, BQ), column),
                pl.BlockSpec((heads, BQ), column),
                pl.BlockSpec((2, BQ), column),
                pl.BlockSpec((HD // 2, BQ), column),
                pl.BlockSpec((HD // 2, BQ), column),
                pl.BlockSpec((count, HD), whole),
                pl.BlockSpec((count, HD), whole),
                pl.BlockSpec((HD, count), whole),
                pl.BlockSpec((count, 1), whole),
            ],
            out_specs=[
                pl.BlockSpec((width, BQ), column),
                pl.BlockSpec((count, HD), whole),
                pl.BlockSpec((count, HD), whole),
            ],
            scratch_shapes=[pltpu.VMEM((width, BQ), F32), pltpu.VMEM((heads, BQ), F32)],
        ),
        compiler_params=pltpu.CompilerParams(vmem_limit_bytes=32 << 20),
        cost_estimate=SMALL_COST,
        name="attend_back",
    )(flags, q_t, grad_t, o_t, lse, info, cosine_t, sine_t, keys, values, keys_t, codes)


def block_flags(codes, starts, key_codes):
    top = jnp.max(codes.reshape(-1, BQ), axis=1)
    low = jnp.min(starts.reshape(-1, BQ), axis=1)
    blocks = key_codes.reshape(-1, BK)
    key_low = jnp.min(blocks, axis=1)
    key_top = jnp.max(jnp.where(blocks < NEVER, blocks, -1), axis=1)
    seen = (key_low[None, :] <= top[:, None]) & (key_top[None, :] >= low[:, None])
    return seen.astype(jnp.int32).reshape(-1)


def rowwise_kernel(fn, bounds, lists, flats, consts, outs, choice, *refs):
    pieces = len(bounds)
    n_list = lists * pieces
    step = pl.program_id(0)
    flat_refs = refs[n_list : n_list + flats]
    const_refs = refs[n_list + flats : n_list + flats + consts]
    out_refs = refs[len(refs) - outs[0] - outs[1] : len(refs) - outs[1]]
    sum_refs = refs[len(refs) - outs[1] :]

    if outs[1]:
        @pl.when(step == 0)
        def _():
            for ref in sum_refs:
                ref[...] = jnp.zeros_like(ref)

    for j, (lo, hi) in enumerate(bounds):
        @pl.when((step >= lo) & (step < hi))
        def _():
            got, sums = fn(
                choice[0],
                [refs[k * pieces + j][...].astype(F32) for k in range(lists)],
                [ref[...].astype(F32) for ref in flat_refs],
                [ref[...] for ref in const_refs],
            )
            for ref, value in zip(out_refs, got):
                ref[...] = value.astype(ref.dtype)
            for ref, value in zip(sum_refs, sums):
                ref[...] += value


def tile_of(size):
    return next(tile for tile in (128, 160, 96, 64, 32, 16) if size % tile == 0)


def rowwise(fn, choice, lists, flats, consts, outs, sums=0, after=(), name="rowwise"):
    tile = tile_of(lists[0][0].shape[0])
    sizes = [piece.shape[0] // tile for piece in lists[0]]
    width = lists[0][0].shape[1]
    bounds, lo = [], 0
    for size in sizes:
        bounds.append((lo, lo + size))
        lo += size
    total = lo

    def piece_map(lo, size):
        return lambda i, c: (jnp.clip(i - lo, 0, size - 1), 0)

    in_specs, operands = [], []
    for pieces in lists:
        for piece, (lo, hi) in zip(pieces, bounds):
            in_specs.append(pl.BlockSpec((tile, width), piece_map(lo, hi - lo)))
            operands.append(piece)
    for array, first in flats:
        offset = first // tile
        in_specs.append(pl.BlockSpec((tile, array.shape[1]), lambda i, c, offset=offset: (i + offset, 0)))
        operands.append(array)
    for array in consts:
        in_specs.append(pl.BlockSpec((1, array.shape[1]), lambda i, c: (0, 0)))
        operands.append(array)
    for array in after:
        in_specs.append(pl.BlockSpec(memory_space=pl.ANY))
        operands.append(array)
    rows = total * tile
    return pl.pallas_call(
        functools.partial(rowwise_kernel, fn, bounds, len(lists), len(flats), len(consts), (len(outs), sums)),
        out_shape=[jax.ShapeDtypeStruct((rows, width), dtype) for dtype in outs]
        + [jax.ShapeDtypeStruct((1, width), F32)] * sums,
        grid_spec=pltpu.PrefetchScalarGridSpec(
            num_scalar_prefetch=1,
            grid=(total,),
            in_specs=in_specs,
            out_specs=[pl.BlockSpec((tile, width), lambda i, c: (i, 0))] * len(outs)
            + [pl.BlockSpec((1, width), lambda i, c: (0, 0))] * sums,
        ),
        compiler_params=pltpu.CompilerParams(vmem_limit_bytes=32 << 20),
        cost_estimate=SMALL_COST,
        name=name,
    )(choice, *operands)


def add_fn(choice, lists, flats, consts):
    return [lists[0] + lists[1]], []


def pick(choice, total, third):
    return jnp.where(choice > 0, total, third)


def row_scale(values):
    return lax.rsqrt(jnp.mean(values * values, axis=1, keepdims=True) + EPS)


def middle_fn(choice, lists, flats, consts):
    branch = pick(choice, lists[0], lists[1])
    middle = flats[0] + branch
    return [branch, middle * row_scale(middle) * consts[0]], []


def column_sum(values):
    return jnp.sum(values, axis=0, keepdims=True)


def grad_middle_fn(choice, lists, flats, consts):
    grad = pick(choice, lists[0], lists[1])
    tokens, branch, seed, live = flats
    middle = tokens + branch
    scale = row_scale(middle)
    weighted = grad * consts[0]
    mean = jnp.mean(weighted * middle, axis=1, keepdims=True)
    out = seed * live + scale * weighted - middle * scale**3 * mean
    return [out, out], [column_sum(grad * middle * scale)]


def input_grad_fn(choice, lists, flats, consts):
    grad = pick(choice, lists[0], lists[1])
    tokens, grad_middle = flats
    scale = row_scale(tokens)
    weighted = grad * consts[0]
    mean = jnp.mean(weighted * tokens, axis=1, keepdims=True)
    return [grad_middle + scale * weighted - tokens * scale**3 * mean], []


def result_fn(choice, lists, flats, consts):
    mlp_branch = pick(choice, lists[0], lists[1])
    tokens, branch, live = flats
    result = (tokens + branch + mlp_branch) * live
    return [result], [
        column_sum(result * result),
        column_sum(branch * branch * live),
        column_sum(mlp_branch * mlp_branch * live),
    ]


def send_in(part):
    return lax.ppermute(part, "tensor", [(0, 1), (3, 2)])


def send_across(pair):
    return lax.ppermute(pair, "tensor", [(1, 2), (2, 1)])


def send_out(total):
    return lax.ppermute(total, "tensor", [(1, 0), (2, 3)])


def held_back(value, dep):
    return value + dep[:1, :1].astype(F32) * 0.0


class Sums:
    def __init__(self, choice):
        self.choice = choice
        self.last = None
        self.order = []
        self.parts, self.firsts, self.pairs, self.seconds, self.totals, self.thirds = {}, {}, {}, {}, {}, {}

    def ordered(self, fn, *args, **more):
        after = tuple(more.pop("after", ()))
        if self.last is not None:
            after += (self.last,)
        got = rowwise(fn, self.choice, *args, after=after, **more)
        self.last = got[0]
        return got

    def push(self, k, part):
        self.order.append(k)
        self.parts[k] = part
        self.firsts[k] = send_in(part)

    def pair(self, k, after=()):
        spot = self.order.index(k)
        if spot >= 3:
            after = tuple(after) + (self.thirds[self.order[spot - 3]],)
        both = [[self.parts[k]], [self.firsts[k]]]
        self.pairs[k] = self.ordered(add_fn, both, [], [], [BF16], after=after, name="pair")[0]
        self.seconds[k] = send_across(self.pairs[k])

    def total(self, k, after=()):
        both = [[self.pairs[k]], [self.seconds[k]]]
        self.totals[k] = self.ordered(add_fn, both, [], [], [BF16], after=after, name="total")[0]
        self.thirds[k] = send_out(self.totals[k])

    def of(self, picked):
        return [self.totals[k] for k in picked], [self.thirds[k] for k in picked]


def small_sum(part):
    part = part + lax.ppermute(part, "tensor", [(0, 1), (1, 0), (2, 3), (3, 2)])
    return part + lax.ppermute(part, "tensor", [(0, 2), (2, 0), (1, 3), (3, 1)])


def gather_rows(shard):
    return lax.all_gather(shard, ROW_AXES, axis=0, tiled=True)


def scatter_rows(grads):
    return lax.psum_scatter(grads, ROW_AXES, scatter_dimension=0, tiled=True).astype(F32)


def fold(values, row_count):
    return jnp.broadcast_to(values, (row_count,)).astype(BF16)[:, None]


def spread_small(values):
    size = lax.axis_size("dp")
    step = 1
    while step < size:
        values = values + lax.ppermute(values, "dp", [(i, i ^ step) for i in range(size)])
        step *= 2
    return values + lax.ppermute(values, "ctx", [(0, 1), (1, 0)])


def body(hidden_in, lengths, w_query, w_keyval, w_output, w_gateup, w_down, gain_attn, gain_mlp, cotangent):
    micro, span, width = hidden_in.shape
    rows = micro * span
    shard_rows = w_query.shape[0]
    q_width = w_query.shape[1]
    ff = w_down.shape[1]
    heads = q_width // HD
    half = HD // 2
    here = lax.axis_index("ctx")
    place = lax.axis_index("tensor")
    choice = ((place == 1) | (place == 2)).astype(jnp.int32).reshape(1)
    sums = Sums(choice)
    join = lambda parts: jnp.concatenate(parts, axis=0)

    gains = jnp.stack([gain_attn, gain_mlp], axis=1)
    gains = jnp.pad(gains, ((0, 0), (0, 126)))
    packed = jnp.concatenate([w_query, w_keyval.reshape(shard_rows, -1), gains], axis=1)
    first = gather_rows(packed)
    qkv_w = first[:, : q_width + 2 * HD]
    gain_pair = first[:, q_width + 2 * HD : q_width + 2 * HD + 2].astype(F32).T
    attn_gain, mlp_gain = gain_pair[0:1], gain_pair[1:2]
    output_w = gather_rows(w_output)
    gateup_w = gather_rows(w_gateup.reshape(shard_rows, 2 * ff))
    down_w = gather_rows(w_down)

    slot_lengths = lax.dynamic_slice_in_dim(lengths, lax.axis_index("dp") * micro, micro)
    slot_of = jnp.repeat(jnp.arange(micro, dtype=jnp.int32), span)
    length_of = jnp.repeat(slot_lengths, span)
    offset = jnp.tile(jnp.arange(span, dtype=jnp.int32), micro)
    position = here * span + offset
    other_position = (1 - here) * span + offset
    live = (position < length_of).astype(F32)[:, None]
    starts = slot_of * SLOT_STEP
    codes = starts + position
    own_codes = jnp.where(position < length_of, codes, NEVER)
    other_codes = jnp.where(other_position < length_of, starts + other_position, NEVER)
    info = jnp.stack([codes, starts])

    frequency = THETA ** (-jnp.arange(0, HD, 2).astype(F32) / HD)
    angles = position.astype(F32)[:, None] * frequency[None, :]
    cosine, sine = jnp.cos(angles), jnp.sin(angles)
    cosine_t, sine_t = cosine.T, sine.T

    hidden_flat = hidden_in.reshape(rows, width)
    seed_flat = cotangent.reshape(rows, width)
    tokens = hidden_flat.astype(F32)

    attn_scale = rms_scale(tokens)
    normed = (tokens * attn_scale * attn_gain).astype(BF16)
    kv_lin = dot(normed, qkv_w[:, q_width:], 1, 0)
    k_low, k_high = kv_lin[:, :half], kv_lin[:, half:HD]
    own_pair = jnp.concatenate(
        [k_low * cosine - k_high * sine, k_high * cosine + k_low * sine, kv_lin[:, HD:]], axis=1
    ).astype(BF16)
    other_pair = lax.ppermute(own_pair, "ctx", [(0, 1), (1, 0)])
    q_lin = dot(qkv_w[:, :q_width], normed, 0, 1).reshape(heads, 2, half, rows) * HD**-0.5
    q_t = jnp.stack(
        [
            q_lin[:, 0] * cosine_t - q_lin[:, 1] * sine_t,
            q_lin[:, 1] * cosine_t + q_lin[:, 0] * sine_t,
        ],
        axis=1,
    ).astype(BF16).reshape(q_width, rows)

    chunk = span // 2
    one, two = slice(0, span), slice(span, 2 * span)
    groups = []
    for at in (one, two):
        pairs = join([own_pair[at], other_pair[at]])
        pairs_t = pairs.T
        key_codes = join([own_codes[at], other_codes[at]])
        groups.append(
            dict(
                flags=block_flags(codes[at], starts[at], key_codes),
                keys=pairs[:, :HD],
                values=pairs[:, HD:],
                keys_t=pairs_t[:HD],
                values_t=pairs_t[HD:],
                codes=key_codes[:, None],
                context=[],
                lse=[],
            )
        )

    def attend_chunk(group, k):
        g = groups[group]
        blocks = 2 * span // BK * chunk // BQ
        lo = group * span + k * chunk
        at = slice(lo, lo + chunk)
        flags = g["flags"][k * blocks : (k + 1) * blocks]
        context, lse = attend(flags, q_t[:, at], info[:, at], g["keys"], g["values_t"], g["codes"])
        g["context"].append(context)
        g["lse"].append(lse)
        return dot(context, output_w, 0, 1)

    def push(k, part):
        for n in range(part.shape[0] // chunk):
            sums.push(k + n, part[n * chunk : (n + 1) * chunk].astype(BF16))

    push(0, attend_chunk(0, 0))
    push(1, attend_chunk(0, 1))
    push(2, attend_chunk(1, 0))
    sums.pair(0, (sums.parts[2],))
    push(3, attend_chunk(1, 1))
    sums.pair(1, (sums.parts[3],))
    sums.total(0)
    sums.pair(2)
    sums.total(1)
    sums.pair(3)
    sums.total(2)

    def middle_of(first, at, after=()):
        return sums.ordered(
            middle_fn, sums.of([first, first + 1]), [(hidden_flat, at.start)], [mlp_gain], [BF16, BF16], after=after, name="middle"
        )

    def forward(normed_rows):
        return dot(normed_rows, gateup_w, 1, 0)

    def products(gateup, seed_rows):
        grad_hidden = dot(seed_rows, down_w, 1, 0)
        gate, up = gateup[:, :ff], gateup[:, ff:]
        sigma = jax.nn.sigmoid(gate)
        activated = gate * sigma
        grad_gate = grad_hidden * up * (sigma * (1.0 + gate * (1.0 - sigma)))
        return (activated * up).astype(BF16), jnp.concatenate([grad_gate, grad_hidden * activated], axis=1).astype(BF16)

    mlp_seed = (seed_flat.astype(F32) * live).astype(BF16)
    attn_out_one, normed_one = middle_of(0, one)
    gateup = forward(normed_one)
    sums.total(3, (gateup,))
    hidden_one, grad_gateup_one = products(gateup, mlp_seed[one])
    push(4, dot(grad_gateup_one, gateup_w, 1, 1))
    attn_out_two, normed_two = middle_of(2, two, (sums.parts[5],))
    gateup = forward(normed_two)
    sums.pair(4, (gateup,))
    hidden_two, grad_gateup_two = products(gateup, mlp_seed[two])
    push(6, held_back(dot(grad_gateup_two, gateup_w, 1, 1), sums.last))
    sums.pair(5, (sums.parts[7],))
    sums.total(4)
    push(8, held_back(dot(hidden_one, down_w, 1, 1), sums.last))
    sums.pair(6, (sums.parts[9],))
    sums.total(5)
    grad_gateup_w = held_back(
        dot(join([normed_one, normed_two]), join([grad_gateup_one, grad_gateup_two]), 0, 0), sums.last
    ).astype(BF16)

    def grad_middle_of(first, at, attn_out, after=()):
        return sums.ordered(
            grad_middle_fn,
            sums.of([first, first + 1]),
            [(hidden_flat, at.start), (attn_out, 0), (seed_flat, at.start), (live, at.start)],
            [mlp_gain],
            [F32, BF16],
            sums=1,
            after=after,
            name="grad_middle",
        )

    def attend_back_group(group, grad_context_t):
        g = groups[group]
        blocks = 2 * span // BK * chunk // BQ
        grad_q, grad_keys, grad_values = [], 0.0, 0.0
        at = slice(group * span, (group + 1) * span)
        got = attend_back(
            g["flags"],
            q_t[:, at],
            grad_context_t,
            jnp.concatenate(g["context"], axis=1),
            jnp.concatenate(g["lse"], axis=1),
            info[:, at],
            cosine_t[:, at],
            sine_t[:, at],
            g["keys"],
            g["values"],
            g["keys_t"],
            g["codes"],
        )
        sent = jnp.concatenate([got[1][span:], got[2][span:]], axis=1)
        returned = lax.ppermute(sent, "ctx", [(0, 1), (1, 0)])
        own_keys = got[1][:span] + returned[:, :HD]
        own_values = got[2][:span] + returned[:, HD:]
        low, high = own_keys[:, :half], own_keys[:, half:]
        cos_rows, sin_rows = cosine[at], sine[at]
        grad_pair = jnp.concatenate([low * cos_rows + high * sin_rows, high * cos_rows - low * sin_rows, own_values], axis=1)
        return got[0], jnp.concatenate([got[0], grad_pair.astype(BF16).T], axis=0)

    grad_middle_one, attn_seed_one, gain_mlp_one = grad_middle_of(4, one, attn_out_one, (grad_gateup_w,))
    sums.pair(7)
    sums.total(6)
    grad_context_t = held_back(dot(output_w, attn_seed_one, 0, 1), sums.last).astype(BF16)
    grad_q_one, grad_qkv_one = attend_back_group(0, grad_context_t)
    sums.pair(8, (grad_q_one,))
    sums.total(7)
    grad_down = held_back(dot(mlp_seed, join([hidden_one, hidden_two]), 0, 0), sums.last).astype(BF16)
    grad_gateup_w = scatter_rows(grad_gateup_w)
    push(12, held_back(dot(grad_qkv_one, qkv_w, 0, 1), grad_down))
    push(10, held_back(dot(hidden_two, down_w, 1, 1), sums.parts[13]))
    grad_middle_two, attn_seed_two, gain_mlp_two = grad_middle_of(6, two, attn_out_two, (sums.parts[11],))
    sums.pair(9)
    sums.total(8)
    grad_context_t = held_back(dot(output_w, attn_seed_two, 0, 1), sums.last).astype(BF16)
    grad_q_two, grad_qkv_two = attend_back_group(1, grad_context_t)
    sums.pair(12, (grad_q_two,))
    sums.total(9)
    push(14, held_back(dot(grad_qkv_two, qkv_w, 0, 1), sums.last))
    grad_down = scatter_rows(grad_down)
    gain_attn_part = 0.0
    for k in range(4):
        at = slice(k * chunk, (k + 1) * chunk)
        gain_attn_part = gain_attn_part + jnp.sum(sums.parts[12 + k].astype(F32) * tokens[at] * attn_scale[at], axis=0)
    sums.pair(13, (sums.parts[15],))
    sums.total(12)
    extra = jnp.concatenate([fold(gain_attn_part, width), fold((gain_mlp_one + gain_mlp_two)[0], width)], axis=1)
    extra = jnp.pad(extra, ((0, 0), (0, 126)))
    grad_qkv_t = jnp.concatenate([grad_qkv_one, grad_qkv_two], axis=1)
    context_t = jnp.concatenate(groups[0]["context"] + groups[1]["context"], axis=1)
    last = jnp.concatenate(
        [
            held_back(dot(normed, grad_qkv_t, 0, 1), sums.last).astype(BF16),
            extra,
            held_back(dot(join([attn_seed_one, attn_seed_two]), context_t, 0, 1), sums.last).astype(BF16),
        ],
        axis=1,
    )

    def result_of(first, at, attn_out, after=()):
        return sums.ordered(
            result_fn,
            sums.of([first, first + 1]),
            [(hidden_flat, at.start), (attn_out, 0), (live, at.start)],
            [],
            [BF16],
            sums=3,
            after=after,
            name="result",
        )

    def input_grad_of(first, at, grad_middle, after=()):
        return sums.ordered(
            input_grad_fn,
            sums.of([first, first + 1]),
            [(hidden_flat, at.start), (grad_middle, 0)],
            [attn_gain],
            [BF16],
            after=after,
            name="input_grad",
        )[0]

    sums.pair(10, (last,))
    sums.total(13)
    last = scatter_rows(last)
    output_one, *squares_one = result_of(8, one, attn_out_one)
    sums.pair(11)
    sums.total(10)
    sums.pair(14, (grad_gateup_w,))
    sums.total(11)
    input_grad_one = input_grad_of(12, one, grad_middle_one)
    sums.pair(15)
    sums.total(14)
    output_two, *squares_two = result_of(10, two, attn_out_two)
    sums.total(15)
    input_grad_two = input_grad_of(14, two, grad_middle_two)
    squares = [jnp.sum(x) + jnp.sum(y) for x, y in zip(squares_one, squares_two)]
    squares = spread_small(jnp.broadcast_to(jnp.stack(squares + [0.0])[None, :], (8, 4)))[0, :3]
    root_means = jnp.sqrt(squares / (jnp.sum(lengths).astype(F32) * width))
    at = q_width + 2 * HD
    return (
        join([output_one, output_two]).reshape(hidden_in.shape),
        join([input_grad_one, input_grad_two]).reshape(hidden_in.shape),
        last[:, :q_width],
        last[:, q_width:at].reshape(w_keyval.shape),
        last[:, at + 128 :],
        grad_gateup_w.reshape(w_gateup.shape),
        grad_down,
        small_sum(last[:, at]),
        last[:, at + 1],
        root_means,
    )


def solution(mesh):
    placed = (
        P("dp", "ctx", None),
        P(),
        P(("dp", "ctx"), "tensor"),
        P(("dp", "ctx"), "tensor", None),
        P(("dp", "ctx"), "tensor"),
        P(("dp", "ctx"), None, "tensor"),
        P(("dp", "ctx"), "tensor"),
        P(("dp", "ctx")),
        P(("dp", "ctx")),
        P("dp", "ctx", None),
    )
    return jax.shard_map(
        body,
        mesh=mesh,
        in_specs=placed,
        out_specs=(
            P("dp", "ctx", None),
            P("dp", "ctx", None),
            P(("dp", "ctx"), "tensor"),
            P(("dp", "ctx"), "tensor", None),
            P(("dp", "ctx"), "tensor"),
            P(("dp", "ctx"), None, "tensor"),
            P(("dp", "ctx"), "tensor"),
            P(("dp", "ctx")),
            P(("dp", "ctx")),
            P(),
        ),
        check_vma=False,
    )
```

time: 1050 us -> 735 us (0.70)
  waiting for transfers between devices: 649 us -> 171 us
  starting transfers between devices: 51.6 us -> 160 us
  Pallas kernels: 29.7 us -> 113 us
  other arithmetic: 123 us -> 54.2 us
  local copies, waits for them, and re-layouts: 29.8 us -> 78.3 us
  blocking collectives: 27.5 us -> 0 us
  between operations: 16.9 us -> 29.8 us
    ppermute x25 -> x55, waiting for transfers between devices: 621 us -> 131 us  [the longest x16 74.5 us: send_in(): return lax.ppermute(part, 'tensor', [(0, 1), (3, 2)])]
    ppermute x25 -> x55, starting transfers between devices: 49.4 us -> 158 us  [the longest x16 83.6 us: send_in(): return lax.ppermute(part, 'tensor', [(0, 1), (3, 2)])]
    pallas_call x0 -> x40, Pallas kernels: none -> 83.5 us  [rowwise(): pl.pallas_call(functools.partial(rowwise_kernel, fn, bounds, len(lists),...]
    convert_element_type x21 -> x3, other arithmetic: 47.2 us -> 2.89 us  [the longest x1 2.86 us: body(): mlp_seed = (seed_flat.astype(F32) * live).astype(BF16)]
    psum x1 -> x0, blocking collectives: 27.5 us -> none  [body(): small = lax.psum(small, ROW_AXES)]
    unnamed x186 -> x353, local copies, waits for them, and re-layouts: 9.39 us -> 36 us
    slice x17 -> x46, local copies, waits for them, and re-layouts: 6.64 us -> 27 us  [the longest x10 7.24 us: held_back(): return value + dep[:1, :1].astype(F32) * 0.0]
    reduce_sum x4 -> x8, other arithmetic: 17.6 us -> 6.15 us  [the longest x3 1.96 us: body(): jnp.sum(x) + jnp.sum(y)]
  transfers between devices with their start and end apart: 34 -> 63, of which waited for: 19 -> 20; matrix products, arithmetic and copies ran while one was open for 21% -> 27% of each run, Pallas kernels for 3% -> 15%
where the time goes in v2:
time: 735 us; the launch traced here: 727 us
  waiting for transfers between devices  171 us (23%)
  starting transfers between devices  160 us (22%)
  matrix products  120 us (16%)
  Pallas kernels  113 us (15%)
  local copies, waits for them, and re-layouts  78.3 us (11%)
  other arithmetic  54.2 us (7%)
  between operations  29.8 us (4%)
    dot_general x22, matrix products, dot(): lax.dot_general(left, right, (((left_dim,), (right_dim,)), ((), ())), pre...  120 us
    ppermute x16, starting transfers between devices, send_in(): return lax.ppermute(part, 'tensor', [(0, 1), (3, 2)])  83.6 us
    pallas_call x40, Pallas kernels, rowwise(): pl.pallas_call(functools.partial(rowwise_kernel, fn, bounds, len(lists),...  83.5 us
    ppermute x16, waiting for transfers between devices, send_in(): return lax.ppermute(part, 'tensor', [(0, 1), (3, 2)])  74.5 us
    ppermute x16, waiting for transfers between devices, send_out(): return lax.ppermute(total, 'tensor', [(1, 0), (2, 3)])  54.3 us
    unnamed x353, local copies, waits for them, and re-layouts  36 us
    all_gather x4, waiting for transfers between devices, gather_rows(): return lax.all_gather(shard, ROW_AXES, axis=0, tiled=True)  34.4 us
    ppermute x2, starting transfers between devices, attend_back_group(): returned = lax.ppermute(sent, 'ctx', [(0, 1), (1, 0)])  24.6 us
  transfers between devices with their start and end apart: 63, of which 20 were waited for; matrix products, arithmetic and copies ran while one was open for 27% of the time, Pallas kernels for 15%

profile of v2, /device:TPU:0, one launch (start us, length us, event | category | flops | bytes accessed | tf_op | source)
XLA Modules:
  0.0 726.6 jit_solution(13155419642030023158)
XLA Ops:
  21.3 25.9 %all-gather.5.cloned.1.call-done = bf16[2048,768]{0,1:T(8,128)(2,1)} async-done(((bf16[256,768]{0,1:T(8,128)(2,1)}), bf16[2048,768]{0,1:T(8,128)(2,1)}) %all-gather.5.cloned.1.call-update) | async-done | bytes 3145744 | tf_op jit(solution)/shard_map/all_gather | solution.py:428
  70.9 8.5 %all-gather.7.cloned.1.call-done = bf16[2048,512]{1,0:T(8,128)(2,1)} async-done(((bf16[256,512]{1,0:T(8,128)(2,1)}), bf16[2048,512]{1,0:T(8,128)(2,1)}) %all-gather.7.cloned.1.call-update) | async-done | bytes 2097168 | tf_op jit(solution)/shard_map/all_gather | solution.py:428
  112.5 18.9 %collective-permute-done.3.refs_1_ = bf16[256,2048]{1,0:T(8,128)(2,1)} collective-permute-done((bf16[256,2048]{1,0:T(8,128)(2,1)S(1)}, bf16[256,2048]{1,0:T(8,128)(2,1)}, u32[]{:S(2)}, u32[]{:S(2)}) %collective-permute-start.3) | collective-permute-done | bytes 1048608 | tf_op jit(solution)/shard_map/ppermute | solution.py:370
  133.5 7.4 %collective-permute-start.9 = (bf16[256,2048]{1,0:T(8,128)(2,1)S(1)}, bf16[256,2048]{1,0:T(8,128)(2,1)S(1)}, u32[]{:S(2)}, u32[]{:S(2)}) collective-permute-start(bf16[256,2048]{1,0:T(8,128)(2,1)S(1)} %convolution_convert_fusion.1.refs_2_.refs_0_), channel_id=1, source_target_pairs={{0,1},{3,2},{4,5},{7,6},{8,9},{11,10},{12,13},{15,14},{16,17},{19,... | collective-permute-start | bytes 3145736 | tf_op jit(solution)/shard_map/ppermute | solution.py:370
  142.5 11.4 %collective-permute-done.5.refs_1_ = bf16[256,2048]{1,0:T(8,128)(2,1)S(1)} collective-permute-done((bf16[256,2048]{1,0:T(8,128)(2,1)S(1)}, bf16[256,2048]{1,0:T(8,128)(2,1)S(1)}, u32[]{:S(2)}, u32[]{:S(2)}) %collective-permute-start.5) | collective-permute-done | bytes 1048608 | tf_op jit(solution)/shard_map/ppermute | solution.py:370
  159.8 15.9 %collective-permute-done.9.refs_1_ = bf16[256,2048]{1,0:T(8,128)(2,1)S(1)} collective-permute-done((bf16[256,2048]{1,0:T(8,128)(2,1)S(1)}, bf16[256,2048]{1,0:T(8,128)(2,1)S(1)}, u32[]{:S(2)}, u32[]{:S(2)}) %collective-permute-start.9) | collective-permute-done | bytes 1048608 | tf_op jit(solution)/shard_map/ppermute | solution.py:370
  180.6 11.1 %collective-permute-done.7.refs_3_ = bf16[256,2048]{1,0:T(8,128)(2,1)S(1)} collective-permute-done((bf16[256,2048]{1,0:T(8,128)(2,1)S(1)}, bf16[256,2048]{1,0:T(8,128)(2,1)S(1)}, u32[]{:S(2)}, u32[]{:S(2)}) %collective-permute-start.7) | collective-permute-done | bytes 1048608 | tf_op jit(solution)/shard_map/ppermute | solution.py:378
  196.0 10.9 %fusion.128.refs_2_ = f32[512,2816]{1,0:T(8,128)S(1)} fusion(bf16[512,2048]{1,0:T(8,128)(2,1)} %copy-done.111, bf16[2048,2816]{1,0:T(8,128)(2,1)} %all-gather.9.cloned.1.call-done), kind=kOutput, calls=%fused_computation.252 | convolution fusion | flops 5905580032 | bytes 19398656 | tf_op jit(solution)/shard_map/dot_general | solution.py:26
  212.2 9.2 %multiply_convert_fusion.6 = (bf16[512,1408]{1,0:T(8,128)(2,1)S(1)}, bf16[512,1408]{1,0:T(8,128)(2,1)S(1)}, bf16[512,1408]{1,0:T(8,128)(2,1)S(1)}) fusion(f32[512,2816]{1,0:T(8,128)} %copy-done.47, bf16[2048,1408]{1,0:T(8,128)(2,1)} %all-gather.11.cloned.1.call-done, bf16[1024,2048]{1,0:T(8,128)(2,1)} %multiply_convert_fusion), kind=kOutput, calls=%fused_computation.54 | convolution fusion | flops 2963603456 | bytes 17956864 | tf_op jit(solution)/shard_map/dot_general | solution.py:26
  222.5 9.4 %convolution_convert_fusion = bf16[512,2048]{1,0:T(8,128)(2,1)S(1)} fusion(bf16[2048,2816]{1,0:T(8,128)(2,1)} %all-gather.9.cloned.1.call-done, bf16[512,1408]{1,0:T(8,128)(2,1)S(1)} %get-tuple-element.123, bf16[512,1408]{1,0:T(8,128)(2,1)S(1)} %get-tuple-element.122), kind=kOutput, calls=%fused_computation.38 | convolution fusion | flops 5912395776 | bytes 16515072 | tf_op jit(solution)/shard_map/dot_general | solution.py:26
  244.8 11.0 %fusion.129.refs_2_ = f32[512,2816]{1,0:T(8,128)S(1)} fusion(bf16[512,2048]{1,0:T(8,128)(2,1)S(1)} %get-tuple-element.48, bf16[2048,2816]{1,0:T(8,128)(2,1)} %all-gather.9.cloned.1.call-done), kind=kOutput, calls=%fused_computation.253 | convolution fusion | flops 5905580032 | bytes 19398656 | tf_op jit(solution)/shard_map/dot_general | solution.py:26
  268.8 9.8 %add_convert_fusion.8 = bf16[512,2048]{1,0:T(8,128)(2,1)S(1)} fusion(bf16[2048,2816]{1,0:T(8,128)(2,1)} %all-gather.9.cloned.1.call-done, bf16[512,1408]{1,0:T(8,128)(2,1)} %get-tuple-element.121, bf16[512,1408]{1,0:T(8,128)(2,1)} %get-tuple-element.120, f32[]{:T(128)} %bitcast.24), kind=kOutput, calls=%fused_computation.37 | convolution fusion | flops 5913444352 | bytes 16515076 | tf_op jit(solution)/shard_map/dot_general | solution.py:26
  302.3 17.6 %add_convert_fusion.refs_9_ = bf16[2048,2816]{1,0:T(8,128)(2,1)} fusion(f32[]{:T(128)} %bitcast.26, bf16[512,1408]{1,0:T(8,128)(2,1)} %get-tuple-element.121, bf16[512,1408]{1,0:T(8,128)(2,1)} %get-tuple-element.120, bf16[512,1408]{1,0:T(8,128)(2,1)} %copy-done.164, bf16[512,1408]{1,0:T(8,128)(2,1)S(1)} %copy-done.163, bf16[512,2048]{1,0:T(8,128)(2,1)} %copy-done.113, ...), kind=kOutput, calls=%fused_computation | convolution fusion | flops 11854151680 | bytes 21495812 | tf_op jit(solution)/shard_map/dot_general | solution.py:26
  331.0 8.6 %bitcast_convert_fusion = f32[1024,2048]{1,0:T(8,128)} fusion(bf16[2,512,2048]{2,1,0:T(8,128)(2,1)} %param.10), kind=kLoop, calls=%fused_computation.228 | loop fusion | flops 2097152 | bytes 12582912 | tf_op jit(solution)/shard_map/convert_element_type | solution.py:493
  349.1 7.5 %collective-permute-done.20.refs_3_ = bf16[256,2048]{1,0:T(8,128)(2,1)S(1)} collective-permute-done((bf16[256,2048]{1,0:T(8,128)(2,1)}, bf16[256,2048]{1,0:T(8,128)(2,1)S(1)}, u32[]{:S(2)}, u32[]{:S(2)}) %collective-permute-start.20) | collective-permute-done | bytes 1048608 | tf_op jit(solution)/shard_map/ppermute | solution.py:378
  356.6 12.0 %collective-permute-done.19.refs_2_ = bf16[256,2048]{1,0:T(8,128)(2,1)S(1)} collective-permute-done((bf16[256,2048]{1,0:T(8,128)(2,1)}, bf16[256,2048]{1,0:T(8,128)(2,1)S(1)}, u32[]{:S(2)}, u32[]{:S(2)}) %collective-permute-start.19) | collective-permute-done | bytes 1048608 | tf_op jit(solution)/shard_map/ppermute | solution.py:378
  412.7 17.3 %collective-permute-start.28 = (f32[512,128]{0,1:T(8,128)}, f32[512,128]{0,1:T(8,128)}, u32[]{:S(2)}, u32[]{:S(2)}) collective-permute-start(f32[512,128]{0,1:T(8,128)} %pad_maximum_fusion.9), channel_id=1, source_target_pairs={{0,4},{4,0},{1,5},{5,1},{2,6},{6,2},{3,7},{7,3},{8,12},{12,8},{9,1... | collective-permute-start | bytes 786440 | tf_op jit(solution)/shard_map/ppermute | solution.py:627
  441.4 8.8 %add_convert_fusion.1 = bf16[2048,1408]{1,0:T(8,128)(2,1)} fusion(bf16[1024,2048]{1,0:T(8,128)(2,1)S(1)} %copy-done.124, f32[]{:T(128)} %bitcast.30, bf16[512,1408]{1,0:T(8,128)(2,1)S(1)} %copy-done.158, bf16[512,1408]{1,0:T(8,128)(2,1)S(1)} %copy-done.161), kind=kOutput, calls=%fused_computation.3 | convolution fusion | flops 5917114368 | bytes 12845060 | tf_op jit(solution)/shard_map/dot_general | solution.py:26
  463.7 7.4 %collective-permute-start.30 = (bf16[256,2048]{1,0:T(8,128)(2,1)}, bf16[256,2048]{1,0:T(8,128)(2,1)}, u32[]{:S(2)}, u32[]{:S(2)}) collective-permute-start(bf16[256,2048]{1,0:T(8,128)(2,1)} %get-tuple-element.131.refs_0_), channel_id=1, source_target_pairs={{0,1},{3,2},{4,5},{7,6},{8,9},{11,10},{12,13},{15,14},{16,17},{19,... | collective-permute-start | bytes 3145736 | tf_op jit(solution)/shard_map/ppermute | solution.py:370
  508.4 7.3 %collective-permute-start.34 = (f32[512,128]{0,1:T(8,128)S(1)}, f32[512,128]{0,1:T(8,128)S(1)}, u32[]{:S(2)}, u32[]{:S(2)}) collective-permute-start(f32[512,128]{0,1:T(8,128)S(1)} %pad_maximum_fusion.10), channel_id=1, source_target_pairs={{0,4},{4,0},{1,5},{5,1},{2,6},{6,2},{3,7},{7,3},{8,12},{12,8},{9,1... | collective-permute-start | bytes 786440 | tf_op jit(solution)/shard_map/ppermute | solution.py:627
  544.8 12.6 %collective-permute-start.36 = (bf16[256,2048]{1,0:T(8,128)(2,1)}, bf16[256,2048]{1,0:T(8,128)(2,1)S(1)}, u32[]{:S(2)}, u32[]{:S(2)}) collective-permute-start(bf16[256,2048]{1,0:T(8,128)(2,1)} %get-tuple-element.133.refs_0_), channel_id=1, source_target_pairs={{0,1},{3,2},{4,5},{7,6},{8,9},{11,10},{12,13},{15,14},{16,17},{19,... | collective-permute-start | bytes 3145736 | tf_op jit(solution)/shard_map/ppermute | solution.py:370
  559.5 7.5 %collective-permute-start.39 = (bf16[256,2048]{1,0:T(8,128)(2,1)}, bf16[256,2048]{1,0:T(8,128)(2,1)S(1)}, u32[]{:S(2)}, u32[]{:S(2)}) collective-permute-start(bf16[256,2048]{1,0:T(8,128)(2,1)} %copy-done.31), channel_id=1, source_target_pairs={{0,1},{3,2},{4,5},{7,6},{8,9},{11,10},{12,13},{15,14},{16,17},{19,... | collective-permute-start | bytes 3145736 | tf_op jit(solution)/shard_map/ppermute | solution.py:370
  568.2 13.0 %collective-permute-done.36.refs_1_ = bf16[256,2048]{1,0:T(8,128)(2,1)S(1)} collective-permute-done((bf16[256,2048]{1,0:T(8,128)(2,1)}, bf16[256,2048]{1,0:T(8,128)(2,1)S(1)}, u32[]{:S(2)}, u32[]{:S(2)}) %collective-permute-start.36) | collective-permute-done | bytes 1048608 | tf_op jit(solution)/shard_map/ppermute | solution.py:370
  644.3 8.1 %collective-permute-done.44.refs_2_ = bf16[256,2048]{1,0:T(8,128)(2,1)} collective-permute-done((bf16[256,2048]{1,0:T(8,128)(2,1)}, bf16[256,2048]{1,0:T(8,128)(2,1)}, u32[]{:S(2)}, u32[]{:S(2)}) %collective-permute-start.44) | collective-permute-done | bytes 1048608 | tf_op jit(solution)/shard_map/ppermute | solution.py:378
  (676 shorter events, 419.7 us)
Async XLA Ops:
  7.2 40.0 %all-gather.5.cloned.1.call-start = ((), (), s32[]{:S(2)}) async-start(), calls=%async_computation.3 | async-start | bytes 3538944 | tf_op jit(solution)/shard_map/all_gather | solution.py:428
  11.5 67.9 %all-gather.7.cloned.1.call-start = ((), (), s32[]{:S(2)}) async-start(), calls=%async_computation.4 | async-start | bytes 2359296 | tf_op jit(solution)/shard_map/all_gather | solution.py:428
  12.3 183.7 %all-gather.9.cloned.1.call-start = ((), (), s32[]{:S(2)}) async-start(), calls=%async_computation.5 | async-start | bytes 12976128 | tf_op jit(solution)/shard_map/all_gather | solution.py:428
  13.6 198.6 %all-gather.11.cloned.1.call-start = ((), (), s32[]{:S(2)}) async-start(), calls=%async_computation.6 | async-start | bytes 6488064 | tf_op jit(solution)/shard_map/all_gather | solution.py:428
  14.2 603.2 %reduce-scatter.4.cloned.1.call-start = ((), (), s32[]{:S(2)}) async-start(), calls=%async_computation.7 | async-start | bytes 12976128 | tf_op jit(solution)/shard_map/reduce_scatter | solution.py:432
  103.0 50.9 %collective-permute-start.5 = (bf16[256,2048]{1,0:T(8,128)(2,1)S(1)}, bf16[256,2048]{1,0:T(8,128)(2,1)S(1)}, u32[]{:S(2)}, u32[]{:S(2)}) collective-permute-start(bf16[256,2048]{1,0:T(8,128)(2,1)S(1)} %convolution_convert_fusion.3.refs_2_.refs_0_), channel_id=1, source_target_pairs={{0,1},{3,2},{4,5},{7,6},{8,9},{11,10},{12,13},{15,14},{16,17},{19,... | collective-permute-start | bytes 3145736 | tf_op jit(solution)/shard_map/ppermute | solution.py:370
  133.5 42.2 %collective-permute-start.9 = (bf16[256,2048]{1,0:T(8,128)(2,1)S(1)}, bf16[256,2048]{1,0:T(8,128)(2,1)S(1)}, u32[]{:S(2)}, u32[]{:S(2)}) collective-permute-start(bf16[256,2048]{1,0:T(8,128)(2,1)S(1)} %convolution_convert_fusion.1.refs_2_.refs_0_), channel_id=1, source_target_pairs={{0,1},{3,2},{4,5},{7,6},{8,9},{11,10},{12,13},{15,14},{16,17},{19,... | collective-permute-start | bytes 3145736 | tf_op jit(solution)/shard_map/ppermute | solution.py:370
  178.9 59.8 %collective-permute-start.12 = (bf16[256,2048]{1,0:T(8,128)(2,1)S(1)}, bf16[256,2048]{1,0:T(8,128)(2,1)}, u32[]{:S(2)}, u32[]{:S(2)}) collective-permute-start(bf16[256,2048]{1,0:T(8,128)(2,1)S(1)} %total.18.refs_6_.refs_0_), channel_id=1, source_target_pairs={{1,0},{2,3},{5,4},{6,7},{9,8},{10,11},{13,12},{14,15},{17,16},{18,... | collective-permute-start | bytes 3145736 | tf_op jit(solution)/shard_map/ppermute | solution.py:378
  237.1 47.7 %collective-permute-start.15 = (bf16[256,2048]{1,0:T(8,128)(2,1)S(1)}, bf16[256,2048]{1,0:T(8,128)(2,1)S(1)}, u32[]{:S(2)}, u32[]{:S(2)}) collective-permute-start(bf16[256,2048]{1,0:T(8,128)(2,1)S(1)} %get-tuple-element.139.refs_6_.refs_0_), channel_id=1, source_target_pairs={{0,1},{3,2},{4,5},{7,6},{8,9},{11,10},{12,13},{15,14},{16,17},{19,... | collective-permute-start | bytes 3145736 | tf_op jit(solution)/shard_map/ppermute | solution.py:370
  319.9 339.8 %reduce-scatter.8.cloned.1.call-start = ((), (), s32[]{:S(2)}) async-start(), calls=%async_computation.9 | async-start | bytes 6488064 | tf_op jit(solution)/shard_map/reduce_scatter | solution.py:432
  322.7 51.1 %collective-permute-start.22 = (bf16[256,2048]{1,0:T(8,128)(2,1)}, bf16[256,2048]{1,0:T(8,128)(2,1)S(1)}, u32[]{:S(2)}, u32[]{:S(2)}) collective-permute-start(bf16[256,2048]{1,0:T(8,128)(2,1)} %copy-done.33), channel_id=1, source_target_pairs={{0,1},{3,2},{4,5},{7,6},{8,9},{11,10},{12,13},{15,14},{16,17},{19,... | collective-permute-start | bytes 3145736 | tf_op jit(solution)/shard_map/ppermute | solution.py:370
  329.7 38.9 %collective-permute-start.19 = (bf16[256,2048]{1,0:T(8,128)(2,1)}, bf16[256,2048]{1,0:T(8,128)(2,1)S(1)}, u32[]{:S(2)}, u32[]{:S(2)}) collective-permute-start(bf16[256,2048]{1,0:T(8,128)(2,1)} %copy-done.23), channel_id=1, source_target_pairs={{1,0},{2,3},{5,4},{6,7},{9,8},{10,11},{13,12},{14,15},{17,16},{18,... | collective-permute-start | bytes 3145736 | tf_op jit(solution)/shard_map/ppermute | solution.py:378
  339.7 48.2 %collective-permute-start.21 = (bf16[256,2048]{1,0:T(8,128)(2,1)}, bf16[256,2048]{1,0:T(8,128)(2,1)}, u32[]{:S(2)}, u32[]{:S(2)}) collective-permute-start(bf16[256,2048]{1,0:T(8,128)(2,1)} %pair.22.refs_2_.refs_0_), channel_id=1, source_target_pairs={{1,2},{2,1},{5,6},{6,5},{9,10},{10,9},{13,14},{14,13},{17,18},{18,... | collective-permute-start | bytes 3145736 | tf_op jit(solution)/shard_map/ppermute | solution.py:374
  342.2 87.7 %collective-permute-start.16 = (bf16[256,2048]{1,0:T(8,128)(2,1)}, bf16[256,2048]{1,0:T(8,128)(2,1)}, u32[]{:S(2)}, u32[]{:S(2)}) collective-permute-start(bf16[256,2048]{1,0:T(8,128)(2,1)} %get-tuple-element.134.refs_0_), channel_id=1, source_target_pairs={{0,1},{3,2},{4,5},{7,6},{8,9},{11,10},{12,13},{15,14},{16,17},{19,... | collective-permute-start | bytes 3145736 | tf_op jit(solution)/shard_map/ppermute | solution.py:370
  376.8 60.7 %collective-permute-start.26 = (bf16[256,2048]{1,0:T(8,128)(2,1)}, bf16[256,2048]{1,0:T(8,128)(2,1)}, u32[]{:S(2)}, u32[]{:S(2)}) collective-permute-start(bf16[256,2048]{1,0:T(8,128)(2,1)} %pair.23.refs_2_.refs_0_), channel_id=1, source_target_pairs={{1,2},{2,1},{5,6},{6,5},{9,10},{10,9},{13,14},{14,13},{17,18},{18,... | collective-permute-start | bytes 3145736 | tf_op jit(solution)/shard_map/ppermute | solution.py:374
  384.9 101.0 %collective-permute-start.24 = (bf16[256,2048]{1,0:T(8,128)(2,1)}, bf16[256,2048]{1,0:T(8,128)(2,1)}, u32[]{:S(2)}, u32[]{:S(2)}) collective-permute-start(bf16[256,2048]{1,0:T(8,128)(2,1)} %copy-done.29), channel_id=1, source_target_pairs={{0,1},{3,2},{4,5},{7,6},{8,9},{11,10},{12,13},{15,14},{16,17},{19,... | collective-permute-start | bytes 3145736 | tf_op jit(solution)/shard_map/ppermute | solution.py:370
  391.6 84.5 %collective-permute-start.25 = (bf16[256,2048]{1,0:T(8,128)(2,1)}, bf16[256,2048]{1,0:T(8,128)(2,1)}, u32[]{:S(2)}, u32[]{:S(2)}) collective-permute-start(bf16[256,2048]{1,0:T(8,128)(2,1)} %total.22.refs_4_.refs_0_), channel_id=1, source_target_pairs={{1,0},{2,3},{5,4},{6,7},{9,8},{10,11},{13,12},{14,15},{17,16},{18,... | collective-permute-start | bytes 3145736 | tf_op jit(solution)/shard_map/ppermute | solution.py:378
  435.8 54.1 %collective-permute-start.23 = (bf16[256,2048]{1,0:T(8,128)(2,1)}, bf16[256,2048]{1,0:T(8,128)(2,1)}, u32[]{:S(2)}, u32[]{:S(2)}) collective-permute-start(bf16[256,2048]{1,0:T(8,128)(2,1)} %pair.24.refs_2_.refs_0_), channel_id=1, source_target_pairs={{1,2},{2,1},{5,6},{6,5},{9,10},{10,9},{13,14},{14,13},{17,18},{18,... | collective-permute-start | bytes 3145736 | tf_op jit(solution)/shard_map/ppermute | solution.py:374
  450.1 211.9 %reduce-scatter.6.cloned.1.call-start = ((), (), s32[]{:S(2)}) async-start(), calls=%async_computation.8 | async-start | bytes 5898240 | tf_op jit(solution)/shard_map/reduce_scatter | solution.py:432
  463.7 52.1 %collective-permute-start.30 = (bf16[256,2048]{1,0:T(8,128)(2,1)}, bf16[256,2048]{1,0:T(8,128)(2,1)}, u32[]{:S(2)}, u32[]{:S(2)}) collective-permute-start(bf16[256,2048]{1,0:T(8,128)(2,1)} %get-tuple-element.131.refs_0_), channel_id=1, source_target_pairs={{0,1},{3,2},{4,5},{7,6},{8,9},{11,10},{12,13},{15,14},{16,17},{19,... | collective-permute-start | bytes 3145736 | tf_op jit(solution)/shard_map/ppermute | solution.py:370
  476.0 50.2 %collective-permute-start.33 = (bf16[256,2048]{1,0:T(8,128)(2,1)}, bf16[256,2048]{1,0:T(8,128)(2,1)}, u32[]{:S(2)}, u32[]{:S(2)}) collective-permute-start(bf16[256,2048]{1,0:T(8,128)(2,1)} %get-tuple-element.130.refs_0_), channel_id=1, source_target_pairs={{0,1},{3,2},{4,5},{7,6},{8,9},{11,10},{12,13},{15,14},{16,17},{19,... | collective-permute-start | bytes 3145736 | tf_op jit(solution)/shard_map/ppermute | solution.py:370
  559.5 45.8 %collective-permute-start.39 = (bf16[256,2048]{1,0:T(8,128)(2,1)}, bf16[256,2048]{1,0:T(8,128)(2,1)S(1)}, u32[]{:S(2)}, u32[]{:S(2)}) collective-permute-start(bf16[256,2048]{1,0:T(8,128)(2,1)} %copy-done.31), channel_id=1, source_target_pairs={{0,1},{3,2},{4,5},{7,6},{8,9},{11,10},{12,13},{15,14},{16,17},{19,... | collective-permute-start | bytes 3145736 | tf_op jit(solution)/shard_map/ppermute | solution.py:370
  566.9 40.9 %collective-permute-start.40 = (bf16[256,2048]{1,0:T(8,128)(2,1)}, bf16[256,2048]{1,0:T(8,128)(2,1)S(1)}, u32[]{:S(2)}, u32[]{:S(2)}) collective-permute-start(bf16[256,2048]{1,0:T(8,128)(2,1)} %copy-done.35), channel_id=1, source_target_pairs={{1,0},{2,3},{5,4},{6,7},{9,8},{10,11},{13,12},{14,15},{17,16},{18,... | collective-permute-start | bytes 3145736 | tf_op jit(solution)/shard_map/ppermute | solution.py:378
  671.9 39.3 %collective-permute-start.49 = (bf16[256,2048]{1,0:T(8,128)(2,1)}, bf16[256,2048]{1,0:T(8,128)(2,1)}, u32[]{:S(2)}, u32[]{:S(2)}) collective-permute-start(bf16[256,2048]{1,0:T(8,128)(2,1)} %total.30.refs_7_.refs_0_), channel_id=1, source_target_pairs={{1,0},{2,3},{5,4},{6,7},{9,8},{10,11},{13,12},{14,15},{17,16},{18,... | collective-permute-start | bytes 3145736 | tf_op jit(solution)/shard_map/ppermute | solution.py:378
  (211 other events, 2784.3 us)
Sparse Core Ops, SparseCore 0:
  11.6 35.5 all-gather.4
  49.1 30.2 all-gather.6
  81.9 67.6 all-gather.8
  151.3 43.3 all-gather.10
  320.0 92.7 reduce-scatter.3
  450.3 65.7 reduce-scatter.7
  544.9 64.0 reduce-scatter.5

commit v3 on v2

--- a/solution.py
+++ b/solution.py
@@ -50,11 +50,11 @@
     return beside([ref[r : r + 1, :] for r in rows])
 
 
-def attend_kernel(heads, blocks, flags, q_ref, info_ref, k_ref, vt_ref, code_ref, o_ref, lse_ref, m_ref, l_ref, acc_ref):
+def attend_kernel(heads, blocks, first, flags, q_ref, info_ref, k_ref, vt_ref, code_ref, o_ref, lse_ref, m_ref, l_ref, acc_ref):
     m_ref[...] = jnp.full_like(m_ref, NEG_FILL)
     l_ref[...] = jnp.zeros_like(l_ref)
     acc_ref[...] = jnp.zeros_like(acc_ref)
-    row = pl.program_id(0)
+    row = first + pl.program_id(0)
 
     def step(kb, carry):
         @pl.when(flags[row * blocks + kb] > 0)
@@ -89,22 +89,24 @@
         o_ref[part, :] = (acc_ref[part, :] / total[h : h + 1, :]).astype(BF16)
 
 
-def attend(flags, q_t, info, keys, values_t, codes):
-    width, rows = q_t.shape
+def attend(flags, q_t, info, keys, values_t, codes, first, base, steps):
+    width = q_t.shape[0]
+    rows = steps * BQ
     heads = width // HD
     count = keys.shape[0]
     blocks = count // BK
     whole = lambda i, f: (0, 0)
-    column = lambda i, f: (0, i)
+    column = lambda i, f: (0, base + first + i)
+    made = lambda i, f: (0, i)
     return pl.pallas_call(
-        functools.partial(attend_kernel, heads, blocks),
+        functools.partial(attend_kernel, heads, blocks, first),
         out_shape=(
             jax.ShapeDtypeStruct((width, rows), BF16),
             jax.ShapeDtypeStruct((heads, rows), F32),
         ),
         grid_spec=pltpu.PrefetchScalarGridSpec(
             num_scalar_prefetch=1,
-            grid=(rows // BQ,),
+            grid=(steps,),
             in_specs=[
                 pl.BlockSpec((width, BQ), column),
                 pl.BlockSpec((2, BQ), column),
@@ -112,7 +114,7 @@
                 pl.BlockSpec((HD, count), whole),
                 pl.BlockSpec((count, 1), whole),
             ],
-            out_specs=[pl.BlockSpec((width, BQ), column), pl.BlockSpec((heads, BQ), column)],
+            out_specs=[pl.BlockSpec((width, BQ), made), pl.BlockSpec((heads, BQ), made)],
             scratch_shapes=[
                 pltpu.VMEM((heads, BQ), F32),
                 pltpu.VMEM((heads, BQ), F32),
@@ -126,15 +128,13 @@
 
 
 def attend_back_kernel(
-    heads, blocks, flags, q_ref, do_ref, o_ref, lse_ref, info_ref, cos_ref, sin_ref, k_ref, v_ref, kt_ref, code_ref,
-    dq_ref, dk_ref, dv_ref, acc_ref, delta_ref,
+    heads, blocks, first, carried, flags, q_ref, do_ref, o_ref, lse_ref, info_ref, cos_ref, sin_ref, k_ref, v_ref, kt_ref,
+    code_ref, *refs
 ):
-    row = pl.program_id(0)
-
-    @pl.when(row == 0)
-    def _():
-        dk_ref[...] = jnp.zeros_like(dk_ref)
-        dv_ref[...] = jnp.zeros_like(dv_ref)
+    row = first
+    dq_ref, own_ref, other_ref, acc_ref, delta_ref, dk_ref, dv_ref = refs[-7:]
+    dk_ref[...] = jnp.zeros_like(dk_ref)
+    dv_ref[...] = jnp.zeros_like(dv_ref)
 
     acc_ref[...] = jnp.zeros_like(acc_ref)
     for h in range(heads):
@@ -178,30 +178,35 @@
         upper = acc_ref[h * HD + half : (h + 1) * HD, :] * HD**-0.5
         dq_ref[h * HD : h * HD + half, :] = (lower * cosine + upper * sine).astype(BF16)
         dq_ref[h * HD + half : (h + 1) * HD, :] = (upper * cosine - lower * sine).astype(BF16)
-
-
-def attend_back(flags, q_t, grad_t, o_t, lse, info, cosine_t, sine_t, keys, values, keys_t, codes):
-    width, rows = q_t.shape
+    half_count = own_ref.shape[0]
+    for ref, lo, more in ((own_ref, 0, refs[0]), (other_ref, half_count, refs[1])):
+        made = beside([dk_ref[lo : lo + half_count, :], dv_ref[lo : lo + half_count, :]])
+        ref[...] = made + more[...] if carried else made
+
+
+def attend_back(flags, q_t, grad_t, o_t, lse, info, cosine_t, sine_t, keys, values, keys_t, codes, first, base, carry):
+    width = q_t.shape[0]
     heads = width // HD
     count = keys.shape[0]
     blocks = count // BK
     whole = lambda i, f: (0, 0)
-    column = lambda i, f: (0, i)
+    column = lambda i, f: (0, base + first)
+    pair = pl.BlockSpec((count // 2, 2 * HD), whole)
     return pl.pallas_call(
-        functools.partial(attend_back_kernel, heads, blocks),
+        functools.partial(attend_back_kernel, heads, blocks, first, carry is not None),
         out_shape=(
-            jax.ShapeDtypeStruct((width, rows), BF16),
-            jax.ShapeDtypeStruct((count, HD), F32),
-            jax.ShapeDtypeStruct((count, HD), F32),
+            jax.ShapeDtypeStruct((width, BQ), BF16),
+            jax.ShapeDtypeStruct((count // 2, 2 * HD), F32),
+            jax.ShapeDtypeStruct((count // 2, 2 * HD), F32),
         ),
         grid_spec=pltpu.PrefetchScalarGridSpec(
             num_scalar_prefetch=1,
-            grid=(rows // BQ,),
+            grid=(1,),
             in_specs=[
                 pl.BlockSpec((width, BQ), column),
-                pl.BlockSpec((width, BQ), column),
-                pl.BlockSpec((width, BQ), column),
-                pl.BlockSpec((heads, BQ), column),
+                pl.BlockSpec((width, BQ), lambda i, f: (0, first)),
+                pl.BlockSpec((width, BQ), whole),
+                pl.BlockSpec((heads, BQ), whole),
                 pl.BlockSpec((2, BQ), column),
                 pl.BlockSpec((HD // 2, BQ), column),
                 pl.BlockSpec((HD // 2, BQ), column),
@@ -209,18 +214,20 @@
                 pl.BlockSpec((count, HD), whole),
                 pl.BlockSpec((HD, count), whole),
                 pl.BlockSpec((count, 1), whole),
+            ]
+            + ([pair, pair] if carry is not None else []),
+            out_specs=[pl.BlockSpec((width, BQ), whole), pair, pair],
+            scratch_shapes=[
+                pltpu.VMEM((width, BQ), F32),
+                pltpu.VMEM((heads, BQ), F32),
+                pltpu.VMEM((count, HD), F32),
+                pltpu.VMEM((count, HD), F32),
             ],
-            out_specs=[
-                pl.BlockSpec((width, BQ), column),
-                pl.BlockSpec((count, HD), whole),
-                pl.BlockSpec((count, HD), whole),
-            ],
-            scratch_shapes=[pltpu.VMEM((width, BQ), F32), pltpu.VMEM((heads, BQ), F32)],
         ),
         compiler_params=pltpu.CompilerParams(vmem_limit_bytes=32 << 20),
         cost_estimate=SMALL_COST,
         name="attend_back",
-    )(flags, q_t, grad_t, o_t, lse, info, cosine_t, sine_t, keys, values, keys_t, codes)
+    )(flags, q_t, grad_t, o_t, lse, info, cosine_t, sine_t, keys, values, keys_t, codes, *(carry or ()))
 
 
 def block_flags(codes, starts, key_codes):
@@ -355,6 +362,10 @@
     return [grad_middle + scale * weighted - tokens * scale**3 * mean], []
 
 
+def gain_fn(choice, lists, flats, consts):
+    return [], [column_sum(lists[0] * flats[0] * row_scale(flats[0]))]
+
+
 def result_fn(choice, lists, flats, consts):
     mlp_branch = pick(choice, lists[0], lists[1])
     tokens, branch, live = flats
@@ -366,6 +377,34 @@
     ]
 
 
+def pair_back_kernel(own_ref, returned_ref, cos_ref, sin_ref, out_ref):
+    both = (own_ref[...] + returned_ref[...]).T
+    half = HD // 2
+    low, high = both[:half, :], both[half:HD, :]
+    cosine, sine = cos_ref[...], sin_ref[...]
+    out_ref[:half, :] = (low * cosine + high * sine).astype(BF16)
+    out_ref[half:HD, :] = (high * cosine - low * sine).astype(BF16)
+    out_ref[HD:, :] = both[HD:, :].astype(BF16)
+
+
+def pair_back(own, returned, cosine_t, sine_t, block):
+    rows = own.shape[0]
+    whole = pl.BlockSpec((rows, 2 * HD), lambda i: (0, 0))
+    table = pl.BlockSpec((HD // 2, rows), lambda i: (0, block))
+    return pl.pallas_call(
+        pair_back_kernel,
+        out_shape=jax.ShapeDtypeStruct((2 * HD, rows), BF16),
+        grid_spec=pltpu.PrefetchScalarGridSpec(
+            num_scalar_prefetch=0,
+            grid=(1,),
+            in_specs=[whole, whole, table, table],
+            out_specs=pl.BlockSpec((2 * HD, rows), lambda i: (0, 0)),
+        ),
+        cost_estimate=SMALL_COST,
+        name="pair_back",
+    )(own, returned, cosine_t, sine_t)
+
+
 def send_in(part):
     return lax.ppermute(part, "tensor", [(0, 1), (3, 2)])
 
@@ -397,6 +436,11 @@
         self.last = got[0]
         return got
 
+    def ordered_sum(self, fn, lists, flats, name):
+        got = rowwise(fn, self.choice, lists, flats, [], [], sums=1, after=(self.last,), name=name)
+        self.last = got[0]
+        return got[0]
+
     def push(self, k, part):
         self.order.append(k)
         self.parts[k] = part
@@ -404,8 +448,8 @@
 
     def pair(self, k, after=()):
         spot = self.order.index(k)
-        if spot >= 3:
-            after = tuple(after) + (self.thirds[self.order[spot - 3]],)
+        if spot == 3:
+            after = tuple(after) + (self.thirds[self.order[0]],)
         both = [[self.parts[k]], [self.firsts[k]]]
         self.pairs[k] = self.ordered(add_fn, both, [], [], [BF16], after=after, name="pair")[0]
         self.seconds[k] = send_across(self.pairs[k])
@@ -426,6 +470,23 @@
 
 def gather_rows(shard):
     return lax.all_gather(shard, ROW_AXES, axis=0, tiled=True)
+
+
+def same(ref, *rest):
+    pass
+
+
+def once(value, after):
+    anywhere = pl.BlockSpec(memory_space=pl.ANY)
+    return pl.pallas_call(
+        same,
+        out_shape=jax.ShapeDtypeStruct(value.shape, value.dtype),
+        in_specs=[anywhere] * (1 + len(after)),
+        out_specs=anywhere,
+        input_output_aliases={0: 0},
+        cost_estimate=SMALL_COST,
+        name="once",
+    )(value, *after)
 
 
 def scatter_rows(grads):
@@ -531,18 +592,16 @@
 
     def attend_chunk(group, k):
         g = groups[group]
-        blocks = 2 * span // BK * chunk // BQ
-        lo = group * span + k * chunk
-        at = slice(lo, lo + chunk)
-        flags = g["flags"][k * blocks : (k + 1) * blocks]
-        context, lse = attend(flags, q_t[:, at], info[:, at], g["keys"], g["values_t"], g["codes"])
+        context, lse = attend(
+            g["flags"], q_t, info, g["keys"], g["values_t"], g["codes"], k, group * span // BQ, chunk // BQ
+        )
         g["context"].append(context)
         g["lse"].append(lse)
         return dot(context, output_w, 0, 1)
 
-    def push(k, part):
-        for n in range(part.shape[0] // chunk):
-            sums.push(k + n, part[n * chunk : (n + 1) * chunk].astype(BF16))
+    def push(k, part, size=chunk):
+        for n in range(part.shape[0] // size):
+            sums.push(k + n, part[n * size : (n + 1) * size].astype(BF16))
 
     push(0, attend_chunk(0, 0))
     push(1, attend_chunk(0, 1))
@@ -585,12 +644,17 @@
     push(6, held_back(dot(grad_gateup_two, gateup_w, 1, 1), sums.last))
     sums.pair(5, (sums.parts[7],))
     sums.total(4)
-    push(8, held_back(dot(hidden_one, down_w, 1, 1), sums.last))
-    sums.pair(6, (sums.parts[9],))
+    hidden = join([hidden_one, hidden_two])
+    push(8, held_back(dot(hidden_one, down_w, 1, 1), sums.last), span)
+    push(10, held_back(dot(hidden_two, down_w, 1, 1), sums.parts[8]), span)
+    sums.pair(6, (sums.parts[10], sums.thirds[4]))
     sums.total(5)
     grad_gateup_w = held_back(
         dot(join([normed_one, normed_two]), join([grad_gateup_one, grad_gateup_two]), 0, 0), sums.last
     ).astype(BF16)
+    sums.pair(7, (grad_gateup_w, sums.thirds[5]))
+    sums.total(6)
+    grad_gateup_w = scatter_rows(once(grad_gateup_w, (sums.totals[6],)))
 
     def grad_middle_of(first, at, attn_out, after=()):
         return sums.ordered(
@@ -604,63 +668,46 @@
             name="grad_middle",
         )
 
-    def attend_back_group(group, grad_context_t):
+    def attend_back_group(group, seeds):
         g = groups[group]
-        blocks = 2 * span // BK * chunk // BQ
-        grad_q, grad_keys, grad_values = [], 0.0, 0.0
-        at = slice(group * span, (group + 1) * span)
-        got = attend_back(
-            g["flags"],
-            q_t[:, at],
-            grad_context_t,
-            jnp.concatenate(g["context"], axis=1),
-            jnp.concatenate(g["lse"], axis=1),
-            info[:, at],
-            cosine_t[:, at],
-            sine_t[:, at],
-            g["keys"],
-            g["values"],
-            g["keys_t"],
-            g["codes"],
-        )
-        sent = jnp.concatenate([got[1][span:], got[2][span:]], axis=1)
-        returned = lax.ppermute(sent, "ctx", [(0, 1), (1, 0)])
-        own_keys = got[1][:span] + returned[:, :HD]
-        own_values = got[2][:span] + returned[:, HD:]
-        low, high = own_keys[:, :half], own_keys[:, half:]
-        cos_rows, sin_rows = cosine[at], sine[at]
-        grad_pair = jnp.concatenate([low * cos_rows + high * sin_rows, high * cos_rows - low * sin_rows, own_values], axis=1)
-        return got[0], jnp.concatenate([got[0], grad_pair.astype(BF16).T], axis=0)
-
-    grad_middle_one, attn_seed_one, gain_mlp_one = grad_middle_of(4, one, attn_out_one, (grad_gateup_w,))
-    sums.pair(7)
-    sums.total(6)
-    grad_context_t = held_back(dot(output_w, attn_seed_one, 0, 1), sums.last).astype(BF16)
-    grad_q_one, grad_qkv_one = attend_back_group(0, grad_context_t)
-    sums.pair(8, (grad_q_one,))
-    sums.total(7)
-    grad_down = held_back(dot(mlp_seed, join([hidden_one, hidden_two]), 0, 0), sums.last).astype(BF16)
-    grad_gateup_w = scatter_rows(grad_gateup_w)
-    push(12, held_back(dot(grad_qkv_one, qkv_w, 0, 1), grad_down))
-    push(10, held_back(dot(hidden_two, down_w, 1, 1), sums.parts[13]))
-    grad_middle_two, attn_seed_two, gain_mlp_two = grad_middle_of(6, two, attn_out_two, (sums.parts[11],))
-    sums.pair(9)
+        grad_context_t = held_back(dot(output_w, seeds, 0, 1), sums.last).astype(BF16)
+        carry, grads = None, []
+        for k in range(2):
+            grad_q, *carry = attend_back(
+                g["flags"], q_t, grad_context_t, g["context"][k], g["lse"][k], info, cosine_t, sine_t,
+                g["keys"], g["values"], g["keys_t"], g["codes"], k, group * span // BQ, carry,
+            )
+            grads.append(grad_q)
+        returned = lax.ppermute(carry[1], "ctx", [(0, 1), (1, 0)])
+        grad_pair = pair_back(carry[0], returned, cosine_t, sine_t, group)
+        g["grad"] = jnp.concatenate([jnp.concatenate(grads, axis=1), grad_pair], axis=0)
+        return grads[1]
+
+    def attn_back_of(group):
+        return dot(groups[group]["grad"], qkv_w, 0, 1)
+
+    grad_middle_one, attn_seed_one, gain_mlp_one = grad_middle_of(4, one, attn_out_one)
+    sums.total(7, (sums.thirds[6],))
+    done = attend_back_group(0, attn_seed_one)
+    sums.pair(8, (done,))
+    grad_middle_two, attn_seed_two, gain_mlp_two = grad_middle_of(6, two, attn_out_two)
+    push(12, held_back(attn_back_of(0), sums.last))
+    done = attend_back_group(1, attn_seed_two)
+    sums.pair(10, (done, sums.parts[13]))
     sums.total(8)
-    grad_context_t = held_back(dot(output_w, attn_seed_two, 0, 1), sums.last).astype(BF16)
-    grad_q_two, grad_qkv_two = attend_back_group(1, grad_context_t)
-    sums.pair(12, (grad_q_two,))
-    sums.total(9)
-    push(14, held_back(dot(grad_qkv_two, qkv_w, 0, 1), sums.last))
-    grad_down = scatter_rows(grad_down)
-    gain_attn_part = 0.0
-    for k in range(4):
-        at = slice(k * chunk, (k + 1) * chunk)
-        gain_attn_part = gain_attn_part + jnp.sum(sums.parts[12 + k].astype(F32) * tokens[at] * attn_scale[at], axis=0)
-    sums.pair(13, (sums.parts[15],))
+    grad_down = held_back(dot(mlp_seed, hidden, 0, 0), sums.last).astype(BF16)
+    push(14, held_back(attn_back_of(1), grad_down))
+    sums.pair(12, (sums.parts[15],))
+    sums.pair(13, (sums.thirds[8],))
+    sums.total(10)
+    grad_down = scatter_rows(once(grad_down, (sums.totals[10], grad_gateup_w)))
     sums.total(12)
-    extra = jnp.concatenate([fold(gain_attn_part, width), fold((gain_mlp_one + gain_mlp_two)[0], width)], axis=1)
+    gain_attn_part = sums.ordered_sum(
+        gain_fn, [[sums.parts[12 + k] for k in range(4)]], [(hidden_flat, 0)], "gain_attn"
+    )
+    extra = jnp.concatenate([fold(gain_attn_part[0], width), fold((gain_mlp_one + gain_mlp_two)[0], width)], axis=1)
     extra = jnp.pad(extra, ((0, 0), (0, 126)))
-    grad_qkv_t = jnp.concatenate([grad_qkv_one, grad_qkv_two], axis=1)
+    grad_qkv_t = jnp.concatenate([groups[0]["grad"], groups[1]["grad"]], axis=1)
     context_t = jnp.concatenate(groups[0]["context"] + groups[1]["context"], axis=1)
     last = jnp.concatenate(
         [
@@ -674,7 +721,7 @@
     def result_of(first, at, attn_out, after=()):
         return sums.ordered(
             result_fn,
-            sums.of([first, first + 1]),
+            sums.of([first]),
             [(hidden_flat, at.start), (attn_out, 0), (live, at.start)],
             [],
             [BF16],
@@ -694,19 +741,15 @@
             name="input_grad",
         )[0]
 
-    sums.pair(10, (last,))
+    sums.pair(14, (last,))
     sums.total(13)
-    last = scatter_rows(last)
+    sums.pair(15, (sums.thirds[10],))
+    sums.total(14)
+    last = scatter_rows(once(last, (sums.totals[14], grad_down)))
+    sums.total(15)
     output_one, *squares_one = result_of(8, one, attn_out_one)
-    sums.pair(11)
-    sums.total(10)
-    sums.pair(14, (grad_gateup_w,))
-    sums.total(11)
+    output_two, *squares_two = result_of(10, two, attn_out_two)
     input_grad_one = input_grad_of(12, one, grad_middle_one)
-    sums.pair(15)
-    sums.total(14)
-    output_two, *squares_two = result_of(10, two, attn_out_two)
-    sums.total(15)
     input_grad_two = input_grad_of(14, two, grad_middle_two)
     squares = [jnp.sum(x) + jnp.sum(y) for x, y in zip(squares_one, squares_two)]
     squares = spread_small(jnp.broadcast_to(jnp.stack(squares + [0.0])[None, :], (8, 4)))[0, :3]

time: 735 us -> 726 us (0.988)
  starting transfers between devices: 160 us -> 132 us
  waiting for transfers between devices: 171 us -> 195 us
  other arithmetic: 54.2 us -> 33.4 us
  Pallas kernels: 113 us -> 122 us
  local copies, waits for them, and re-layouts: 78.3 us -> 85.8 us
    unnamed x353 -> x350, local copies, waits for them, and re-layouts: 36 us -> 62 us
    ppermute x16 -> x14, starting transfers between devices: 83.6 us -> 63.9 us  [send_in(): return lax.ppermute(part, 'tensor', [(0, 1), (3, 2)])]
    ppermute x16 -> x14, waiting for transfers between devices: 54.3 us -> 73.8 us  [send_out(): return lax.ppermute(total, 'tensor', [(1, 0), (2, 3)])]
    ppermute x16 -> x14, waiting for transfers between devices: 74.5 us -> 64.1 us  [send_in(): return lax.ppermute(part, 'tensor', [(0, 1), (3, 2)])]
    ppermute x2, waiting for transfers between devices: 0.22 us -> 9.03 us  [attend_back_group(): returned = lax.ppermute(carry[1], 'ctx', [(0, 1), (1, 0)])]
    reduce_scatter x3, waiting for transfers between devices: 0.02 us -> 8.67 us  [scatter_rows(): lax.psum_scatter(grads, ROW_AXES, scatter_dimension=0, tiled=True)]
    convert_element_type x1 -> x0, other arithmetic: 8.61 us -> none  [body(): tokens = hidden_flat.astype(F32)]
    slice x16 -> x4, local copies, waits for them, and re-layouts: 11.7 us -> 3.75 us  [push(): sums.push(k + n, part[n * size:(n + 1) * size].astype(BF16))]
  transfers between devices with their start and end apart: 63 -> 57, of which waited for: 20 -> 19; matrix products, arithmetic and copies ran while one was open for 27% -> 23% of each run, Pallas kernels for 15% -> 17%
where the time goes in v3:
time: 726 us; the launch traced here: 714 us
  waiting for transfers between devices  195 us (27%)
  starting transfers between devices  132 us (18%)
  Pallas kernels  122 us (17%)
  matrix products  118 us (16%)
  local copies, waits for them, and re-layouts  85.8 us (12%)
  other arithmetic  33.4 us (5%)
  between operations  27.8 us (4%)
    dot_general x22, matrix products, dot(): lax.dot_general(left, right, (((left_dim,), (right_dim,)), ((), ())), pre...  118 us
    pallas_call x37, Pallas kernels, rowwise(): pl.pallas_call(functools.partial(rowwise_kernel, fn, bounds, len(lists),...  86 us
    ppermute x14, waiting for transfers between devices, send_out(): return lax.ppermute(total, 'tensor', [(1, 0), (2, 3)])  73.8 us
    ppermute x14, waiting for transfers between devices, send_in(): return lax.ppermute(part, 'tensor', [(0, 1), (3, 2)])  64.1 us
    ppermute x14, starting transfers between devices, send_in(): return lax.ppermute(part, 'tensor', [(0, 1), (3, 2)])  63.9 us
    unnamed x350, local copies, waits for them, and re-layouts  62 us
    all_gather x4, waiting for transfers between devices, gather_rows(): return lax.all_gather(shard, ROW_AXES, axis=0, tiled=True)  31.7 us
    ppermute x2, starting transfers between devices, attend_back_group(): returned = lax.ppermute(carry[1], 'ctx', [(0, 1), (1, 0)])  23.5 us
  transfers between devices with their start and end apart: 57, of which 19 were waited for; matrix products, arithmetic and copies ran while one was open for 23% of the time, Pallas kernels for 17%

profile of v3, /device:TPU:0, one launch (start us, length us, event | category | flops | bytes accessed | tf_op | source)
XLA Modules:
  0.0 714.0 jit_solution(15625666216986050962)
XLA Ops:
  20.0 27.2 %all-gather.5.cloned.1.call-done = bf16[2048,768]{0,1:T(8,128)(2,1)} async-done(((bf16[256,768]{0,1:T(8,128)(2,1)}), bf16[2048,768]{0,1:T(8,128)(2,1)}) %all-gather.5.cloned.1.call-update) | async-done | bytes 3145744 | tf_op jit(solution)/shard_map/all_gather | solution.py:472
  111.2 19.7 %collective-permute-done.3.refs_1_ = bf16[256,2048]{1,0:T(8,128)(2,1)} collective-permute-done((bf16[256,2048]{1,0:T(8,128)(2,1)}, bf16[256,2048]{1,0:T(8,128)(2,1)}, u32[]{:S(2)}, u32[]{:S(2)}) %collective-permute-start.3) | collective-permute-done | bytes 1048608 | tf_op jit(solution)/shard_map/ppermute | solution.py:409
  133.3 7.3 %collective-permute-start.9 = (bf16[256,2048]{1,0:T(8,128)(2,1)S(1)}, bf16[256,2048]{1,0:T(8,128)(2,1)S(1)}, u32[]{:S(2)}, u32[]{:S(2)}) collective-permute-start(bf16[256,2048]{1,0:T(8,128)(2,1)S(1)} %convolution_convert_fusion.1.refs_2_.refs_0_), channel_id=1, source_target_pairs={{0,1},{3,2},{4,5},{7,6},{8,9},{11,10},{12,13},{15,14},{16,17},{19,... | collective-permute-start | bytes 3145736 | tf_op jit(solution)/shard_map/ppermute | solution.py:409
  142.2 11.0 %collective-permute-done.5.refs_1_ = bf16[256,2048]{1,0:T(8,128)(2,1)S(1)} collective-permute-done((bf16[256,2048]{1,0:T(8,128)(2,1)S(1)}, bf16[256,2048]{1,0:T(8,128)(2,1)S(1)}, u32[]{:S(2)}, u32[]{:S(2)}) %collective-permute-start.5) | collective-permute-done | bytes 1048608 | tf_op jit(solution)/shard_map/ppermute | solution.py:409
  159.1 15.9 %collective-permute-done.9.refs_1_ = bf16[256,2048]{1,0:T(8,128)(2,1)S(1)} collective-permute-done((bf16[256,2048]{1,0:T(8,128)(2,1)S(1)}, bf16[256,2048]{1,0:T(8,128)(2,1)S(1)}, u32[]{:S(2)}, u32[]{:S(2)}) %collective-permute-start.9) | collective-permute-done | bytes 1048608 | tf_op jit(solution)/shard_map/ppermute | solution.py:409
  180.3 10.5 %collective-permute-done.7.refs_3_ = bf16[256,2048]{1,0:T(8,128)(2,1)S(1)} collective-permute-done((bf16[256,2048]{1,0:T(8,128)(2,1)S(1)}, bf16[256,2048]{1,0:T(8,128)(2,1)S(1)}, u32[]{:S(2)}, u32[]{:S(2)}) %collective-permute-start.7) | collective-permute-done | bytes 1048608 | tf_op jit(solution)/shard_map/ppermute | solution.py:417
  194.2 10.9 %fusion.121.refs_2_ = f32[512,2816]{1,0:T(8,128)S(1)} fusion(bf16[512,2048]{1,0:T(8,128)(2,1)} %copy-done.128, bf16[2048,2816]{1,0:T(8,128)(2,1)} %all-gather.9.cloned.1.call-done), kind=kOutput, calls=%fused_computation.208 | convolution fusion | flops 5905580032 | bytes 19398656 | tf_op jit(solution)/shard_map/dot_general | solution.py:26
  210.9 10.3 %multiply_convert_fusion.6 = (bf16[512,1408]{1,0:T(8,128)(2,1)S(1)}, bf16[512,1408]{1,0:T(8,128)(2,1)S(1)}, bf16[512,1408]{1,0:T(8,128)(2,1)}) fusion(f32[512,2816]{1,0:T(8,128)} %copy-done.78, bf16[2048,1408]{1,0:T(8,128)(2,1)} %all-gather.11.cloned.1.call-done, bf16[1024,2048]{1,0:T(8,128)(2,1)} %multiply_convert_fusion), kind=kOutput, calls=%fused_computation.54 | convolution fusion | flops 2963603456 | bytes 17956864 | tf_op jit(solution)/shard_map/dot_general | solution.py:26
  221.1 10.1 %convolution_convert_fusion = bf16[512,2048]{1,0:T(8,128)(2,1)S(1)} fusion(bf16[2048,2816]{1,0:T(8,128)(2,1)} %all-gather.9.cloned.1.call-done, bf16[512,1408]{1,0:T(8,128)(2,1)S(1)} %get-tuple-element.129, bf16[512,1408]{1,0:T(8,128)(2,1)S(1)} %get-tuple-element.128), kind=kOutput, calls=%fused_computation.38 | convolution fusion | flops 5912395776 | bytes 16515072 | tf_op jit(solution)/shard_map/dot_general | solution.py:26
  244.0 11.0 %fusion.122.refs_2_ = f32[512,2816]{1,0:T(8,128)S(1)} fusion(bf16[512,2048]{1,0:T(8,128)(2,1)S(1)} %get-tuple-element.54, bf16[2048,2816]{1,0:T(8,128)(2,1)} %all-gather.9.cloned.1.call-done), kind=kOutput, calls=%fused_computation.209 | convolution fusion | flops 5905580032 | bytes 19398656 | tf_op jit(solution)/shard_map/dot_general | solution.py:26
  268.0 10.0 %add_convert_fusion.8 = bf16[512,2048]{1,0:T(8,128)(2,1)S(1)} fusion(bf16[2048,2816]{1,0:T(8,128)(2,1)} %all-gather.9.cloned.1.call-done, bf16[512,1408]{1,0:T(8,128)(2,1)} %get-tuple-element.127, bf16[512,1408]{1,0:T(8,128)(2,1)S(1)} %get-tuple-element.126, f32[]{:T(128)} %bitcast.20), kind=kOutput, calls=%fused_computation.37 | convolution fusion | flops 5913444352 | bytes 16515076 | tf_op jit(solution)/shard_map/dot_general | solution.py:26
  299.8 8.5 %collective-permute-done.18.refs_1_ = bf16[256,2048]{1,0:T(8,128)(2,1)S(1)} collective-permute-done((bf16[256,2048]{1,0:T(8,128)(2,1)S(1)}, bf16[256,2048]{1,0:T(8,128)(2,1)S(1)}, u32[]{:S(2)}, u32[]{:S(2)}) %collective-permute-start.18) | collective-permute-done | bytes 1048608 | tf_op jit(solution)/shard_map/ppermute | solution.py:409
  315.4 18.3 %add_convert_fusion.refs_2_.ref = bf16[2048,2816]{1,0:T(8,128)(2,1)} fusion(f32[]{:T(128)} %bitcast.23, bf16[512,1408]{1,0:T(8,128)(2,1)} %get-tuple-element.127, bf16[512,1408]{1,0:T(8,128)(2,1)} %copy-done.167, bf16[512,1408]{1,0:T(8,128)(2,1)} %copy-done.166, bf16[512,1408]{1,0:T(8,128)(2,1)} %copy-done.165, bf16[512,2048]{1,0:T(8,128)(2,1)} %copy-done.129, ...), kind=kOutput, calls=%fused_computation | convolution fusion | flops 11854151680 | bytes 21495812 | tf_op jit(solution)/shard_map/dot_general | solution.py:26
  343.5 9.8 %collective-permute-start.16 = (bf16[512,2048]{1,0:T(8,128)(2,1)}, bf16[512,2048]{1,0:T(8,128)(2,1)}, u32[]{:S(2)}, u32[]{:S(2)}) collective-permute-start(bf16[512,2048]{1,0:T(8,128)(2,1)} %copy-done.85), channel_id=1, source_target_pairs={{0,1},{3,2},{4,5},{7,6},{8,9},{11,10},{12,13},{15,14},{16,17},{19,... | collective-permute-start | bytes 6291464 | tf_op jit(solution)/shard_map/ppermute | solution.py:409
  409.2 13.4 %collective-permute-start.28 = (f32[512,128]{1,0:T(8,128)}, f32[512,128]{1,0:T(8,128)}, u32[]{:S(2)}, u32[]{:S(2)}) collective-permute-start(f32[512,128]{1,0:T(8,128)} %get-tuple-element.72), channel_id=1, source_target_pairs={{0,4},{4,0},{1,5},{5,1},{2,6},{6,2},{3,7},{7,3},{8,12},{12,8},{9,1... | collective-permute-start | bytes 786440 | tf_op jit(solution)/shard_map/ppermute | solution.py:681
  423.4 9.0 %collective-permute-done.28.returned_ref = f32[512,128]{1,0:T(8,128)} collective-permute-done((f32[512,128]{1,0:T(8,128)}, f32[512,128]{1,0:T(8,128)}, u32[]{:S(2)}, u32[]{:S(2)}) %collective-permute-start.28) | collective-permute-done | bytes 262176 | tf_op jit(solution)/shard_map/ppermute | solution.py:681
  458.4 10.1 %collective-permute-start.30 = (f32[512,128]{1,0:T(8,128)S(1)}, f32[512,128]{1,0:T(8,128)S(1)}, u32[]{:S(2)}, u32[]{:S(2)}) collective-permute-start(f32[512,128]{1,0:T(8,128)S(1)} %get-tuple-element.75), channel_id=1, source_target_pairs={{0,4},{4,0},{1,5},{5,1},{2,6},{6,2},{3,7},{7,3},{8,12},{12,8},{9,1... | collective-permute-start | bytes 786440 | tf_op jit(solution)/shard_map/ppermute | solution.py:681
  471.5 8.6 %collective-permute-start.34 = (bf16[256,2048]{1,0:T(8,128)(2,1)}, bf16[256,2048]{1,0:T(8,128)(2,1)}, u32[]{:S(2)}, u32[]{:S(2)}) collective-permute-start(bf16[256,2048]{1,0:T(8,128)(2,1)} %get-tuple-element.136.refs_0_), channel_id=1, source_target_pairs={{0,1},{3,2},{4,5},{7,6},{8,9},{11,10},{12,13},{15,14},{16,17},{19,... | collective-permute-start | bytes 3145736 | tf_op jit(solution)/shard_map/ppermute | solution.py:409
  509.9 12.1 %collective-permute-done.29.refs_2_.refs_1_ = bf16[512,2048]{1,0:T(8,128)(2,1)S(1)} collective-permute-done((bf16[512,2048]{1,0:T(8,128)(2,1)S(1)}, bf16[512,2048]{1,0:T(8,128)(2,1)S(1)}, u32[]{:S(2)}, u32[]{:S(2)}) %collective-permute-start.29) | collective-permute-done | bytes 2097184 | tf_op jit(solution)/shard_map/ppermute | solution.py:417
  567.8 8.1 %collective-permute-done.35.refs_2_.refs_1_ = bf16[512,2048]{1,0:T(8,128)(2,1)} collective-permute-done((bf16[512,2048]{1,0:T(8,128)(2,1)S(1)}, bf16[512,2048]{1,0:T(8,128)(2,1)}, u32[]{:S(2)}, u32[]{:S(2)}) %collective-permute-start.35) | collective-permute-done | bytes 2097184 | tf_op jit(solution)/shard_map/ppermute | solution.py:417
  579.6 8.7 %reduce-scatter.6.cloned.1.call-done = bf16[256,1408]{1,0:T(8,128)(2,1)} async-done(((bf16[2048,1408]{1,0:T(8,128)(2,1)}), bf16[256,1408]{1,0:T(8,128)(2,1)}) %reduce-scatter.6.cloned.1.call-update) | async-done | bytes 720912 | tf_op jit(solution)/shard_map/reduce_scatter | solution.py:493
  637.1 8.9 %collective-permute-done.42.refs_3_ = bf16[256,2048]{1,0:T(8,128)(2,1)} collective-permute-done((bf16[256,2048]{1,0:T(8,128)(2,1)}, bf16[256,2048]{1,0:T(8,128)(2,1)}, u32[]{:S(2)}, u32[]{:S(2)}) %collective-permute-start.42) | collective-permute-done | bytes 1048608 | tf_op jit(solution)/shard_map/ppermute | solution.py:417
  655.3 13.2 %collective-permute-done.43.refs_2_ = bf16[256,2048]{1,0:T(8,128)(2,1)} collective-permute-done((bf16[256,2048]{1,0:T(8,128)(2,1)S(1)}, bf16[256,2048]{1,0:T(8,128)(2,1)}, u32[]{:S(2)}, u32[]{:S(2)}) %collective-permute-start.43) | collective-permute-done | bytes 1048608 | tf_op jit(solution)/shard_map/ppermute | solution.py:417
  668.5 19.0 %collective-permute-done.44.refs_3_ = bf16[256,2048]{1,0:T(8,128)(2,1)} collective-permute-done((bf16[256,2048]{1,0:T(8,128)(2,1)}, bf16[256,2048]{1,0:T(8,128)(2,1)}, u32[]{:S(2)}, u32[]{:S(2)}) %collective-permute-start.44) | collective-permute-done | bytes 1048608 | tf_op jit(solution)/shard_map/ppermute | solution.py:417
  (630 shorter events, 394.5 us)
Async XLA Ops:
  7.2 40.0 %all-gather.5.cloned.1.call-start = ((), (), s32[]{:S(2)}) async-start(), calls=%async_computation.3 | async-start | bytes 3538944 | tf_op jit(solution)/shard_map/all_gather | solution.py:472
  11.5 67.3 %all-gather.7.cloned.1.call-start = ((), (), s32[]{:S(2)}) async-start(), calls=%async_computation.4 | async-start | bytes 2359296 | tf_op jit(solution)/shard_map/all_gather | solution.py:472
  12.3 181.9 %all-gather.9.cloned.1.call-start = ((), (), s32[]{:S(2)}) async-start(), calls=%async_computation.5 | async-start | bytes 12976128 | tf_op jit(solution)/shard_map/all_gather | solution.py:472
  13.6 197.3 %all-gather.11.cloned.1.call-start = ((), (), s32[]{:S(2)}) async-start(), calls=%async_computation.6 | async-start | bytes 6488064 | tf_op jit(solution)/shard_map/all_gather | solution.py:472
  14.2 514.9 %reduce-scatter.4.cloned.1.call-start = ((), (), s32[]{:S(2)}) async-start(), calls=%async_computation.7 | async-start | bytes 12976128 | tf_op jit(solution)/shard_map/reduce_scatter | solution.py:493
  87.8 43.1 %collective-permute-start.3 = (bf16[256,2048]{1,0:T(8,128)(2,1)}, bf16[256,2048]{1,0:T(8,128)(2,1)}, u32[]{:S(2)}, u32[]{:S(2)}) collective-permute-start(bf16[256,2048]{1,0:T(8,128)(2,1)} %convolution_convert_fusion.2.refs_0_), channel_id=1, source_target_pairs={{0,1},{3,2},{4,5},{7,6},{8,9},{11,10},{12,13},{15,14},{16,17},{19,... | collective-permute-start | bytes 3145736 | tf_op jit(solution)/shard_map/ppermute | solution.py:409
  102.9 50.3 %collective-permute-start.5 = (bf16[256,2048]{1,0:T(8,128)(2,1)S(1)}, bf16[256,2048]{1,0:T(8,128)(2,1)S(1)}, u32[]{:S(2)}, u32[]{:S(2)}) collective-permute-start(bf16[256,2048]{1,0:T(8,128)(2,1)S(1)} %convolution_convert_fusion.3.refs_2_.refs_0_), channel_id=1, source_target_pairs={{0,1},{3,2},{4,5},{7,6},{8,9},{11,10},{12,13},{15,14},{16,17},{19,... | collective-permute-start | bytes 3145736 | tf_op jit(solution)/shard_map/ppermute | solution.py:409
  133.3 41.8 %collective-permute-start.9 = (bf16[256,2048]{1,0:T(8,128)(2,1)S(1)}, bf16[256,2048]{1,0:T(8,128)(2,1)S(1)}, u32[]{:S(2)}, u32[]{:S(2)}) collective-permute-start(bf16[256,2048]{1,0:T(8,128)(2,1)S(1)} %convolution_convert_fusion.1.refs_2_.refs_0_), channel_id=1, source_target_pairs={{0,1},{3,2},{4,5},{7,6},{8,9},{11,10},{12,13},{15,14},{16,17},{19,... | collective-permute-start | bytes 3145736 | tf_op jit(solution)/shard_map/ppermute | solution.py:409
  154.7 36.2 %collective-permute-start.7 = (bf16[256,2048]{1,0:T(8,128)(2,1)S(1)}, bf16[256,2048]{1,0:T(8,128)(2,1)S(1)}, u32[]{:S(2)}, u32[]{:S(2)}) collective-permute-start(bf16[256,2048]{1,0:T(8,128)(2,1)S(1)} %total.15.refs_3_.refs_1_), channel_id=1, source_target_pairs={{1,0},{2,3},{5,4},{6,7},{9,8},{10,11},{13,12},{14,15},{17,16},{18,... | collective-permute-start | bytes 3145736 | tf_op jit(solution)/shard_map/ppermute | solution.py:417
  179.0 58.7 %collective-permute-start.12 = (bf16[256,2048]{1,0:T(8,128)(2,1)}, bf16[256,2048]{1,0:T(8,128)(2,1)}, u32[]{:S(2)}, u32[]{:S(2)}) collective-permute-start(bf16[256,2048]{1,0:T(8,128)(2,1)} %total.16.refs_6_.refs_0_), channel_id=1, source_target_pairs={{1,0},{2,3},{5,4},{6,7},{9,8},{10,11},{13,12},{14,15},{17,16},{18,... | collective-permute-start | bytes 3145736 | tf_op jit(solution)/shard_map/ppermute | solution.py:417
  236.4 50.7 %collective-permute-start.15 = (bf16[256,2048]{1,0:T(8,128)(2,1)S(1)}, bf16[256,2048]{1,0:T(8,128)(2,1)S(1)}, u32[]{:S(2)}, u32[]{:S(2)}) collective-permute-start(bf16[256,2048]{1,0:T(8,128)(2,1)S(1)} %get-tuple-element.141.refs_6_.refs_0_), channel_id=1, source_target_pairs={{0,1},{3,2},{4,5},{7,6},{8,9},{11,10},{12,13},{15,14},{16,17},{19,... | collective-permute-start | bytes 3145736 | tf_op jit(solution)/shard_map/ppermute | solution.py:409
  284.8 48.9 %collective-permute-start.22 = (bf16[256,2048]{1,0:T(8,128)(2,1)}, bf16[256,2048]{1,0:T(8,128)(2,1)}, u32[]{:S(2)}, u32[]{:S(2)}) collective-permute-start(bf16[256,2048]{1,0:T(8,128)(2,1)} %get-tuple-element.139.refs_2_.refs_0_), channel_id=1, source_target_pairs={{0,1},{3,2},{4,5},{7,6},{8,9},{11,10},{12,13},{15,14},{16,17},{19,... | collective-permute-start | bytes 3145736 | tf_op jit(solution)/shard_map/ppermute | solution.py:409
  343.4 244.8 %reduce-scatter.6.cloned.1.call-start = ((), (), s32[]{:S(2)}) async-start(), calls=%async_computation.8 | async-start | bytes 6488064 | tf_op jit(solution)/shard_map/reduce_scatter | solution.py:493
  343.5 59.5 %collective-permute-start.16 = (bf16[512,2048]{1,0:T(8,128)(2,1)}, bf16[512,2048]{1,0:T(8,128)(2,1)}, u32[]{:S(2)}, u32[]{:S(2)}) collective-permute-start(bf16[512,2048]{1,0:T(8,128)(2,1)} %copy-done.85), channel_id=1, source_target_pairs={{0,1},{3,2},{4,5},{7,6},{8,9},{11,10},{12,13},{15,14},{16,17},{19,... | collective-permute-start | bytes 6291464 | tf_op jit(solution)/shard_map/ppermute | solution.py:409
  358.1 124.3 %collective-permute-start.26 = (bf16[512,2048]{1,0:T(8,128)(2,1)}, bf16[512,2048]{1,0:T(8,128)(2,1)}, u32[]{:S(2)}, u32[]{:S(2)}) collective-permute-start(bf16[512,2048]{1,0:T(8,128)(2,1)} %copy-done.72), channel_id=1, source_target_pairs={{0,1},{3,2},{4,5},{7,6},{8,9},{11,10},{12,13},{15,14},{16,17},{19,... | collective-permute-start | bytes 6291464 | tf_op jit(solution)/shard_map/ppermute | solution.py:409
  389.9 44.4 %collective-permute-start.27 = (bf16[256,2048]{1,0:T(8,128)(2,1)}, bf16[256,2048]{1,0:T(8,128)(2,1)}, u32[]{:S(2)}, u32[]{:S(2)}) collective-permute-start(bf16[256,2048]{1,0:T(8,128)(2,1)} %total.21.refs_3_.refs_1_), channel_id=1, source_target_pairs={{1,0},{2,3},{5,4},{6,7},{9,8},{10,11},{13,12},{14,15},{17,16},{18,... | collective-permute-start | bytes 3145736 | tf_op jit(solution)/shard_map/ppermute | solution.py:417
  407.2 82.4 %collective-permute-start.25 = (bf16[512,2048]{1,0:T(8,128)(2,1)}, bf16[512,2048]{1,0:T(8,128)(2,1)}, u32[]{:S(2)}, u32[]{:S(2)}) collective-permute-start(bf16[512,2048]{1,0:T(8,128)(2,1)} %pair.22.refs_9_.refs_0_), channel_id=1, source_target_pairs={{1,2},{2,1},{5,6},{6,5},{9,10},{10,9},{13,14},{14,13},{17,18},{18,... | collective-permute-start | bytes 6291464 | tf_op jit(solution)/shard_map/ppermute | solution.py:413
  471.5 36.3 %collective-permute-start.34 = (bf16[256,2048]{1,0:T(8,128)(2,1)}, bf16[256,2048]{1,0:T(8,128)(2,1)}, u32[]{:S(2)}, u32[]{:S(2)}) collective-permute-start(bf16[256,2048]{1,0:T(8,128)(2,1)} %get-tuple-element.136.refs_0_), channel_id=1, source_target_pairs={{0,1},{3,2},{4,5},{7,6},{8,9},{11,10},{12,13},{15,14},{16,17},{19,... | collective-permute-start | bytes 3145736 | tf_op jit(solution)/shard_map/ppermute | solution.py:409
  485.0 39.1 %collective-permute-start.32 = (bf16[512,2048]{1,0:T(8,128)(2,1)S(1)}, bf16[512,2048]{1,0:T(8,128)(2,1)}, u32[]{:S(2)}, u32[]{:S(2)}) collective-permute-start(bf16[512,2048]{1,0:T(8,128)(2,1)S(1)} %pair.23.refs_2_.refs_0_), channel_id=1, source_target_pairs={{1,2},{2,1},{5,6},{6,5},{9,10},{10,9},{13,14},{14,13},{17,18},{18,... | collective-permute-start | bytes 6291464 | tf_op jit(solution)/shard_map/ppermute | solution.py:413
  532.2 161.4 %reduce-scatter.8.cloned.1.call-start = ((), (), s32[]{:S(2)}) async-start(), calls=%async_computation.9 | async-start | bytes 5898240 | tf_op jit(solution)/shard_map/reduce_scatter | solution.py:493
  592.4 44.7 %collective-permute-start.41 = (bf16[256,2048]{1,0:T(8,128)(2,1)}, bf16[256,2048]{1,0:T(8,128)(2,1)}, u32[]{:S(2)}, u32[]{:S(2)}) collective-permute-start(bf16[256,2048]{1,0:T(8,128)(2,1)} %copy-done.55), channel_id=1, source_target_pairs={{1,0},{2,3},{5,4},{6,7},{9,8},{10,11},{13,12},{14,15},{17,16},{18,... | collective-permute-start | bytes 3145736 | tf_op jit(solution)/shard_map/ppermute | solution.py:417
  593.7 52.4 %collective-permute-start.42 = (bf16[256,2048]{1,0:T(8,128)(2,1)}, bf16[256,2048]{1,0:T(8,128)(2,1)}, u32[]{:S(2)}, u32[]{:S(2)}) collective-permute-start(bf16[256,2048]{1,0:T(8,128)(2,1)} %copy-done.41), channel_id=1, source_target_pairs={{1,0},{2,3},{5,4},{6,7},{9,8},{10,11},{13,12},{14,15},{17,16},{18,... | collective-permute-start | bytes 3145736 | tf_op jit(solution)/shard_map/ppermute | solution.py:417
  596.3 72.2 %collective-permute-start.43 = (bf16[256,2048]{1,0:T(8,128)(2,1)S(1)}, bf16[256,2048]{1,0:T(8,128)(2,1)}, u32[]{:S(2)}, u32[]{:S(2)}) collective-permute-start(bf16[256,2048]{1,0:T(8,128)(2,1)S(1)} %copy-done.23), channel_id=1, source_target_pairs={{1,0},{2,3},{5,4},{6,7},{9,8},{10,11},{13,12},{14,15},{17,16},{18,... | collective-permute-start | bytes 3145736 | tf_op jit(solution)/shard_map/ppermute | solution.py:417
  601.5 86.0 %collective-permute-start.44 = (bf16[256,2048]{1,0:T(8,128)(2,1)}, bf16[256,2048]{1,0:T(8,128)(2,1)}, u32[]{:S(2)}, u32[]{:S(2)}) collective-permute-start(bf16[256,2048]{1,0:T(8,128)(2,1)} %total.27.refs_5_.refs_1_), channel_id=1, source_target_pairs={{1,0},{2,3},{5,4},{6,7},{9,8},{10,11},{13,12},{14,15},{17,16},{18,... | collective-permute-start | bytes 3145736 | tf_op jit(solution)/shard_map/ppermute | solution.py:417
  (204 other events, 2160.0 us)
Sparse Core Ops, SparseCore 0:
  11.6 35.5 all-gather.4
  49.1 29.6 all-gather.6
  81.3 67.7 all-gather.8
  150.7 43.3 all-gather.10
  343.5 101.3 reduce-scatter.3
  532.4 55.8 reduce-scatter.5
  592.0 56.5 reduce-scatter.7

commit v4 on v3

--- a/solution.py
+++ b/solution.py
@@ -274,7 +274,7 @@
     return next(tile for tile in (128, 160, 96, 64, 32, 16) if size % tile == 0)
 
 
-def rowwise(fn, choice, lists, flats, consts, outs, sums=0, after=(), name="rowwise"):
+def rowwise(fn, choice, lists, flats, consts, outs, sums=0, after=(), name="rowwise", into=None):
     tile = tile_of(lists[0][0].shape[0])
     sizes = [piece.shape[0] // tile for piece in lists[0]]
     width = lists[0][0].shape[1]
@@ -303,19 +303,28 @@
         in_specs.append(pl.BlockSpec(memory_space=pl.ANY))
         operands.append(array)
     rows = total * tile
+    aliases, out_first, out_rows = {}, 0, rows
+    if into is not None:
+        held, out_first, out_rows = into
+        if held is not None:
+            aliases = {1 + len(operands): 0}
+            in_specs.append(pl.BlockSpec(memory_space=pl.ANY))
+            operands.append(held)
+    shift = out_first // tile
     return pl.pallas_call(
         functools.partial(rowwise_kernel, fn, bounds, len(lists), len(flats), len(consts), (len(outs), sums)),
-        out_shape=[jax.ShapeDtypeStruct((rows, width), dtype) for dtype in outs]
+        out_shape=[jax.ShapeDtypeStruct((rows if n else out_rows, width), dtype) for n, dtype in enumerate(outs)]
         + [jax.ShapeDtypeStruct((1, width), F32)] * sums,
         grid_spec=pltpu.PrefetchScalarGridSpec(
             num_scalar_prefetch=1,
             grid=(total,),
             in_specs=in_specs,
-            out_specs=[pl.BlockSpec((tile, width), lambda i, c: (i, 0))] * len(outs)
+            out_specs=[pl.BlockSpec((tile, width), lambda i, c, n=n: (i if n else i + shift, 0)) for n in range(len(outs))]
             + [pl.BlockSpec((1, width), lambda i, c: (0, 0))] * sums,
         ),
-        compiler_params=pltpu.CompilerParams(vmem_limit_bytes=32 << 20),
+        compiler_params=pltpu.CompilerParams(vmem_limit_bytes=(60 if len(flats) > 1 else 32) << 20),
         cost_estimate=SMALL_COST,
+        input_output_aliases=aliases,
         name=name,
     )(choice, *operands)
 
@@ -430,7 +439,8 @@
 
     def ordered(self, fn, *args, **more):
         after = tuple(more.pop("after", ()))
-        if self.last is not None:
+        held = more.get("into", (None,))[0]
+        if self.last is not None and self.last is not held:
             after += (self.last,)
         got = rowwise(fn, self.choice, *args, after=after, **more)
         self.last = got[0]
@@ -718,7 +728,7 @@
         axis=1,
     )
 
-    def result_of(first, at, attn_out, after=()):
+    def result_of(first, at, attn_out, held, after=()):
         return sums.ordered(
             result_fn,
             sums.of([first]),
@@ -727,10 +737,11 @@
             [BF16],
             sums=3,
             after=after,
+            into=(held, at.start, rows),
             name="result",
         )
 
-    def input_grad_of(first, at, grad_middle, after=()):
+    def input_grad_of(first, at, grad_middle, held, after=()):
         return sums.ordered(
             input_grad_fn,
             sums.of([first, first + 1]),
@@ -738,6 +749,7 @@
             [attn_gain],
             [BF16],
             after=after,
+            into=(held, at.start, rows),
             name="input_grad",
         )[0]
 
@@ -745,23 +757,24 @@
     sums.total(13)
     sums.pair(15, (sums.thirds[10],))
     sums.total(14)
-    last = scatter_rows(once(last, (sums.totals[14], grad_down)))
-    sums.total(15)
-    output_one, *squares_one = result_of(8, one, attn_out_one)
-    output_two, *squares_two = result_of(10, two, attn_out_two)
-    input_grad_one = input_grad_of(12, one, grad_middle_one)
-    input_grad_two = input_grad_of(14, two, grad_middle_two)
+    sums.total(15, (sums.thirds[12],))
+    last = scatter_rows(once(last, (sums.totals[15], grad_down)))
+    output, *squares_one = result_of(8, one, attn_out_one, None)
+    output, *squares_two = result_of(10, two, attn_out_two, output)
+    grad_gateup_w = grad_gateup_w.reshape(w_gateup.shape)
+    input_grad = input_grad_of(12, one, grad_middle_one, None)
+    input_grad = input_grad_of(14, two, grad_middle_two, input_grad, (grad_gateup_w, grad_down))
     squares = [jnp.sum(x) + jnp.sum(y) for x, y in zip(squares_one, squares_two)]
     squares = spread_small(jnp.broadcast_to(jnp.stack(squares + [0.0])[None, :], (8, 4)))[0, :3]
     root_means = jnp.sqrt(squares / (jnp.sum(lengths).astype(F32) * width))
     at = q_width + 2 * HD
     return (
-        join([output_one, output_two]).reshape(hidden_in.shape),
-        join([input_grad_one, input_grad_two]).reshape(hidden_in.shape),
+        output.reshape(hidden_in.shape),
+        input_grad.reshape(hidden_in.shape),
         last[:, :q_width],
         last[:, q_width:at].reshape(w_keyval.shape),
         last[:, at + 128 :],
-        grad_gateup_w.reshape(w_gateup.shape),
+        grad_gateup_w,
         grad_down,
         small_sum(last[:, at]),
         last[:, at + 1],

time: 726 us -> 681 us (0.938)
  local copies, waits for them, and re-layouts: 85.8 us -> 54.5 us
  starting transfers between devices: 132 us -> 114 us
  Pallas kernels: 122 us -> 133 us
    unnamed x350 -> x298, local copies, waits for them, and re-layouts: 62 us -> 31.3 us
    ppermute x14, waiting for transfers between devices: 73.8 us -> 55.5 us  [send_out(): return lax.ppermute(total, 'tensor', [(1, 0), (2, 3)])]
    ppermute x2, starting transfers between devices: 23.5 us -> 9.97 us  [attend_back_group(): returned = lax.ppermute(carry[1], 'ctx', [(0, 1), (1, 0)])]
    pallas_call x37, Pallas kernels: 86 us -> 98.4 us  [rowwise(): pl.pallas_call(functools.partial(rowwise_kernel, fn, bounds, len(lists),...]
    ppermute x14, waiting for transfers between devices: 64.1 us -> 73.8 us  [send_in(): return lax.ppermute(part, 'tensor', [(0, 1), (3, 2)])]
    concatenate x5 -> x3, other arithmetic: 8.54 us -> 0.78 us  [body(): join = lambda parts: jnp.concatenate(parts, axis=0)]
  transfers between devices with their start and end apart: 57 -> 57, of which waited for: 19 -> 19; matrix products, arithmetic and copies ran while one was open for 23% -> 25% of each run, Pallas kernels for 17% -> 20%
where the time goes in v4:
time: 681 us; the launch traced here: 670 us
  waiting for transfers between devices  192 us (28%)
  Pallas kernels  133 us (20%)
  matrix products  121 us (18%)
  starting transfers between devices  114 us (17%)
  local copies, waits for them, and re-layouts  54.5 us (8%)
  other arithmetic  28.1 us (4%)
  between operations  27.6 us (4%)
    dot_general x22, matrix products, dot(): lax.dot_general(left, right, (((left_dim,), (right_dim,)), ((), ())), pre...  121 us
    pallas_call x37, Pallas kernels, rowwise(): pl.pallas_call(functools.partial(rowwise_kernel, fn, bounds, len(lists),...  98.4 us
    ppermute x14, waiting for transfers between devices, send_in(): return lax.ppermute(part, 'tensor', [(0, 1), (3, 2)])  73.8 us
    ppermute x14, starting transfers between devices, send_in(): return lax.ppermute(part, 'tensor', [(0, 1), (3, 2)])  61.1 us
    ppermute x14, waiting for transfers between devices, send_out(): return lax.ppermute(total, 'tensor', [(1, 0), (2, 3)])  55.5 us
    unnamed x298, local copies, waits for them, and re-layouts  31.3 us
    all_gather x4, waiting for transfers between devices, gather_rows(): return lax.all_gather(shard, ROW_AXES, axis=0, tiled=True)  30 us
    ppermute x14, starting transfers between devices, send_out(): return lax.ppermute(total, 'tensor', [(1, 0), (2, 3)])  19.8 us
  transfers between devices with their start and end apart: 57, of which 19 were waited for; matrix products, arithmetic and copies ran while one was open for 25% of the time, Pallas kernels for 20%

profile of v4, /device:TPU:0, one launch (start us, length us, event | category | flops | bytes accessed | tf_op | source)
XLA Modules:
  0.0 670.3 jit_solution(8316070335022456626)
XLA Ops:
  21.6 25.6 %all-gather.5.cloned.1.call-done = bf16[2048,768]{0,1:T(8,128)(2,1)} async-done(((bf16[256,768]{0,1:T(8,128)(2,1)}), bf16[2048,768]{0,1:T(8,128)(2,1)}) %all-gather.5.cloned.1.call-update) | async-done | bytes 3145744 | tf_op jit(solution)/shard_map/all_gather | solution.py:482
  111.0 19.7 %collective-permute-done.4.refs_1_ = bf16[256,2048]{1,0:T(8,128)(2,1)} collective-permute-done((bf16[256,2048]{1,0:T(8,128)(2,1)}, bf16[256,2048]{1,0:T(8,128)(2,1)}, u32[]{:S(2)}, u32[]{:S(2)}) %collective-permute-start.4) | collective-permute-done | bytes 1048608 | tf_op jit(solution)/shard_map/ppermute | solution.py:418
  133.1 7.3 %collective-permute-start.6 = (bf16[256,2048]{1,0:T(8,128)(2,1)S(1)}, bf16[256,2048]{1,0:T(8,128)(2,1)S(1)}, u32[]{:S(2)}, u32[]{:S(2)}) collective-permute-start(bf16[256,2048]{1,0:T(8,128)(2,1)S(1)} %convolution_convert_fusion.1.refs_2_.refs_0_), channel_id=1, source_target_pairs={{0,1},{3,2},{4,5},{7,6},{8,9},{11,10},{12,13},{15,14},{16,17},{19,... | collective-permute-start | bytes 3145736 | tf_op jit(solution)/shard_map/ppermute | solution.py:418
  142.1 11.0 %collective-permute-done.1.refs_1_ = bf16[256,2048]{1,0:T(8,128)(2,1)S(1)} collective-permute-done((bf16[256,2048]{1,0:T(8,128)(2,1)S(1)}, bf16[256,2048]{1,0:T(8,128)(2,1)S(1)}, u32[]{:S(2)}, u32[]{:S(2)}) %collective-permute-start.1) | collective-permute-done | bytes 1048608 | tf_op jit(solution)/shard_map/ppermute | solution.py:418
  159.0 15.9 %collective-permute-done.6.refs_1_ = bf16[256,2048]{1,0:T(8,128)(2,1)S(1)} collective-permute-done((bf16[256,2048]{1,0:T(8,128)(2,1)S(1)}, bf16[256,2048]{1,0:T(8,128)(2,1)S(1)}, u32[]{:S(2)}, u32[]{:S(2)}) %collective-permute-start.6) | collective-permute-done | bytes 1048608 | tf_op jit(solution)/shard_map/ppermute | solution.py:418
  180.2 10.6 %collective-permute-done.10.refs_3_ = bf16[256,2048]{1,0:T(8,128)(2,1)S(1)} collective-permute-done((bf16[256,2048]{1,0:T(8,128)(2,1)S(1)}, bf16[256,2048]{1,0:T(8,128)(2,1)S(1)}, u32[]{:S(2)}, u32[]{:S(2)}) %collective-permute-start.10) | collective-permute-done | bytes 1048608 | tf_op jit(solution)/shard_map/ppermute | solution.py:426
  194.0 10.9 %fusion.121.refs_2_ = f32[512,2816]{1,0:T(8,128)S(1)} fusion(bf16[512,2048]{1,0:T(8,128)(2,1)} %copy-done.90, bf16[2048,2816]{1,0:T(8,128)(2,1)} %all-gather.9.cloned.1.call-done), kind=kOutput, calls=%fused_computation.206 | convolution fusion | flops 5905580032 | bytes 19398656 | tf_op jit(solution)/shard_map/dot_general | solution.py:26
  210.7 10.3 %multiply_convert_fusion.7 = (bf16[512,1408]{1,0:T(8,128)(2,1)S(1)}, bf16[512,1408]{1,0:T(8,128)(2,1)S(1)}, bf16[512,1408]{1,0:T(8,128)(2,1)}) fusion(f32[512,2816]{1,0:T(8,128)} %copy-done.48, bf16[2048,1408]{1,0:T(8,128)(2,1)} %all-gather.11.cloned.1.call-done, bf16[1024,2048]{1,0:T(8,128)(2,1)} %multiply_convert_fusion), kind=kOutput, calls=%fused_computation.53 | convolution fusion | flops 2963603456 | bytes 17956864 | tf_op jit(solution)/shard_map/dot_general | solution.py:26
  222.6 9.0 %convolution_convert_fusion = bf16[512,2048]{1,0:T(8,128)(2,1)S(1)} fusion(bf16[2048,2816]{1,0:T(8,128)(2,1)} %all-gather.9.cloned.1.call-done, bf16[512,1408]{1,0:T(8,128)(2,1)S(1)} %get-tuple-element.129, bf16[512,1408]{1,0:T(8,128)(2,1)S(1)} %get-tuple-element.128), kind=kOutput, calls=%fused_computation.36 | convolution fusion | flops 5912395776 | bytes 16515072 | tf_op jit(solution)/shard_map/dot_general | solution.py:26
  242.3 11.1 %fusion.122.refs_2_ = f32[512,2816]{1,0:T(8,128)S(1)} fusion(bf16[512,2048]{1,0:T(8,128)(2,1)S(1)} %get-tuple-element.54, bf16[2048,2816]{1,0:T(8,128)(2,1)} %all-gather.9.cloned.1.call-done), kind=kOutput, calls=%fused_computation.207 | convolution fusion | flops 5905580032 | bytes 19398656 | tf_op jit(solution)/shard_map/dot_general | solution.py:26
  268.4 10.0 %add_convert_fusion.8 = bf16[512,2048]{1,0:T(8,128)(2,1)S(1)} fusion(bf16[2048,2816]{1,0:T(8,128)(2,1)} %all-gather.9.cloned.1.call-done, bf16[512,1408]{1,0:T(8,128)(2,1)} %get-tuple-element.127, bf16[512,1408]{1,0:T(8,128)(2,1)S(1)} %get-tuple-element.126, f32[]{:T(128)} %bitcast.20), kind=kOutput, calls=%fused_computation.35 | convolution fusion | flops 5913444352 | bytes 16515076 | tf_op jit(solution)/shard_map/dot_general | solution.py:26
  298.3 9.4 %collective-permute-done.17.refs_1_ = bf16[256,2048]{1,0:T(8,128)(2,1)S(1)} collective-permute-done((bf16[256,2048]{1,0:T(8,128)(2,1)S(1)}, bf16[256,2048]{1,0:T(8,128)(2,1)S(1)}, u32[]{:S(2)}, u32[]{:S(2)}) %collective-permute-start.17) | collective-permute-done | bytes 1048608 | tf_op jit(solution)/shard_map/ppermute | solution.py:418
  314.8 18.3 %add_convert_fusion.refs_2_.ref = bf16[2048,2816]{1,0:T(8,128)(2,1)} fusion(f32[]{:T(128)} %bitcast.23, bf16[512,1408]{1,0:T(8,128)(2,1)} %get-tuple-element.127, bf16[512,1408]{1,0:T(8,128)(2,1)} %copy-done.141, bf16[512,1408]{1,0:T(8,128)(2,1)} %copy-done.140, bf16[512,1408]{1,0:T(8,128)(2,1)} %copy-done.139, bf16[512,2048]{1,0:T(8,128)(2,1)} %copy-done.91, ...), kind=kOutput, calls=%fused_computation | convolution fusion | flops 11854151680 | bytes 21495812 | tf_op jit(solution)/shard_map/dot_general | solution.py:26
  344.0 9.0 %collective-permute-start.26 = (bf16[512,2048]{1,0:T(8,128)(2,1)}, bf16[512,2048]{1,0:T(8,128)(2,1)}, u32[]{:S(2)}, u32[]{:S(2)}) collective-permute-start(bf16[512,2048]{1,0:T(8,128)(2,1)} %copy-done.52), channel_id=1, source_target_pairs={{0,1},{3,2},{4,5},{7,6},{8,9},{11,10},{12,13},{15,14},{16,17},{19,... | collective-permute-start | bytes 6291464 | tf_op jit(solution)/shard_map/ppermute | solution.py:418
  364.9 9.5 %grad_middle.2 = (f32[512,2048]{1,0:T(8,128)}, bf16[512,2048]{1,0:T(8,128)(2,1)}, f32[1,2048]{1,0:T(1,128)}) custom-call(s32[1]{0:T(128)} %bitcast.choice, bf16[256,2048]{1,0:T(8,128)(2,1)} %copy-done.32, bf16[256,2048]{1,0:T(8,128)(2,1)} %copy-done.23, bf16[256,2048]{1,0:T(8,128)(2,1)} %copy-done.50, bf16[256,2048]{1,0:T(8,128)(2,1)} %copy-done.49, ...), custom_call_target="tpu_custom_call" | custom-call | flops 1024 | bytes 1024 | tf_op jit(solution)/shard_map/grad_middle/pallas_call | solution.py:314
  414.8 9.4 %grad_middle.3 = (f32[512,2048]{1,0:T(8,128)}, bf16[512,2048]{1,0:T(8,128)(2,1)}, f32[1,2048]{1,0:T(1,128)}) custom-call(s32[1]{0:T(128)} %bitcast.choice, bf16[256,2048]{1,0:T(8,128)(2,1)} %copy-done.11, bf16[256,2048]{1,0:T(8,128)(2,1)} %copy-done.27, bf16[256,2048]{1,0:T(8,128)(2,1)} %collective-permute-done.24.refs_2_, ...), custom_call_target="tpu_custom_call" | custom-call | flops 1024 | bytes 1024 | tf_op jit(solution)/shard_map/grad_middle/pallas_call | solution.py:314
  437.8 8.8 %collective-permute-start.33 = (f32[512,128]{1,0:T(8,128)S(1)}, f32[512,128]{1,0:T(8,128)S(1)}, u32[]{:S(2)}, u32[]{:S(2)}) collective-permute-start(f32[512,128]{1,0:T(8,128)S(1)} %get-tuple-element.75), channel_id=1, source_target_pairs={{0,4},{4,0},{1,5},{5,1},{2,6},{6,2},{3,7},{7,3},{8,12},{12,8},{9,1... | collective-permute-start | bytes 786440 | tf_op jit(solution)/shard_map/ppermute | solution.py:691
  486.0 14.4 %collective-permute-done.31.refs_2_.refs_1_ = bf16[512,2048]{1,0:T(8,128)(2,1)S(1)} collective-permute-done((bf16[512,2048]{1,0:T(8,128)(2,1)S(1)}, bf16[512,2048]{1,0:T(8,128)(2,1)S(1)}, u32[]{:S(2)}, u32[]{:S(2)}) %collective-permute-start.31) | collective-permute-done | bytes 2097184 | tf_op jit(solution)/shard_map/ppermute | solution.py:426
  550.0 17.5 %collective-permute-done.34.refs_2_.refs_1_ = bf16[512,2048]{1,0:T(8,128)(2,1)} collective-permute-done((bf16[512,2048]{1,0:T(8,128)(2,1)S(1)}, bf16[512,2048]{1,0:T(8,128)(2,1)}, u32[]{:S(2)}, u32[]{:S(2)}) %collective-permute-start.34) | collective-permute-done | bytes 2097184 | tf_op jit(solution)/shard_map/ppermute | solution.py:426
  570.0 11.6 %collective-permute-done.40.refs_2_ = bf16[256,2048]{1,0:T(8,128)(2,1)} collective-permute-done((bf16[256,2048]{1,0:T(8,128)(2,1)}, bf16[256,2048]{1,0:T(8,128)(2,1)}, u32[]{:S(2)}, u32[]{:S(2)}) %collective-permute-start.40) | collective-permute-done | bytes 1048608 | tf_op jit(solution)/shard_map/ppermute | solution.py:426
  590.6 7.7 %result.2 = (bf16[1024,2048]{1,0:T(8,128)(2,1)}, f32[1,2048]{1,0:T(1,128)}, f32[1,2048]{1,0:T(1,128)}, f32[1,2048]{1,0:T(1,128)}) custom-call(s32[1]{0:T(128)} %bitcast.choice, bf16[512,2048]{1,0:T(8,128)(2,1)} %copy-done.10, bf16[512,2048]{1,0:T(8,128)(2,1)} %copy-done.35, bf16[1024,2048]{1,0:T(8,128)(2,1)} %bitcast.109, bf16[512,2048]{1,0:T(8,128)(2,1)} %copy-done.8, ...), custom_call_target="tpu_custom_call" | custom-call | flops 1024 | bytes 1024 | tf_op jit(solution)/shard_map/result/pallas_call | solution.py:314
  598.3 7.7 %result.3 = (bf16[1024,2048]{1,0:T(8,128)(2,1)}, f32[1,2048]{1,0:T(1,128)}, f32[1,2048]{1,0:T(1,128)}, f32[1,2048]{1,0:T(1,128)}) custom-call(s32[1]{0:T(128)} %bitcast.choice, bf16[512,2048]{1,0:T(8,128)(2,1)} %copy-done.6, bf16[512,2048]{1,0:T(8,128)(2,1)} %collective-permute-done.34.refs_2_.refs_1_, ...), custom_call_target="tpu_custom_call", output_to_operand_aliasing={{0}: (6, {})} | custom-call | flops 1024 | bytes 1024 | tf_op jit(solution)/shard_map/result/pallas_call | solution.py:314
  620.9 7.2 %input_grad.2.refs_9_ = bf16[1024,2048]{1,0:T(8,128)(2,1)} custom-call(s32[1]{0:T(128)} %bitcast.choice, bf16[256,2048]{1,0:T(8,128)(2,1)} %total.24.refs_5_.refs_0_, bf16[256,2048]{1,0:T(8,128)(2,1)} %copy-done.21, bf16[256,2048]{1,0:T(8,128)(2,1)} %collective-permute-done.40.refs_2_, bf16[256,2048]{1,0:T(8,128)(2,1)} %collective-permute-done.44.refs_3_, ...), custom_call_target="tpu_custom_call" | custom-call | flops 1024 | bytes 1024 | tf_op jit(solution)/shard_map/input_grad/pallas_call | solution.py:314
  628.1 15.9 %reduce-scatter.8.cloned.1.call-done = bf16[256,1280]{1,0:T(8,128)(2,1)} async-done(((bf16[2048,1280]{1,0:T(8,128)(2,1)}), bf16[256,1280]{1,0:T(8,128)(2,1)}) %reduce-scatter.8.cloned.1.call-update) | async-done | bytes 655376 | tf_op jit(solution)/shard_map/reduce_scatter | solution.py:503
  (576 shorter events, 355.0 us)
Async XLA Ops:
  7.2 40.0 %all-gather.5.cloned.1.call-start = ((), (), s32[]{:S(2)}) async-start(), calls=%async_computation.3 | async-start | bytes 3538944 | tf_op jit(solution)/shard_map/all_gather | solution.py:482
  11.5 67.2 %all-gather.7.cloned.1.call-start = ((), (), s32[]{:S(2)}) async-start(), calls=%async_computation.4 | async-start | bytes 2359296 | tf_op jit(solution)/shard_map/all_gather | solution.py:482
  12.3 181.8 %all-gather.9.cloned.1.call-start = ((), (), s32[]{:S(2)}) async-start(), calls=%async_computation.5 | async-start | bytes 12976128 | tf_op jit(solution)/shard_map/all_gather | solution.py:482
  13.6 197.1 %all-gather.11.cloned.1.call-start = ((), (), s32[]{:S(2)}) async-start(), calls=%async_computation.6 | async-start | bytes 6488064 | tf_op jit(solution)/shard_map/all_gather | solution.py:482
  14.2 493.5 %reduce-scatter.4.cloned.1.call-start = ((), (), s32[]{:S(2)}) async-start(), calls=%async_computation.7 | async-start | bytes 12976128 | tf_op jit(solution)/shard_map/reduce_scatter | solution.py:503
  87.6 43.1 %collective-permute-start.4 = (bf16[256,2048]{1,0:T(8,128)(2,1)}, bf16[256,2048]{1,0:T(8,128)(2,1)}, u32[]{:S(2)}, u32[]{:S(2)}) collective-permute-start(bf16[256,2048]{1,0:T(8,128)(2,1)} %convolution_convert_fusion.2.refs_0_), channel_id=1, source_target_pairs={{0,1},{3,2},{4,5},{7,6},{8,9},{11,10},{12,13},{15,14},{16,17},{19,... | collective-permute-start | bytes 3145736 | tf_op jit(solution)/shard_map/ppermute | solution.py:418
  102.7 50.3 %collective-permute-start.1 = (bf16[256,2048]{1,0:T(8,128)(2,1)S(1)}, bf16[256,2048]{1,0:T(8,128)(2,1)S(1)}, u32[]{:S(2)}, u32[]{:S(2)}) collective-permute-start(bf16[256,2048]{1,0:T(8,128)(2,1)S(1)} %convolution_convert_fusion.4.refs_2_.refs_0_), channel_id=1, source_target_pairs={{0,1},{3,2},{4,5},{7,6},{8,9},{11,10},{12,13},{15,14},{16,17},{19,... | collective-permute-start | bytes 3145736 | tf_op jit(solution)/shard_map/ppermute | solution.py:418
  133.1 41.8 %collective-permute-start.6 = (bf16[256,2048]{1,0:T(8,128)(2,1)S(1)}, bf16[256,2048]{1,0:T(8,128)(2,1)S(1)}, u32[]{:S(2)}, u32[]{:S(2)}) collective-permute-start(bf16[256,2048]{1,0:T(8,128)(2,1)S(1)} %convolution_convert_fusion.1.refs_2_.refs_0_), channel_id=1, source_target_pairs={{0,1},{3,2},{4,5},{7,6},{8,9},{11,10},{12,13},{15,14},{16,17},{19,... | collective-permute-start | bytes 3145736 | tf_op jit(solution)/shard_map/ppermute | solution.py:418
  154.6 36.1 %collective-permute-start.10 = (bf16[256,2048]{1,0:T(8,128)(2,1)S(1)}, bf16[256,2048]{1,0:T(8,128)(2,1)S(1)}, u32[]{:S(2)}, u32[]{:S(2)}) collective-permute-start(bf16[256,2048]{1,0:T(8,128)(2,1)S(1)} %total.15.refs_3_.refs_1_), channel_id=1, source_target_pairs={{1,0},{2,3},{5,4},{6,7},{9,8},{10,11},{13,12},{14,15},{17,16},{18,... | collective-permute-start | bytes 3145736 | tf_op jit(solution)/shard_map/ppermute | solution.py:426
  178.9 59.3 %collective-permute-start.11 = (bf16[256,2048]{1,0:T(8,128)(2,1)}, bf16[256,2048]{1,0:T(8,128)(2,1)}, u32[]{:S(2)}, u32[]{:S(2)}) collective-permute-start(bf16[256,2048]{1,0:T(8,128)(2,1)} %total.16.refs_6_.refs_0_), channel_id=1, source_target_pairs={{1,0},{2,3},{5,4},{6,7},{9,8},{10,11},{13,12},{14,15},{17,16},{18,... | collective-permute-start | bytes 3145736 | tf_op jit(solution)/shard_map/ppermute | solution.py:426
  236.8 48.7 %collective-permute-start.15 = (bf16[256,2048]{1,0:T(8,128)(2,1)S(1)}, bf16[256,2048]{1,0:T(8,128)(2,1)S(1)}, u32[]{:S(2)}, u32[]{:S(2)}) collective-permute-start(bf16[256,2048]{1,0:T(8,128)(2,1)S(1)} %get-tuple-element.141.refs_6_.refs_0_), channel_id=1, source_target_pairs={{0,1},{3,2},{4,5},{7,6},{8,9},{11,10},{12,13},{15,14},{16,17},{19,... | collective-permute-start | bytes 3145736 | tf_op jit(solution)/shard_map/ppermute | solution.py:418
  284.2 48.9 %collective-permute-start.20 = (bf16[256,2048]{1,0:T(8,128)(2,1)S(1)}, bf16[256,2048]{1,0:T(8,128)(2,1)S(1)}, u32[]{:S(2)}, u32[]{:S(2)}) collective-permute-start(bf16[256,2048]{1,0:T(8,128)(2,1)S(1)} %get-tuple-element.139.refs_2_.refs_0_), channel_id=1, source_target_pairs={{0,1},{3,2},{4,5},{7,6},{8,9},{11,10},{12,13},{15,14},{16,17},{19,... | collective-permute-start | bytes 3145736 | tf_op jit(solution)/shard_map/ppermute | solution.py:418
  343.9 239.0 %reduce-scatter.6.cloned.1.call-start = ((), (), s32[]{:S(2)}) async-start(), calls=%async_computation.8 | async-start | bytes 6488064 | tf_op jit(solution)/shard_map/reduce_scatter | solution.py:503
  344.0 53.9 %collective-permute-start.26 = (bf16[512,2048]{1,0:T(8,128)(2,1)}, bf16[512,2048]{1,0:T(8,128)(2,1)}, u32[]{:S(2)}, u32[]{:S(2)}) collective-permute-start(bf16[512,2048]{1,0:T(8,128)(2,1)} %copy-done.52), channel_id=1, source_target_pairs={{0,1},{3,2},{4,5},{7,6},{8,9},{11,10},{12,13},{15,14},{16,17},{19,... | collective-permute-start | bytes 6291464 | tf_op jit(solution)/shard_map/ppermute | solution.py:418
  357.8 101.2 %collective-permute-start.16 = (bf16[512,2048]{1,0:T(8,128)(2,1)}, bf16[512,2048]{1,0:T(8,128)(2,1)}, u32[]{:S(2)}, u32[]{:S(2)}) collective-permute-start(bf16[512,2048]{1,0:T(8,128)(2,1)} %copy-done.42), channel_id=1, source_target_pairs={{0,1},{3,2},{4,5},{7,6},{8,9},{11,10},{12,13},{15,14},{16,17},{19,... | collective-permute-start | bytes 6291464 | tf_op jit(solution)/shard_map/ppermute | solution.py:418
  378.6 36.2 %collective-permute-start.25 = (bf16[256,2048]{1,0:T(8,128)(2,1)S(1)}, bf16[256,2048]{1,0:T(8,128)(2,1)}, u32[]{:S(2)}, u32[]{:S(2)}) collective-permute-start(bf16[256,2048]{1,0:T(8,128)(2,1)S(1)} %total.21.refs_3_.refs_1_), channel_id=1, source_target_pairs={{1,0},{2,3},{5,4},{6,7},{9,8},{10,11},{13,12},{14,15},{17,16},{18,... | collective-permute-start | bytes 3145736 | tf_op jit(solution)/shard_map/ppermute | solution.py:426
  401.9 64.2 %collective-permute-start.30 = (bf16[512,2048]{1,0:T(8,128)(2,1)}, bf16[512,2048]{1,0:T(8,128)(2,1)}, u32[]{:S(2)}, u32[]{:S(2)}) collective-permute-start(bf16[512,2048]{1,0:T(8,128)(2,1)} %pair.22.refs_9_.refs_0_), channel_id=1, source_target_pairs={{1,2},{2,1},{5,6},{6,5},{9,10},{10,9},{13,14},{14,13},{17,18},{18,... | collective-permute-start | bytes 6291464 | tf_op jit(solution)/shard_map/ppermute | solution.py:422
  461.6 41.3 %collective-permute-start.28 = (bf16[512,2048]{1,0:T(8,128)(2,1)S(1)}, bf16[512,2048]{1,0:T(8,128)(2,1)}, u32[]{:S(2)}, u32[]{:S(2)}) collective-permute-start(bf16[512,2048]{1,0:T(8,128)(2,1)S(1)} %pair.23.refs_2_.refs_0_), channel_id=1, source_target_pairs={{1,2},{2,1},{5,6},{6,5},{9,10},{10,9},{13,14},{14,13},{17,18},{18,... | collective-permute-start | bytes 6291464 | tf_op jit(solution)/shard_map/ppermute | solution.py:422
  510.9 133.2 %reduce-scatter.8.cloned.1.call-start = ((), (), s32[]{:S(2)}) async-start(), calls=%async_computation.9 | async-start | bytes 5898240 | tf_op jit(solution)/shard_map/reduce_scatter | solution.py:503
  511.8 38.1 %collective-permute-start.35 = (bf16[256,2048]{1,0:T(8,128)(2,1)S(1)}, bf16[256,2048]{1,0:T(8,128)(2,1)}, u32[]{:S(2)}, u32[]{:S(2)}) collective-permute-start(bf16[256,2048]{1,0:T(8,128)(2,1)S(1)} %get-tuple-element.135.refs_2_.refs_3_.refs_0_), channel_id=1, source_target_pairs={{0,1},{3,2},{4,5},{7,6},{8,9},{11,10},{12,13},{15,14},{16,17},{19,... | collective-permute-start | bytes 3145736 | tf_op jit(solution)/shard_map/ppermute | solution.py:418
  523.2 44.3 %collective-permute-start.34 = (bf16[512,2048]{1,0:T(8,128)(2,1)S(1)}, bf16[512,2048]{1,0:T(8,128)(2,1)}, u32[]{:S(2)}, u32[]{:S(2)}) collective-permute-start(bf16[512,2048]{1,0:T(8,128)(2,1)S(1)} %copy-done.7), channel_id=1, source_target_pairs={{1,0},{2,3},{5,4},{6,7},{9,8},{10,11},{13,12},{14,15},{17,16},{18,... | collective-permute-start | bytes 6291464 | tf_op jit(solution)/shard_map/ppermute | solution.py:426
  529.7 51.9 %collective-permute-start.40 = (bf16[256,2048]{1,0:T(8,128)(2,1)}, bf16[256,2048]{1,0:T(8,128)(2,1)}, u32[]{:S(2)}, u32[]{:S(2)}) collective-permute-start(bf16[256,2048]{1,0:T(8,128)(2,1)} %total.24.refs_5_.refs_0_), channel_id=1, source_target_pairs={{1,0},{2,3},{5,4},{6,7},{9,8},{10,11},{13,12},{14,15},{17,16},{18,... | collective-permute-start | bytes 3145736 | tf_op jit(solution)/shard_map/ppermute | solution.py:426
  587.7 63.0 %collective-permute-start.42 = (bf16[256,2048]{1,0:T(8,128)(2,1)S(1)}, bf16[256,2048]{1,0:T(8,128)(2,1)}, u32[]{:S(2)}, u32[]{:S(2)}) collective-permute-start(bf16[256,2048]{1,0:T(8,128)(2,1)S(1)} %total.26.refs_3_.refs_0_), channel_id=1, source_target_pairs={{1,0},{2,3},{5,4},{6,7},{9,8},{10,11},{13,12},{14,15},{17,16},{18,... | collective-permute-start | bytes 3145736 | tf_op jit(solution)/shard_map/ppermute | solution.py:426
  589.0 61.7 %collective-permute-start.43 = (bf16[256,2048]{1,0:T(8,128)(2,1)S(1)}, bf16[256,2048]{1,0:T(8,128)(2,1)}, u32[]{:S(2)}, u32[]{:S(2)}) collective-permute-start(bf16[256,2048]{1,0:T(8,128)(2,1)S(1)} %copy-done.15), channel_id=1, source_target_pairs={{1,0},{2,3},{5,4},{6,7},{9,8},{10,11},{13,12},{14,15},{17,16},{18,... | collective-permute-start | bytes 3145736 | tf_op jit(solution)/shard_map/ppermute | solution.py:426
  (178 other events, 2148.1 us)
Sparse Core Ops, SparseCore 0:
  11.6 35.5 all-gather.4
  49.1 29.6 all-gather.6
  81.2 67.8 all-gather.8
  150.8 43.3 all-gather.10
  344.0 96.6 reduce-scatter.3
  511.0 56.8 reduce-scatter.5
  585.3 58.6 reduce-scatter.7

commit v5 on v4

--- a/solution.py
+++ b/solution.py
@@ -758,12 +758,14 @@
     sums.pair(15, (sums.thirds[10],))
     sums.total(14)
     sums.total(15, (sums.thirds[12],))
-    last = scatter_rows(once(last, (sums.totals[15], grad_down)))
+    last = once(last, (sums.totals[15], grad_down))
+    last = lax.psum_scatter(last, ROW_AXES, scatter_dimension=0, tiled=True)
     output, *squares_one = result_of(8, one, attn_out_one, None)
     output, *squares_two = result_of(10, two, attn_out_two, output)
     grad_gateup_w = grad_gateup_w.reshape(w_gateup.shape)
     input_grad = input_grad_of(12, one, grad_middle_one, None)
     input_grad = input_grad_of(14, two, grad_middle_two, input_grad, (grad_gateup_w, grad_down))
+    last = once(last, (input_grad,)).astype(F32)
     squares = [jnp.sum(x) + jnp.sum(y) for x, y in zip(squares_one, squares_two)]
     squares = spread_small(jnp.broadcast_to(jnp.stack(squares + [0.0])[None, :], (8, 4)))[0, :3]
     root_means = jnp.sqrt(squares / (jnp.sum(lengths).astype(F32) * width))

time: 681 us -> 689 us (1.012)
  starting transfers between devices: 114 us -> 126 us
    reduce_scatter x3 -> x2, waiting for transfers between devices: 15.9 us -> 0.01 us  [scatter_rows(): lax.psum_scatter(grads, ROW_AXES, scatter_dimension=0, tiled=True)]
    ppermute x2, starting transfers between devices: 9.97 us -> 23.4 us  [attend_back_group(): returned = lax.ppermute(carry[1], 'ctx', [(0, 1), (1, 0)])]
    ppermute x14, waiting for transfers between devices: 55.5 us -> 66.2 us  [send_out(): return lax.ppermute(total, 'tensor', [(1, 0), (2, 3)])]
  transfers between devices with their start and end apart: 57 -> 57, of which waited for: 19 -> 22; matrix products, arithmetic and copies ran while one was open for 25% -> 24% of each run, Pallas kernels for 20% -> 20%
where the time goes in v5:
time: 689 us; the launch traced here: 678 us
  waiting for transfers between devices  187 us (27%)
  Pallas kernels  134 us (19%)
  starting transfers between devices  126 us (18%)
  matrix products  121 us (18%)
  local copies, waits for them, and re-layouts  54.3 us (8%)
  other arithmetic  28.2 us (4%)
  between operations  27.6 us (4%)
    dot_general x22, matrix products, dot(): lax.dot_general(left, right, (((left_dim,), (right_dim,)), ((), ())), pre...  121 us
    pallas_call x37, Pallas kernels, rowwise(): pl.pallas_call(functools.partial(rowwise_kernel, fn, bounds, len(lists),...  99.3 us
    ppermute x14, waiting for transfers between devices, send_in(): return lax.ppermute(part, 'tensor', [(0, 1), (3, 2)])  72.9 us
    ppermute x14, waiting for transfers between devices, send_out(): return lax.ppermute(total, 'tensor', [(1, 0), (2, 3)])  66.2 us
    ppermute x14, starting transfers between devices, send_in(): return lax.ppermute(part, 'tensor', [(0, 1), (3, 2)])  61.8 us
    unnamed x298, local copies, waits for them, and re-layouts  31.1 us
    all_gather x4, waiting for transfers between devices, gather_rows(): return lax.all_gather(shard, ROW_AXES, axis=0, tiled=True)  30 us
    ppermute x2, starting transfers between devices, attend_back_group(): returned = lax.ppermute(carry[1], 'ctx', [(0, 1), (1, 0)])  23.4 us
  transfers between devices with their start and end apart: 57, of which 22 were waited for; matrix products, arithmetic and copies ran while one was open for 24% of the time, Pallas kernels for 20%

profile of v5, /device:TPU:0, one launch (start us, length us, event | category | flops | bytes accessed | tf_op | source)
XLA Modules:
  0.0 677.9 jit_solution(2372080143282857361)
XLA Ops:
  21.6 25.6 %all-gather.5.cloned.1.call-done = bf16[2048,768]{0,1:T(8,128)(2,1)} async-done(((bf16[256,768]{0,1:T(8,128)(2,1)}), bf16[2048,768]{0,1:T(8,128)(2,1)}) %all-gather.5.cloned.1.call-update) | async-done | bytes 3145744 | tf_op jit(solution)/shard_map/all_gather | solution.py:482
  111.0 19.7 %collective-permute-done.4.refs_1_ = bf16[256,2048]{1,0:T(8,128)(2,1)} collective-permute-done((bf16[256,2048]{1,0:T(8,128)(2,1)}, bf16[256,2048]{1,0:T(8,128)(2,1)}, u32[]{:S(2)}, u32[]{:S(2)}) %collective-permute-start.4) | collective-permute-done | bytes 1048608 | tf_op jit(solution)/shard_map/ppermute | solution.py:418
  142.1 11.0 %collective-permute-done.1.refs_1_ = bf16[256,2048]{1,0:T(8,128)(2,1)S(1)} collective-permute-done((bf16[256,2048]{1,0:T(8,128)(2,1)S(1)}, bf16[256,2048]{1,0:T(8,128)(2,1)S(1)}, u32[]{:S(2)}, u32[]{:S(2)}) %collective-permute-start.1) | collective-permute-done | bytes 1048608 | tf_op jit(solution)/shard_map/ppermute | solution.py:418
  159.0 15.9 %collective-permute-done.6.refs_1_ = bf16[256,2048]{1,0:T(8,128)(2,1)S(1)} collective-permute-done((bf16[256,2048]{1,0:T(8,128)(2,1)S(1)}, bf16[256,2048]{1,0:T(8,128)(2,1)S(1)}, u32[]{:S(2)}, u32[]{:S(2)}) %collective-permute-start.6) | collective-permute-done | bytes 1048608 | tf_op jit(solution)/shard_map/ppermute | solution.py:418
  180.2 10.5 %collective-permute-done.10.refs_3_ = bf16[256,2048]{1,0:T(8,128)(2,1)S(1)} collective-permute-done((bf16[256,2048]{1,0:T(8,128)(2,1)S(1)}, bf16[256,2048]{1,0:T(8,128)(2,1)S(1)}, u32[]{:S(2)}, u32[]{:S(2)}) %collective-permute-start.10) | collective-permute-done | bytes 1048608 | tf_op jit(solution)/shard_map/ppermute | solution.py:426
  194.0 10.9 %fusion.121.refs_2_ = f32[512,2816]{1,0:T(8,128)S(1)} fusion(bf16[512,2048]{1,0:T(8,128)(2,1)} %copy-done.90, bf16[2048,2816]{1,0:T(8,128)(2,1)} %all-gather.9.cloned.1.call-done), kind=kOutput, calls=%fused_computation.206 | convolution fusion | flops 5905580032 | bytes 19398656 | tf_op jit(solution)/shard_map/dot_general | solution.py:26
  210.6 10.3 %multiply_convert_fusion.7 = (bf16[512,1408]{1,0:T(8,128)(2,1)S(1)}, bf16[512,1408]{1,0:T(8,128)(2,1)S(1)}, bf16[512,1408]{1,0:T(8,128)(2,1)}) fusion(f32[512,2816]{1,0:T(8,128)} %copy-done.48, bf16[2048,1408]{1,0:T(8,128)(2,1)} %all-gather.11.cloned.1.call-done, bf16[1024,2048]{1,0:T(8,128)(2,1)} %multiply_convert_fusion), kind=kOutput, calls=%fused_computation.53 | convolution fusion | flops 2963603456 | bytes 17956864 | tf_op jit(solution)/shard_map/dot_general | solution.py:26
  222.5 9.0 %convolution_convert_fusion = bf16[512,2048]{1,0:T(8,128)(2,1)S(1)} fusion(bf16[2048,2816]{1,0:T(8,128)(2,1)} %all-gather.9.cloned.1.call-done, bf16[512,1408]{1,0:T(8,128)(2,1)S(1)} %get-tuple-element.129, bf16[512,1408]{1,0:T(8,128)(2,1)S(1)} %get-tuple-element.128), kind=kOutput, calls=%fused_computation.36 | convolution fusion | flops 5912395776 | bytes 16515072 | tf_op jit(solution)/shard_map/dot_general | solution.py:26
  242.3 11.1 %fusion.122.refs_2_ = f32[512,2816]{1,0:T(8,128)S(1)} fusion(bf16[512,2048]{1,0:T(8,128)(2,1)S(1)} %get-tuple-element.54, bf16[2048,2816]{1,0:T(8,128)(2,1)} %all-gather.9.cloned.1.call-done), kind=kOutput, calls=%fused_computation.207 | convolution fusion | flops 5905580032 | bytes 19398656 | tf_op jit(solution)/shard_map/dot_general | solution.py:26
  268.3 10.0 %add_convert_fusion.8 = bf16[512,2048]{1,0:T(8,128)(2,1)S(1)} fusion(bf16[2048,2816]{1,0:T(8,128)(2,1)} %all-gather.9.cloned.1.call-done, bf16[512,1408]{1,0:T(8,128)(2,1)} %get-tuple-element.127, bf16[512,1408]{1,0:T(8,128)(2,1)S(1)} %get-tuple-element.126, f32[]{:T(128)} %bitcast.20), kind=kOutput, calls=%fused_computation.35 | convolution fusion | flops 5913444352 | bytes 16515076 | tf_op jit(solution)/shard_map/dot_general | solution.py:26
  298.3 9.4 %collective-permute-done.17.refs_1_ = bf16[256,2048]{1,0:T(8,128)(2,1)S(1)} collective-permute-done((bf16[256,2048]{1,0:T(8,128)(2,1)S(1)}, bf16[256,2048]{1,0:T(8,128)(2,1)S(1)}, u32[]{:S(2)}, u32[]{:S(2)}) %collective-permute-start.17) | collective-permute-done | bytes 1048608 | tf_op jit(solution)/shard_map/ppermute | solution.py:418
  314.7 18.3 %add_convert_fusion.refs_2_.ref = bf16[2048,2816]{1,0:T(8,128)(2,1)} fusion(f32[]{:T(128)} %bitcast.23, bf16[512,1408]{1,0:T(8,128)(2,1)} %get-tuple-element.127, bf16[512,1408]{1,0:T(8,128)(2,1)} %copy-done.141, bf16[512,1408]{1,0:T(8,128)(2,1)} %copy-done.140, bf16[512,1408]{1,0:T(8,128)(2,1)} %copy-done.139, bf16[512,2048]{1,0:T(8,128)(2,1)} %copy-done.91, ...), kind=kOutput, calls=%fused_computation | convolution fusion | flops 11854151680 | bytes 21495812 | tf_op jit(solution)/shard_map/dot_general | solution.py:26
  343.9 9.0 %collective-permute-start.26 = (bf16[512,2048]{1,0:T(8,128)(2,1)}, bf16[512,2048]{1,0:T(8,128)(2,1)}, u32[]{:S(2)}, u32[]{:S(2)}) collective-permute-start(bf16[512,2048]{1,0:T(8,128)(2,1)} %copy-done.52), channel_id=1, source_target_pairs={{0,1},{3,2},{4,5},{7,6},{8,9},{11,10},{12,13},{15,14},{16,17},{19,... | collective-permute-start | bytes 6291464 | tf_op jit(solution)/shard_map/ppermute | solution.py:418
  364.9 10.4 %grad_middle.2 = (f32[512,2048]{1,0:T(8,128)}, bf16[512,2048]{1,0:T(8,128)(2,1)}, f32[1,2048]{1,0:T(1,128)}) custom-call(s32[1]{0:T(128)} %bitcast.choice, bf16[256,2048]{1,0:T(8,128)(2,1)} %copy-done.32, bf16[256,2048]{1,0:T(8,128)(2,1)} %copy-done.23, bf16[256,2048]{1,0:T(8,128)(2,1)} %copy-done.50, bf16[256,2048]{1,0:T(8,128)(2,1)} %copy-done.49, ...), custom_call_target="tpu_custom_call" | custom-call | flops 1024 | bytes 1024 | tf_op jit(solution)/shard_map/grad_middle/pallas_call | solution.py:314
  403.9 13.7 %collective-permute-start.27 = (f32[512,128]{1,0:T(8,128)S(1)}, f32[512,128]{1,0:T(8,128)S(1)}, u32[]{:S(2)}, u32[]{:S(2)}) collective-permute-start(f32[512,128]{1,0:T(8,128)S(1)} %get-tuple-element.72), channel_id=1, source_target_pairs={{0,4},{4,0},{1,5},{5,1},{2,6},{6,2},{3,7},{7,3},{8,12},{12,8},{9,1... | collective-permute-start | bytes 786440 | tf_op jit(solution)/shard_map/ppermute | solution.py:691
  424.5 9.6 %grad_middle.3 = (f32[512,2048]{1,0:T(8,128)}, bf16[512,2048]{1,0:T(8,128)(2,1)}, f32[1,2048]{1,0:T(1,128)}) custom-call(s32[1]{0:T(128)} %bitcast.choice, bf16[256,2048]{1,0:T(8,128)(2,1)} %copy-done.11, bf16[256,2048]{1,0:T(8,128)(2,1)} %copy-done.27, bf16[256,2048]{1,0:T(8,128)(2,1)} %collective-permute-done.24.refs_2_, ...), custom_call_target="tpu_custom_call" | custom-call | flops 1024 | bytes 1024 | tf_op jit(solution)/shard_map/grad_middle/pallas_call | solution.py:314
  447.6 9.7 %collective-permute-start.33 = (f32[512,128]{1,0:T(8,128)S(1)}, f32[512,128]{1,0:T(8,128)S(1)}, u32[]{:S(2)}, u32[]{:S(2)}) collective-permute-start(f32[512,128]{1,0:T(8,128)S(1)} %get-tuple-element.75), channel_id=1, source_target_pairs={{0,4},{4,0},{1,5},{5,1},{2,6},{6,2},{3,7},{7,3},{8,12},{12,8},{9,1... | collective-permute-start | bytes 786440 | tf_op jit(solution)/shard_map/ppermute | solution.py:691
  496.6 12.6 %collective-permute-done.31.refs_2_.refs_1_ = bf16[512,2048]{1,0:T(8,128)(2,1)S(1)} collective-permute-done((bf16[512,2048]{1,0:T(8,128)(2,1)S(1)}, bf16[512,2048]{1,0:T(8,128)(2,1)S(1)}, u32[]{:S(2)}, u32[]{:S(2)}) %collective-permute-start.31) | collective-permute-done | bytes 2097184 | tf_op jit(solution)/shard_map/ppermute | solution.py:426
  559.6 10.1 %collective-permute-done.34.refs_2_.refs_1_ = bf16[512,2048]{1,0:T(8,128)(2,1)} collective-permute-done((bf16[512,2048]{1,0:T(8,128)(2,1)S(1)}, bf16[512,2048]{1,0:T(8,128)(2,1)}, u32[]{:S(2)}, u32[]{:S(2)}) %collective-permute-start.34) | collective-permute-done | bytes 2097184 | tf_op jit(solution)/shard_map/ppermute | solution.py:426
  572.1 8.8 %collective-permute-done.40.refs_2_ = bf16[256,2048]{1,0:T(8,128)(2,1)} collective-permute-done((bf16[256,2048]{1,0:T(8,128)(2,1)}, bf16[256,2048]{1,0:T(8,128)(2,1)}, u32[]{:S(2)}, u32[]{:S(2)}) %collective-permute-start.40) | collective-permute-done | bytes 1048608 | tf_op jit(solution)/shard_map/ppermute | solution.py:426
  589.9 7.4 %result.2 = (bf16[1024,2048]{1,0:T(8,128)(2,1)}, f32[1,2048]{1,0:T(1,128)}, f32[1,2048]{1,0:T(1,128)}, f32[1,2048]{1,0:T(1,128)}) custom-call(s32[1]{0:T(128)} %bitcast.choice, bf16[512,2048]{1,0:T(8,128)(2,1)} %copy-done.10, bf16[512,2048]{1,0:T(8,128)(2,1)} %copy-done.35, bf16[1024,2048]{1,0:T(8,128)(2,1)} %bitcast.109, bf16[512,2048]{1,0:T(8,128)(2,1)} %copy-done.8, ...), custom_call_target="tpu_custom_call" | custom-call | flops 1024 | bytes 1024 | tf_op jit(solution)/shard_map/result/pallas_call | solution.py:314
  597.3 7.7 %result.3 = (bf16[1024,2048]{1,0:T(8,128)(2,1)}, f32[1,2048]{1,0:T(1,128)}, f32[1,2048]{1,0:T(1,128)}, f32[1,2048]{1,0:T(1,128)}) custom-call(s32[1]{0:T(128)} %bitcast.choice, bf16[512,2048]{1,0:T(8,128)(2,1)} %copy-done.6, bf16[512,2048]{1,0:T(8,128)(2,1)} %collective-permute-done.34.refs_2_.refs_1_, ...), custom_call_target="tpu_custom_call", output_to_operand_aliasing={{0}: (6, {})} | custom-call | flops 1024 | bytes 1024 | tf_op jit(solution)/shard_map/result/pallas_call | solution.py:314
  634.2 7.4 %collective-permute-done.42.refs_2_ = bf16[256,2048]{1,0:T(8,128)(2,1)} collective-permute-done((bf16[256,2048]{1,0:T(8,128)(2,1)S(1)}, bf16[256,2048]{1,0:T(8,128)(2,1)}, u32[]{:S(2)}, u32[]{:S(2)}) %collective-permute-start.42) | collective-permute-done | bytes 1048608 | tf_op jit(solution)/shard_map/ppermute | solution.py:426
  641.6 11.2 %collective-permute-done.43.refs_3_ = bf16[256,2048]{1,0:T(8,128)(2,1)} collective-permute-done((bf16[256,2048]{1,0:T(8,128)(2,1)S(1)}, bf16[256,2048]{1,0:T(8,128)(2,1)}, u32[]{:S(2)}, u32[]{:S(2)}) %collective-permute-start.43) | collective-permute-done | bytes 1048608 | tf_op jit(solution)/shard_map/ppermute | solution.py:426
  (577 shorter events, 371.0 us)
Async XLA Ops:
  7.2 40.0 %all-gather.5.cloned.1.call-start = ((), (), s32[]{:S(2)}) async-start(), calls=%async_computation.3 | async-start | bytes 3538944 | tf_op jit(solution)/shard_map/all_gather | solution.py:482
  11.5 67.2 %all-gather.7.cloned.1.call-start = ((), (), s32[]{:S(2)}) async-start(), calls=%async_computation.4 | async-start | bytes 2359296 | tf_op jit(solution)/shard_map/all_gather | solution.py:482
  12.3 181.7 %all-gather.9.cloned.1.call-start = ((), (), s32[]{:S(2)}) async-start(), calls=%async_computation.5 | async-start | bytes 12976128 | tf_op jit(solution)/shard_map/all_gather | solution.py:482
  13.6 197.0 %all-gather.11.cloned.1.call-start = ((), (), s32[]{:S(2)}) async-start(), calls=%async_computation.6 | async-start | bytes 6488064 | tf_op jit(solution)/shard_map/all_gather | solution.py:482
  14.2 502.3 %reduce-scatter.4.cloned.1.call-start = ((), (), s32[]{:S(2)}) async-start(), calls=%async_computation.7 | async-start | bytes 12976128 | tf_op jit(solution)/shard_map/reduce_scatter | solution.py:503
  87.6 43.1 %collective-permute-start.4 = (bf16[256,2048]{1,0:T(8,128)(2,1)}, bf16[256,2048]{1,0:T(8,128)(2,1)}, u32[]{:S(2)}, u32[]{:S(2)}) collective-permute-start(bf16[256,2048]{1,0:T(8,128)(2,1)} %convolution_convert_fusion.2.refs_0_), channel_id=1, source_target_pairs={{0,1},{3,2},{4,5},{7,6},{8,9},{11,10},{12,13},{15,14},{16,17},{19,... | collective-permute-start | bytes 3145736 | tf_op jit(solution)/shard_map/ppermute | solution.py:418
  102.8 50.3 %collective-permute-start.1 = (bf16[256,2048]{1,0:T(8,128)(2,1)S(1)}, bf16[256,2048]{1,0:T(8,128)(2,1)S(1)}, u32[]{:S(2)}, u32[]{:S(2)}) collective-permute-start(bf16[256,2048]{1,0:T(8,128)(2,1)S(1)} %convolution_convert_fusion.4.refs_2_.refs_0_), channel_id=1, source_target_pairs={{0,1},{3,2},{4,5},{7,6},{8,9},{11,10},{12,13},{15,14},{16,17},{19,... | collective-permute-start | bytes 3145736 | tf_op jit(solution)/shard_map/ppermute | solution.py:418
  133.1 41.8 %collective-permute-start.6 = (bf16[256,2048]{1,0:T(8,128)(2,1)S(1)}, bf16[256,2048]{1,0:T(8,128)(2,1)S(1)}, u32[]{:S(2)}, u32[]{:S(2)}) collective-permute-start(bf16[256,2048]{1,0:T(8,128)(2,1)S(1)} %convolution_convert_fusion.1.refs_2_.refs_0_), channel_id=1, source_target_pairs={{0,1},{3,2},{4,5},{7,6},{8,9},{11,10},{12,13},{15,14},{16,17},{19,... | collective-permute-start | bytes 3145736 | tf_op jit(solution)/shard_map/ppermute | solution.py:418
  178.9 59.2 %collective-permute-start.11 = (bf16[256,2048]{1,0:T(8,128)(2,1)}, bf16[256,2048]{1,0:T(8,128)(2,1)}, u32[]{:S(2)}, u32[]{:S(2)}) collective-permute-start(bf16[256,2048]{1,0:T(8,128)(2,1)} %total.16.refs_6_.refs_0_), channel_id=1, source_target_pairs={{1,0},{2,3},{5,4},{6,7},{9,8},{10,11},{13,12},{14,15},{17,16},{18,... | collective-permute-start | bytes 3145736 | tf_op jit(solution)/shard_map/ppermute | solution.py:426
  236.8 48.7 %collective-permute-start.15 = (bf16[256,2048]{1,0:T(8,128)(2,1)S(1)}, bf16[256,2048]{1,0:T(8,128)(2,1)S(1)}, u32[]{:S(2)}, u32[]{:S(2)}) collective-permute-start(bf16[256,2048]{1,0:T(8,128)(2,1)S(1)} %get-tuple-element.141.refs_6_.refs_0_), channel_id=1, source_target_pairs={{0,1},{3,2},{4,5},{7,6},{8,9},{11,10},{12,13},{15,14},{16,17},{19,... | collective-permute-start | bytes 3145736 | tf_op jit(solution)/shard_map/ppermute | solution.py:418
  284.1 48.9 %collective-permute-start.20 = (bf16[256,2048]{1,0:T(8,128)(2,1)S(1)}, bf16[256,2048]{1,0:T(8,128)(2,1)S(1)}, u32[]{:S(2)}, u32[]{:S(2)}) collective-permute-start(bf16[256,2048]{1,0:T(8,128)(2,1)S(1)} %get-tuple-element.139.refs_2_.refs_0_), channel_id=1, source_target_pairs={{0,1},{3,2},{4,5},{7,6},{8,9},{11,10},{12,13},{15,14},{16,17},{19,... | collective-permute-start | bytes 3145736 | tf_op jit(solution)/shard_map/ppermute | solution.py:418
  343.9 238.3 %reduce-scatter.6.cloned.1.call-start = ((), (), s32[]{:S(2)}) async-start(), calls=%async_computation.8 | async-start | bytes 6488064 | tf_op jit(solution)/shard_map/reduce_scatter | solution.py:503
  343.9 54.0 %collective-permute-start.26 = (bf16[512,2048]{1,0:T(8,128)(2,1)}, bf16[512,2048]{1,0:T(8,128)(2,1)}, u32[]{:S(2)}, u32[]{:S(2)}) collective-permute-start(bf16[512,2048]{1,0:T(8,128)(2,1)} %copy-done.52), channel_id=1, source_target_pairs={{0,1},{3,2},{4,5},{7,6},{8,9},{11,10},{12,13},{15,14},{16,17},{19,... | collective-permute-start | bytes 6291464 | tf_op jit(solution)/shard_map/ppermute | solution.py:418
  357.8 111.8 %collective-permute-start.16 = (bf16[512,2048]{1,0:T(8,128)(2,1)}, bf16[512,2048]{1,0:T(8,128)(2,1)}, u32[]{:S(2)}, u32[]{:S(2)}) collective-permute-start(bf16[512,2048]{1,0:T(8,128)(2,1)} %copy-done.42), channel_id=1, source_target_pairs={{0,1},{3,2},{4,5},{7,6},{8,9},{11,10},{12,13},{15,14},{16,17},{19,... | collective-permute-start | bytes 6291464 | tf_op jit(solution)/shard_map/ppermute | solution.py:418
  379.5 44.9 %collective-permute-start.25 = (bf16[256,2048]{1,0:T(8,128)(2,1)S(1)}, bf16[256,2048]{1,0:T(8,128)(2,1)}, u32[]{:S(2)}, u32[]{:S(2)}) collective-permute-start(bf16[256,2048]{1,0:T(8,128)(2,1)S(1)} %total.21.refs_3_.refs_1_), channel_id=1, source_target_pairs={{1,0},{2,3},{5,4},{6,7},{9,8},{10,11},{13,12},{14,15},{17,16},{18,... | collective-permute-start | bytes 3145736 | tf_op jit(solution)/shard_map/ppermute | solution.py:426
  401.9 74.8 %collective-permute-start.30 = (bf16[512,2048]{1,0:T(8,128)(2,1)}, bf16[512,2048]{1,0:T(8,128)(2,1)}, u32[]{:S(2)}, u32[]{:S(2)}) collective-permute-start(bf16[512,2048]{1,0:T(8,128)(2,1)} %pair.22.refs_9_.refs_0_), channel_id=1, source_target_pairs={{1,2},{2,1},{5,6},{6,5},{9,10},{10,9},{13,14},{14,13},{17,18},{18,... | collective-permute-start | bytes 6291464 | tf_op jit(solution)/shard_map/ppermute | solution.py:422
  472.2 39.5 %collective-permute-start.28 = (bf16[512,2048]{1,0:T(8,128)(2,1)S(1)}, bf16[512,2048]{1,0:T(8,128)(2,1)}, u32[]{:S(2)}, u32[]{:S(2)}) collective-permute-start(bf16[512,2048]{1,0:T(8,128)(2,1)S(1)} %pair.23.refs_2_.refs_0_), channel_id=1, source_target_pairs={{1,2},{2,1},{5,6},{6,5},{9,10},{10,9},{13,14},{14,13},{17,18},{18,... | collective-permute-start | bytes 6291464 | tf_op jit(solution)/shard_map/ppermute | solution.py:422
  519.7 140.3 %reduce-scatter.8.cloned.1.call-start = ((), (), s32[]{:S(2)}) async-start(), calls=%async_computation.9 | async-start | bytes 5898240 | tf_op jit(solution)/shard_map/reduce_scatter | solution.py:762
  520.6 38.9 %collective-permute-start.35 = (bf16[256,2048]{1,0:T(8,128)(2,1)S(1)}, bf16[256,2048]{1,0:T(8,128)(2,1)}, u32[]{:S(2)}, u32[]{:S(2)}) collective-permute-start(bf16[256,2048]{1,0:T(8,128)(2,1)S(1)} %get-tuple-element.135.refs_2_.refs_3_.refs_0_), channel_id=1, source_target_pairs={{0,1},{3,2},{4,5},{7,6},{8,9},{11,10},{12,13},{15,14},{16,17},{19,... | collective-permute-start | bytes 3145736 | tf_op jit(solution)/shard_map/ppermute | solution.py:418
  532.8 36.9 %collective-permute-start.34 = (bf16[512,2048]{1,0:T(8,128)(2,1)S(1)}, bf16[512,2048]{1,0:T(8,128)(2,1)}, u32[]{:S(2)}, u32[]{:S(2)}) collective-permute-start(bf16[512,2048]{1,0:T(8,128)(2,1)S(1)} %copy-done.7), channel_id=1, source_target_pairs={{1,0},{2,3},{5,4},{6,7},{9,8},{10,11},{13,12},{14,15},{17,16},{18,... | collective-permute-start | bytes 6291464 | tf_op jit(solution)/shard_map/ppermute | solution.py:426
  539.3 41.6 %collective-permute-start.40 = (bf16[256,2048]{1,0:T(8,128)(2,1)}, bf16[256,2048]{1,0:T(8,128)(2,1)}, u32[]{:S(2)}, u32[]{:S(2)}) collective-permute-start(bf16[256,2048]{1,0:T(8,128)(2,1)} %total.24.refs_5_.refs_0_), channel_id=1, source_target_pairs={{1,0},{2,3},{5,4},{6,7},{9,8},{10,11},{13,12},{14,15},{17,16},{18,... | collective-permute-start | bytes 3145736 | tf_op jit(solution)/shard_map/ppermute | solution.py:426
  585.7 38.3 %collective-permute-start.44 = (bf16[256,2048]{1,0:T(8,128)(2,1)S(1)}, bf16[256,2048]{1,0:T(8,128)(2,1)}, u32[]{:S(2)}, u32[]{:S(2)}) collective-permute-start(bf16[256,2048]{1,0:T(8,128)(2,1)S(1)} %copy-done.22), channel_id=1, source_target_pairs={{1,0},{2,3},{5,4},{6,7},{9,8},{10,11},{13,12},{14,15},{17,16},{18,... | collective-permute-start | bytes 3145736 | tf_op jit(solution)/shard_map/ppermute | solution.py:426
  587.0 54.6 %collective-permute-start.42 = (bf16[256,2048]{1,0:T(8,128)(2,1)S(1)}, bf16[256,2048]{1,0:T(8,128)(2,1)}, u32[]{:S(2)}, u32[]{:S(2)}) collective-permute-start(bf16[256,2048]{1,0:T(8,128)(2,1)S(1)} %total.26.refs_3_.refs_0_), channel_id=1, source_target_pairs={{1,0},{2,3},{5,4},{6,7},{9,8},{10,11},{13,12},{14,15},{17,16},{18,... | collective-permute-start | bytes 3145736 | tf_op jit(solution)/shard_map/ppermute | solution.py:426
  588.3 64.5 %collective-permute-start.43 = (bf16[256,2048]{1,0:T(8,128)(2,1)S(1)}, bf16[256,2048]{1,0:T(8,128)(2,1)}, u32[]{:S(2)}, u32[]{:S(2)}) collective-permute-start(bf16[256,2048]{1,0:T(8,128)(2,1)S(1)} %copy-done.15), channel_id=1, source_target_pairs={{1,0},{2,3},{5,4},{6,7},{9,8},{10,11},{13,12},{14,15},{17,16},{18,... | collective-permute-start | bytes 3145736 | tf_op jit(solution)/shard_map/ppermute | solution.py:426
  (178 other events, 2135.8 us)
Sparse Core Ops, SparseCore 0:
  11.6 35.5 all-gather.4
  49.1 29.6 all-gather.6
  81.2 67.7 all-gather.8
  150.8 43.3 all-gather.10
  344.0 102.3 reduce-scatter.3
  519.8 57.6 reduce-scatter.5
  584.6 66.4 reduce-scatter.7
